TPU v7x, 32 devices: a whole 2x2x4 slice. The times are simulated.
32 devices in a mesh: row: 4 (over z), col: 8 (over y, x, core).
Axes of the slice: x: 2, y: 2, z: 4, core: 2. Of those that a mesh axis runs over, the one named last changes fastest.
Arguments:
- blocks: float32 [4, 8, 170, 128, 128], P('row', 'col'), may hold values from -1 to 1
- coords: int32 [4, 8, 2, 170], P('row', 'col'), may hold values from 0 to 31, as said below
- vectors: float32 [2, 16384, 128], P(None, ('row', 'col')), may hold values from -6 to 6
Outputs:
- basis: float32 [2, 16384, 128], P(None, ('row', 'col'))
Inputs may be any that keep to these rules, and one draw needn't show every extreme that they name: Within each tile the 170 listed positions are distinct, and the positions (0, 0) and (31, 15) are always listed; coords[r, c, 0, k] is below 32 and coords[r, c, 1, k] below 16.
All inputs are finite; a program needn't handle non-finite values.
Results may differ from a plain program's by a relative error of at most 0.0003.
Values sent between devices are 32-bit elements; how exact they have to be, the bound alone decides.
No kernel may reach another device: no remote copies, remote signals or barrier semaphores. Data moves between devices by JAX's collectives and lax.ppermute only.
A program may use at most 192 MiB of HBM per device.

v0:
```python
import functools

import jax
import jax.numpy as jnp
from jax import lax
from jax.experimental import pallas as pl
from jax.experimental.pallas import tpu as pltpu
from jax.sharding import PartitionSpec as P


f32 = jnp.float32
bf16 = jnp.bfloat16
exact_mode = lax.Precision.HIGHEST


def halves(x):
    hi = x.astype(bf16)
    return hi, (x - hi.astype(f32)).astype(bf16)


def swap(x, axis, mask):
    size = lax.axis_size(axis)
    return lax.ppermute(x, axis, [(i, i ^ mask) for i in range(size)])


def chunk_of(listed):
    for size in range(min(listed, 17), 0, -1):
        if listed % size == 0:
            return size
    return 1


def tile_kernel(
    places, here, values_ref, *rest, flipped, in_shards, out_shards, listed, step_blocks, group_blocks
):
    n_in = len(in_shards)
    n_out = len(out_shards)
    in_refs = rest[:n_in]
    out_refs = rest[n_in : n_in + n_out]
    stacked, acc = rest[n_in + n_out :]
    blk = values_ref.shape[1]
    step = pl.program_id(0)

    @pl.when(step == 0)
    def _():
        acc[...] = jnp.zeros_like(acc)
        for ref, shards in zip(in_refs, in_shards):
            for place, mask in enumerate(shards):
                first = (here[0] ^ mask) * group_blocks
                for g in range(group_blocks):
                    hi, lo = halves(ref[pl.ds((place * group_blocks + g) * blk, blk), :])
                    both = jnp.concatenate([hi, lo], axis=1)
                    stacked[first + g, 0:blk, :] = both
                    stacked[first + g, blk : 2 * blk, :] = both

    sums = []
    for q in range(step_blocks):
        k = step * step_blocks + q
        i = places[0, k]
        j = places[1, k]
        source, target = (i, j) if flipped else (j, i)
        entry = values_ref[q]
        hi, lo = halves(entry.T if flipped else entry)
        p = jnp.dot(
            jnp.concatenate([hi, lo], axis=1), stacked[source], preferred_element_type=f32
        )
        nv = p.shape[1] // 2
        sums.append((target, p[:, :nv] + p[:, nv:]))
    for target, p in sums:
        acc[target] = acc[target] + p

    @pl.when(step == listed // step_blocks - 1)
    def _():
        for ref, shards in zip(out_refs, out_shards):
            for place, mask in enumerate(shards):
                first = (here[1] ^ mask) * group_blocks
                for g in range(group_blocks):
                    ref[pl.ds((place * group_blocks + g) * blk, blk), :] = acc[first + g]


def tile_products(values, places, here, pieces, in_shards, out_shards, flipped):
    listed, blk, _ = values.shape
    nv = pieces[0].shape[1]
    group = pieces[0].shape[0] // len(in_shards[0])
    group_blocks = group // blk
    step_blocks = chunk_of(listed)
    n_in = sum(len(s) for s in in_shards) * group_blocks
    n_out = sum(len(s) for s in out_shards) * group_blocks
    whole = lambda shape: pl.BlockSpec(shape, lambda g, *_: (0, 0))
    out_shapes = [(len(s) * group, nv) for s in out_shards]
    body = functools.partial(
        tile_kernel,
        flipped=flipped,
        in_shards=in_shards,
        out_shards=out_shards,
        listed=listed,
        step_blocks=step_blocks,
        group_blocks=group_blocks,
    )
    return pl.pallas_call(
        body,
        name="tile_flipped" if flipped else "tile_direct",
        out_shape=[jax.ShapeDtypeStruct(s, f32) for s in out_shapes],
        grid_spec=pltpu.PrefetchScalarGridSpec(
            num_scalar_prefetch=2,
            grid=(listed // step_blocks,),
            in_specs=[pl.BlockSpec((step_blocks, blk, blk), lambda g, *_: (g, 0, 0))]
            + [whole(p.shape) for p in pieces],
            out_specs=[whole(s) for s in out_shapes],
            scratch_shapes=[
                pltpu.VMEM((n_in, 2 * blk, 2 * nv), bf16),
                pltpu.VMEM((n_out, blk, nv), f32),
            ],
        ),
        cost_estimate=pl.CostEstimate(
            flops=2 * listed * blk * blk * nv * 4, transcendentals=0, bytes_accessed=values.size * 4
        ),
    )(places, here, values, *pieces)


def gram_kernel(here, *rest, n_upper, n_lower, scale):
    upper_refs = rest[:n_upper]
    lower_refs = rest[n_upper : n_upper + n_lower]
    rest = rest[n_upper + n_lower :]
    if scale:
        w_ref, y_ref, mine_ref, other_ref, full = rest
    else:
        mine_ref, other_ref, full = rest
    total = None
    for band, refs in enumerate((upper_refs, lower_refs)):
        y = refs[0][...]
        for r in refs[1:]:
            y = y + r[...]
        if scale:
            y = jnp.dot(y, w_ref[...], precision=exact_mode, preferred_element_type=f32)
            y_ref[band] = y
        part = lax.dot_general(
            y, y, (((0,), (0,)), ((), ())), precision=exact_mode, preferred_element_type=f32
        )
        total = part if total is None else total + part
    full[...] = total
    half = total.shape[0] // 2
    mine_ref[...] = full[pl.ds(here[0] * half, half), :]
    other_ref[...] = full[pl.ds((1 - here[0]) * half, half), :]


def gram_parts(parity, uppers, lowers, weight=None):
    rows, nv = uppers[0].shape
    half = jax.ShapeDtypeStruct((nv // 2, nv), f32)
    out_shape = [half, half]
    args = list(uppers) + list(lowers)
    if weight is not None:
        out_shape = [jax.ShapeDtypeStruct((2, rows, nv), f32)] + out_shape
        args.append(weight)
    vmem = pl.BlockSpec(memory_space=pltpu.VMEM)
    return pl.pallas_call(
        functools.partial(
            gram_kernel, n_upper=len(uppers), n_lower=len(lowers), scale=weight is not None
        ),
        name="gram_scaled" if weight is not None else "gram_plain",
        out_shape=out_shape,
        in_specs=[pl.BlockSpec(memory_space=pltpu.SMEM)] + [vmem] * len(args),
        out_specs=[vmem] * len(out_shape),
        scratch_shapes=[pltpu.VMEM((nv, nv), f32)],
    )(parity, *args)


def factor_kernel(here, *rest, n_own, total_rows, apply):
    own_refs = rest[:n_own]
    other_ref = rest[n_own]
    rest = rest[n_own + 1 :]
    if apply:
        y_ref, out_ref, full = rest
    else:
        w_ref, full = rest
    size = full.shape[0]
    half = size // 2
    own = own_refs[0][...]
    for r in own_refs[1:]:
        own = own + r[...]
    full[pl.ds(here[0] * half, half), :] = own
    full[pl.ds((1 - here[0]) * half, half), :] = other_ref[...]
    sub = 8
    inv_rows = 1.0 / total_rows
    lane = lax.broadcasted_iota(jnp.int32, (sub, size), 1)
    row_in = lax.broadcasted_iota(jnp.int32, (sub, size), 0)
    m = [full[pl.ds(g * sub, sub), :] * inv_rows for g in range(size // sub)]
    for k in range(size):
        g0, s0 = divmod(k, sub)
        at_k = lane == k
        row = m[g0][s0 : s0 + 1, :]
        pivot = row[:, k : k + 1]
        scaled = jnp.where(at_k, 1.0, jnp.broadcast_to(row, (sub, size))) * jnp.broadcast_to(
            1.0 / pivot, (sub, size)
        )
        for g in range(g0, size // sub):
            if g == g0 and s0 == sub - 1:
                continue
            col = jnp.broadcast_to(m[g][:, k : k + 1], (sub, size))
            new = jnp.where(at_k, 0.0, m[g]) - col * scaled
            m[g] = jnp.where(row_in > s0, new, m[g]) if g == g0 else new
    for g in range(size // sub):
        diag = lane == row_in + g * sub
        d = jnp.sum(jnp.where(diag, m[g], 0.0), axis=1, keepdims=True)
        unit = jnp.where(diag, 1.0, jnp.where(lane < row_in + g * sub, m[g], 0.0))
        full[pl.ds(g * sub, sub), :] = unit * lax.rsqrt(d)
    if apply:
        w = full[...]
        for band in range(2):
            out_ref[band] = lax.dot_general(
                y_ref[band],
                w,
                (((1,), (1,)), ((), ())),
                precision=exact_mode,
                preferred_element_type=f32,
            )
    else:
        w_ref[...] = full[...].T


def factor_inverse(parity, own, other, total_rows, applied=None):
    _, nv = other.shape
    vmem = pl.BlockSpec(memory_space=pltpu.VMEM)
    args = list(own) + [other]
    if applied is None:
        out_shape = jax.ShapeDtypeStruct((nv, nv), f32)
    else:
        out_shape = jax.ShapeDtypeStruct(applied.shape, f32)
        args.append(applied)
    return pl.pallas_call(
        functools.partial(
            factor_kernel, n_own=len(own), total_rows=total_rows, apply=applied is not None
        ),
        name="factor" if applied is None else "factor_apply",
        out_shape=out_shape,
        in_specs=[pl.BlockSpec(memory_space=pltpu.SMEM)] + [vmem] * len(args),
        out_specs=vmem,
        scratch_shapes=[pltpu.VMEM((nv, nv), f32)],
    )(parity, *args)


def local(blocks, coords, vectors):
    n_row = lax.axis_size("row")
    n_col = lax.axis_size("col")
    group = vectors.shape[1]
    total_rows = 2 * group * n_row * n_col
    values = blocks.reshape(blocks.shape[2], blocks.shape[3], blocks.shape[4])
    places = coords.reshape(2, coords.shape[3])
    row_id = lax.axis_index("row")
    col_id = lax.axis_index("col")
    here_direct = jnp.stack([row_id, col_id]).astype(jnp.int32)
    here_flipped = jnp.stack([col_id, row_id]).astype(jnp.int32)
    parity = (col_id & 1).astype(jnp.int32).reshape(1)
    even = list(range(2, n_col, 2))
    row_masks = list(range(1, n_row))

    def spread_row(x):
        return [x] + [swap(x, "row", m) for m in row_masks]

    def spread_col(x):
        far = [swap(x, "col", m) for m in even]
        near = swap(x, "col", 1)
        joined = [swap(f, "col", 1) for f in far]
        return [x, near] + far + joined

    row_shards = [[0]] + [[m] for m in row_masks]
    col_shards = [[0], [1]] + [[m] for m in even] + [[m ^ 1] for m in even]
    col_out = [[0] + even, [m ^ 1 for m in [0] + even]]

    def direct(pieces):
        return tile_products(values, places, here_direct, pieces, row_shards, col_out, False)

    def flipped(pieces):
        return tile_products(values, places, here_flipped, pieces, col_shards, row_shards, True)

    def gather_col(outs):
        mine, others = outs
        both = mine + swap(others, "col", 1)
        parts = [both[i * group : (i + 1) * group] for i in range(len(even) + 1)]
        return [parts[0]] + [swap(p, "col", m) for p, m in zip(parts[1:], even)]

    def gather_row(outs):
        return [outs[0]] + [swap(p, "row", m) for p, m in zip(outs[1:], row_masks)]

    def reduce_gram(mine, other):
        own = mine + swap(other, "col", 1)
        own = functools.reduce(jnp.add, [own] + [swap(own, "col", m) for m in even])
        parts = [own] + [swap(own, "row", m) for m in row_masks]
        own = functools.reduce(jnp.add, parts)
        return [own], swap(own, "col", 1)

    upper, lower = vectors[0], vectors[1]
    pieces_z = spread_row(lower)
    lower1 = functools.reduce(jnp.add, gather_row(flipped(spread_col(upper))))
    upper1 = functools.reduce(jnp.add, gather_col(direct(pieces_z)))
    pieces_z = spread_row(lower1)
    lowers = gather_row(flipped(spread_col(upper1)))
    parts = gram_parts(parity, [upper1], [lower1])
    parts = reduce_gram(*parts)
    weight = factor_inverse(parity, *parts, total_rows)
    uppers = gather_col(direct(pieces_z))
    applied, mine, other = gram_parts(parity, uppers, lowers, weight)
    parts = reduce_gram(mine, other)
    return factor_inverse(parity, *parts, total_rows, applied)


def solution(mesh):
    return jax.shard_map(
        local,
        mesh=mesh,
        in_specs=(
            P("row", "col", None, None, None),
            P("row", "col", None, None),
            P(None, ("row", "col"), None),
        ),
        out_specs=P(None, ("row", "col"), None),
        check_vma=False,
    )
```

profile of v0, /device:TPU:1, one launch (start us, length us, event | category | flops | bytes accessed | tf_op | source)
XLA Modules:
  0.0 242.8 jit_solution(10620480897526418825)
XLA Ops:
  1.1 4.2 %collective-permute-start.19 = (f32[512,128]{1,0:T(8,128)S(1)}, f32[512,128]{1,0:T(8,128)S(1)}, u32[]{:S(2)}, u32[]{:S(2)}) collective-permute-start(f32[512,128]{1,0:T(8,128)S(1)} %get-tuple-element.46.rest_0_), channel_id=1, source_target_pairs={{0,24},{8,16},{16,8},{24,0},{1,25},{9,17},{17,9},{25,1},{2,26},{10... | collective-permute-start | bytes 786440 | tf_op jit(solution)/shard_map/ppermute | solution.py:23
  7.9 3.4 %collective-permute-done.19.rest_3_ = f32[512,128]{1,0:T(8,128)S(1)} collective-permute-done((f32[512,128]{1,0:T(8,128)S(1)}, f32[512,128]{1,0:T(8,128)S(1)}, u32[]{:S(2)}, u32[]{:S(2)}) %collective-permute-start.19) | collective-permute-done | bytes 262176 | tf_op jit(solution)/shard_map/ppermute | solution.py:23
  11.4 10.5 %collective-permute-start.17 = (f32[512,128]{1,0:T(8,128)S(1)}, f32[512,128]{1,0:T(8,128)S(1)}, u32[]{:S(2)}, u32[]{:S(2)}) collective-permute-start(f32[512,128]{1,0:T(8,128)S(1)} %get-tuple-element.46.rest_0_), channel_id=1, source_target_pairs={{0,8},{8,0},{16,24},{24,16},{1,9},{9,1},{17,25},{25,17},{2,10},{10... | collective-permute-start | bytes 786440 | tf_op jit(solution)/shard_map/ppermute | solution.py:23
  22.5 4.7 %collective-permute-done.18.rest_2_ = f32[512,128]{1,0:T(8,128)S(1)} collective-permute-done((f32[512,128]{1,0:T(8,128)S(1)}, f32[512,128]{1,0:T(8,128)S(1)}, u32[]{:S(2)}, u32[]{:S(2)}) %collective-permute-start.18) | collective-permute-done | bytes 262176 | tf_op jit(solution)/shard_map/ppermute | solution.py:23
  29.3 4.0 %collective-permute-done.17.rest_1_ = f32[512,128]{1,0:T(8,128)S(1)} collective-permute-done((f32[512,128]{1,0:T(8,128)S(1)}, f32[512,128]{1,0:T(8,128)S(1)}, u32[]{:S(2)}, u32[]{:S(2)}) %collective-permute-start.17) | collective-permute-done | bytes 262176 | tf_op jit(solution)/shard_map/ppermute | solution.py:23
  34.0 12.3 %tile_direct.3 = (f32[2048,128]{1,0:T(8,128)}, f32[2048,128]{1,0:T(8,128)}) custom-call(s32[2,170]{1,0:T(2,128)} %bitcast.13, s32[2]{0:T(128)} %pad_add_fusion.here, f32[170,128,128]{2,1,0:T(8,128)} %bitcast.9, f32[512,128]{1,0:T(8,128)} %copy-done.5, f32[512,128]{1,0:T(8,128)} %copy-done.20, f32[512,128]{1,0:T(8,128)} %copy-done.14, f32[512,128]{1,0:T(8,128)} %copy-done.13), custom_call_target="tpu_custom_call" | custom-call | flops 2852126720 | bytes 11141120 | tf_op jit(solution)/shard_map/tile_direct/pallas_call | solution.py:100
  48.3 12.6 %tile_flipped.2 = (f32[512,128]{1,0:T(8,128)}, f32[512,128]{1,0:T(8,128)}, f32[512,128]{1,0:T(8,128)}, f32[512,128]{1,0:T(8,128)}) custom-call(s32[2,170]{1,0:T(2,128)} %bitcast.14, s32[2]{0:T(128)} %pad_add_fusion.1.here, f32[170,128,128]{2,1,0:T(8,128)} %bitcast.10, f32[512,128]{1,0:T(8,128)} %copy-done.4, f32[512,128]{1,0:T(8,128)} %copy-done.18, ...), custom_call_target="tpu_custom_call" | custom-call | flops 2852126720 | bytes 11141120 | tf_op jit(solution)/shard_map/tile_flipped/pallas_call | solution.py:100
  60.9 2.3 collective-permute-start.8
  64.5 9.7 %collective-permute-done.7 = f32[512,128]{1,0:T(8,128)S(1)} collective-permute-done((f32[512,128]{1,0:T(8,128)}, f32[512,128]{1,0:T(8,128)S(1)}, u32[]{:S(2)}, u32[]{:S(2)}) %collective-permute-start.7) | collective-permute-done | bytes 262176 | tf_op jit(solution)/shard_map/ppermute | solution.py:23
  74.2 6.9 %collective-permute-done.9 = f32[512,128]{1,0:T(8,128)S(1)} collective-permute-done((f32[512,128]{1,0:T(8,128)}, f32[512,128]{1,0:T(8,128)S(1)}, u32[]{:S(2)}, u32[]{:S(2)}) %collective-permute-start.9) | collective-permute-done | bytes 262176 | tf_op jit(solution)/shard_map/ppermute | solution.py:23
  84.3 10.7 %collective-permute-start.11 = (f32[512,128]{1,0:T(8,128)S(1)}, f32[512,128]{1,0:T(8,128)S(1)}, u32[]{:S(2)}, u32[]{:S(2)}) collective-permute-start(f32[512,128]{1,0:T(8,128)S(1)} %add_add_fusion.rest_0_.rest_1_), channel_id=1, source_target_pairs={{0,16},{8,24},{16,0},{24,8},{1,17},{9,25},{17,1},{25,9},{2,18},{10... | collective-permute-start | bytes 786440 | tf_op jit(solution)/shard_map/ppermute | solution.py:23
  98.7 13.4 %collective-permute-done.11.rest_2_ = f32[512,128]{1,0:T(8,128)S(1)} collective-permute-done((f32[512,128]{1,0:T(8,128)S(1)}, f32[512,128]{1,0:T(8,128)S(1)}, u32[]{:S(2)}, u32[]{:S(2)}) %collective-permute-start.11) | collective-permute-done | bytes 262176 | tf_op jit(solution)/shard_map/ppermute | solution.py:23
  112.8 12.2 %tile_direct.2 = (f32[2048,128]{1,0:T(8,128)}, f32[2048,128]{1,0:T(8,128)}) custom-call(s32[2,170]{1,0:T(2,128)} %bitcast.15, s32[2]{0:T(128)} %pad_add_fusion.here, f32[170,128,128]{2,1,0:T(8,128)} %bitcast.11, f32[512,128]{1,0:T(8,128)} %copy-done.1, f32[512,128]{1,0:T(8,128)} %collective-permute-done.10.rest_1_, f32[512,128]{1,0:T(8,128)} %copy-done.24, ...), custom_call_target="tpu_custom_call" | custom-call | flops 2852126720 | bytes 11141120 | tf_op jit(solution)/shard_map/tile_direct/pallas_call | solution.py:100
  127.8 2.4 collective-permute-start.26
  130.4 2.3 gram_plain.1
  136.2 6.3 %collective-permute-done.37 = f32[64,128]{1,0:T(8,128)S(1)} collective-permute-done((f32[64,128]{1,0:T(8,128)S(1)}, f32[64,128]{1,0:T(8,128)S(1)}, u32[]{:S(2)}, u32[]{:S(2)}) %collective-permute-start.37) | collective-permute-done | bytes 32800 | tf_op jit(solution)/shard_map/ppermute | solution.py:23
  148.0 3.6 %collective-permute-start.24 = (f32[512,128]{1,0:T(8,128)}, f32[512,128]{1,0:T(8,128)S(1)}, u32[]{:S(2)}, u32[]{:S(2)}) collective-permute-start(f32[512,128]{1,0:T(8,128)} %copy-done), channel_id=1, source_target_pairs={{0,1},{1,0},{2,3},{3,2},{4,5},{5,4},{6,7},{7,6},{8,9},{9,8},{10,11... | collective-permute-start | bytes 786440 | tf_op jit(solution)/shard_map/ppermute | solution.py:23
  157.3 12.6 %tile_flipped.3 = (f32[512,128]{1,0:T(8,128)}, f32[512,128]{1,0:T(8,128)}, f32[512,128]{1,0:T(8,128)}, f32[512,128]{1,0:T(8,128)}) custom-call(s32[2,170]{1,0:T(2,128)} %bitcast.16, s32[2]{0:T(128)} %pad_add_fusion.1.here, f32[170,128,128]{2,1,0:T(8,128)} %bitcast.12, f32[512,128]{1,0:T(8,128)} %copy-done, f32[512,128]{1,0:T(8,128)} %copy-done.17, ...), custom_call_target="tpu_custom_call" | custom-call | flops 2852126720 | bytes 11141120 | tf_op jit(solution)/shard_map/tile_flipped/pallas_call | solution.py:100
  172.7 2.4 collective-permute-start.33
  180.7 18.6 %factor.1.rest_8_ = f32[128,128]{1,0:T(8,128)} custom-call(s32[1]{0:T(128)} %bitcast.here, f32[64,128]{1,0:T(8,128)} %copy-done.29, f32[64,128]{1,0:T(8,128)} %copy-done.31), custom_call_target="tpu_custom_call" | custom-call | tf_op jit(solution)/shard_map/factor/pallas_call | solution.py:230
  200.3 3.3 %gram_scaled.1 = (f32[2,512,128]{2,1,0:T(8,128)}, f32[64,128]{1,0:T(8,128)}, f32[64,128]{1,0:T(8,128)}) custom-call(s32[1]{0:T(128)} %bitcast.here, f32[512,128]{1,0:T(8,128)} %get-tuple-element.45.rest_0_, f32[512,128]{1,0:T(8,128)} %copy-done.27, f32[512,128]{1,0:T(8,128)} %copy-done.25, f32[512,128]{1,0:T(8,128)} %copy-done.21, ...), custom_call_target="tpu_custom_call" | custom-call | tf_op jit(solution)/shard_map/gram_scaled/pallas_call | solution.py:156
  203.7 2.8 %collective-permute-start.42 = (f32[64,128]{1,0:T(8,128)}, f32[64,128]{1,0:T(8,128)S(1)}, u32[]{:S(2)}, u32[]{:S(2)}) collective-permute-start(f32[64,128]{1,0:T(8,128)} %get-tuple-element.37), channel_id=1, source_target_pairs={{0,1},{1,0},{2,3},{3,2},{4,5},{5,4},{6,7},{7,6},{8,9},{9,8},{10,11... | collective-permute-start | bytes 98312 | tf_op jit(solution)/shard_map/ppermute | solution.py:23
  218.6 3.3 %collective-permute-start.49 = (f32[64,128]{1,0:T(8,128)S(1)}, f32[64,128]{1,0:T(8,128)S(1)}, u32[]{:S(2)}, u32[]{:S(2)}) collective-permute-start(f32[64,128]{1,0:T(8,128)S(1)} %add_add_fusion.1.rest_0_), channel_id=1, source_target_pairs={{0,1},{1,0},{2,3},{3,2},{4,5},{5,4},{6,7},{7,6},{8,9},{9,8},{10,11... | collective-permute-start | bytes 98312 | tf_op jit(solution)/shard_map/ppermute | solution.py:23
  223.3 19.5 %factor_apply.1 = f32[2,512,128]{2,1,0:T(8,128)} custom-call(s32[1]{0:T(128)} %bitcast.here, f32[64,128]{1,0:T(8,128)} %copy-done.28, f32[64,128]{1,0:T(8,128)} %copy-done.30, f32[2,512,128]{2,1,0:T(8,128)} %get-tuple-element.38.rest_2_), custom_call_target="tpu_custom_call" | custom-call | tf_op jit(solution)/shard_map/factor_apply/pallas_call | solution.py:230
  (163 shorter events, 58.4 us)
Async XLA Ops:
  5.3 22.0 %collective-permute-start.18 = (f32[512,128]{1,0:T(8,128)S(1)}, f32[512,128]{1,0:T(8,128)S(1)}, u32[]{:S(2)}, u32[]{:S(2)}) collective-permute-start(f32[512,128]{1,0:T(8,128)S(1)} %get-tuple-element.46.rest_0_), channel_id=1, source_target_pairs={{0,16},{8,24},{16,0},{24,8},{1,17},{9,25},{17,1},{25,9},{2,18},{10... | collective-permute-start | bytes 786440 | tf_op jit(solution)/shard_map/ppermute | solution.py:23
  5.3 23.4 %collective-permute-start.3 = (f32[512,128]{1,0:T(8,128)S(1)}, f32[512,128]{1,0:T(8,128)S(1)}, u32[]{:S(2)}, u32[]{:S(2)}) collective-permute-start(f32[512,128]{1,0:T(8,128)S(1)} %get-tuple-element.47.rest_0_), channel_id=1, source_target_pairs={{0,6},{1,7},{2,4},{3,5},{4,2},{5,3},{6,0},{7,1},{8,14},{9,15},{10,... | collective-permute-start | bytes 786440 | tf_op jit(solution)/shard_map/ppermute | solution.py:23
  7.5 21.3 %collective-permute-start.2 = (f32[512,128]{1,0:T(8,128)S(1)}, f32[512,128]{1,0:T(8,128)S(1)}, u32[]{:S(2)}, u32[]{:S(2)}) collective-permute-start(f32[512,128]{1,0:T(8,128)S(1)} %get-tuple-element.47.rest_0_), channel_id=1, source_target_pairs={{0,4},{1,5},{2,6},{3,7},{4,0},{5,1},{6,2},{7,3},{8,12},{9,13},{10,... | collective-permute-start | bytes 786440 | tf_op jit(solution)/shard_map/ppermute | solution.py:23
  7.7 21.5 %collective-permute-start.1 = (f32[512,128]{1,0:T(8,128)S(1)}, f32[512,128]{1,0:T(8,128)S(1)}, u32[]{:S(2)}, u32[]{:S(2)}) collective-permute-start(f32[512,128]{1,0:T(8,128)S(1)} %get-tuple-element.47.rest_0_), channel_id=1, source_target_pairs={{0,2},{1,3},{2,0},{3,1},{4,6},{5,7},{6,4},{7,5},{8,10},{9,11},{10,... | collective-permute-start | bytes 786440 | tf_op jit(solution)/shard_map/ppermute | solution.py:23
  11.4 22.0 %collective-permute-start.17 = (f32[512,128]{1,0:T(8,128)S(1)}, f32[512,128]{1,0:T(8,128)S(1)}, u32[]{:S(2)}, u32[]{:S(2)}) collective-permute-start(f32[512,128]{1,0:T(8,128)S(1)} %get-tuple-element.46.rest_0_), channel_id=1, source_target_pairs={{0,8},{8,0},{16,24},{24,16},{1,9},{9,1},{17,25},{25,17},{2,10},{10... | collective-permute-start | bytes 786440 | tf_op jit(solution)/shard_map/ppermute | solution.py:23
  27.3 20.4 %collective-permute-start = (f32[512,128]{1,0:T(8,128)S(1)}, f32[512,128]{1,0:T(8,128)S(1)}, u32[]{:S(2)}, u32[]{:S(2)}) collective-permute-start(f32[512,128]{1,0:T(8,128)S(1)} %get-tuple-element.47.rest_0_), channel_id=1, source_target_pairs={{0,1},{1,0},{2,3},{3,2},{4,5},{5,4},{6,7},{7,6},{8,9},{9,8},{10,11... | collective-permute-start | bytes 786440 | tf_op jit(solution)/shard_map/ppermute | solution.py:23
  28.7 19.0 %collective-permute-start.6 = (f32[512,128]{1,0:T(8,128)S(1)}, f32[512,128]{1,0:T(8,128)}, u32[]{:S(2)}, u32[]{:S(2)}) collective-permute-start(f32[512,128]{1,0:T(8,128)S(1)} %collective-permute-done.3.rest_4_), channel_id=1, source_target_pairs={{0,1},{1,0},{2,3},{3,2},{4,5},{5,4},{6,7},{7,6},{8,9},{9,8},{10,11... | collective-permute-start | bytes 786440 | tf_op jit(solution)/shard_map/ppermute | solution.py:23
  28.8 18.9 %collective-permute-start.5 = (f32[512,128]{1,0:T(8,128)S(1)}, f32[512,128]{1,0:T(8,128)}, u32[]{:S(2)}, u32[]{:S(2)}) collective-permute-start(f32[512,128]{1,0:T(8,128)S(1)} %collective-permute-done.2.rest_3_), channel_id=1, source_target_pairs={{0,1},{1,0},{2,3},{3,2},{4,5},{5,4},{6,7},{7,6},{8,9},{9,8},{10,11... | collective-permute-start | bytes 786440 | tf_op jit(solution)/shard_map/ppermute | solution.py:23
  29.2 18.4 %collective-permute-start.4 = (f32[512,128]{1,0:T(8,128)S(1)}, f32[512,128]{1,0:T(8,128)}, u32[]{:S(2)}, u32[]{:S(2)}) collective-permute-start(f32[512,128]{1,0:T(8,128)S(1)} %collective-permute-done.1.rest_2_), channel_id=1, source_target_pairs={{0,1},{1,0},{2,3},{3,2},{4,5},{5,4},{6,7},{7,6},{8,9},{9,8},{10,11... | collective-permute-start | bytes 786440 | tf_op jit(solution)/shard_map/ppermute | solution.py:23
  46.3 48.7 %collective-permute-start.20 = (f32[2048,128]{1,0:T(8,128)}, f32[2048,128]{1,0:T(8,128)S(1)}, u32[]{:S(2)}, u32[]{:S(2)}) collective-permute-start(f32[2048,128]{1,0:T(8,128)} %get-tuple-element.29), channel_id=1, source_target_pairs={{0,1},{1,0},{2,3},{3,2},{4,5},{5,4},{6,7},{7,6},{8,9},{9,8},{10,11... | collective-permute-start | bytes 3145736 | tf_op jit(solution)/shard_map/ppermute | solution.py:23
  63.2 17.9 %collective-permute-start.9 = (f32[512,128]{1,0:T(8,128)}, f32[512,128]{1,0:T(8,128)S(1)}, u32[]{:S(2)}, u32[]{:S(2)}) collective-permute-start(f32[512,128]{1,0:T(8,128)} %get-tuple-element.25), channel_id=1, source_target_pairs={{0,24},{8,16},{16,8},{24,0},{1,25},{9,17},{17,9},{25,1},{2,26},{10... | collective-permute-start | bytes 786440 | tf_op jit(solution)/shard_map/ppermute | solution.py:23
  84.3 27.7 %collective-permute-start.11 = (f32[512,128]{1,0:T(8,128)S(1)}, f32[512,128]{1,0:T(8,128)S(1)}, u32[]{:S(2)}, u32[]{:S(2)}) collective-permute-start(f32[512,128]{1,0:T(8,128)S(1)} %add_add_fusion.rest_0_.rest_1_), channel_id=1, source_target_pairs={{0,16},{8,24},{16,0},{24,8},{1,17},{9,25},{17,1},{25,9},{2,18},{10... | collective-permute-start | bytes 786440 | tf_op jit(solution)/shard_map/ppermute | solution.py:23
  96.0 30.5 %collective-permute-start.21 = (f32[512,128]{1,0:T(8,128)}, f32[512,128]{1,0:T(8,128)}, u32[]{:S(2)}, u32[]{:S(2)}) collective-permute-start(f32[512,128]{1,0:T(8,128)} %get-tuple-element.39), channel_id=1, source_target_pairs={{0,2},{1,3},{2,0},{3,1},{4,6},{5,7},{6,4},{7,5},{8,10},{9,11},{10,... | collective-permute-start | bytes 786440 | tf_op jit(solution)/shard_map/ppermute | solution.py:23
  97.2 29.3 %collective-permute-start.23 = (f32[512,128]{1,0:T(8,128)}, f32[512,128]{1,0:T(8,128)}, u32[]{:S(2)}, u32[]{:S(2)}) collective-permute-start(f32[512,128]{1,0:T(8,128)} %get-tuple-element.40), channel_id=1, source_target_pairs={{0,6},{1,7},{2,4},{3,5},{4,2},{5,3},{6,0},{7,1},{8,14},{9,15},{10,... | collective-permute-start | bytes 786440 | tf_op jit(solution)/shard_map/ppermute | solution.py:23
  98.4 28.1 %collective-permute-start.22 = (f32[512,128]{1,0:T(8,128)S(1)}, f32[512,128]{1,0:T(8,128)}, u32[]{:S(2)}, u32[]{:S(2)}) collective-permute-start(f32[512,128]{1,0:T(8,128)S(1)} %get-tuple-element.41), channel_id=1, source_target_pairs={{0,4},{1,5},{2,6},{3,7},{4,0},{5,1},{6,2},{7,3},{8,12},{9,13},{10,... | collective-permute-start | bytes 786440 | tf_op jit(solution)/shard_map/ppermute | solution.py:23
  125.0 50.1 %collective-permute-start.13 = (f32[2048,128]{1,0:T(8,128)}, f32[2048,128]{1,0:T(8,128)S(1)}, u32[]{:S(2)}, u32[]{:S(2)}) collective-permute-start(f32[2048,128]{1,0:T(8,128)} %get-tuple-element.27), channel_id=1, source_target_pairs={{0,1},{1,0},{2,3},{3,2},{4,5},{5,4},{6,7},{7,6},{8,9},{9,8},{10,11... | collective-permute-start | bytes 3145736 | tf_op jit(solution)/shard_map/ppermute | solution.py:23
  127.7 23.9 %collective-permute-start.27 = (f32[512,128]{1,0:T(8,128)S(1)}, f32[512,128]{1,0:T(8,128)S(1)}, u32[]{:S(2)}, u32[]{:S(2)}) collective-permute-start(f32[512,128]{1,0:T(8,128)S(1)} %fusion.1.rest_0_), channel_id=1, source_target_pairs={{0,6},{1,7},{2,4},{3,5},{4,2},{5,3},{6,0},{7,1},{8,14},{9,15},{10,... | collective-permute-start | bytes 786440 | tf_op jit(solution)/shard_map/ppermute | solution.py:23
  127.8 23.9 %collective-permute-start.26 = (f32[512,128]{1,0:T(8,128)S(1)}, f32[512,128]{1,0:T(8,128)S(1)}, u32[]{:S(2)}, u32[]{:S(2)}) collective-permute-start(f32[512,128]{1,0:T(8,128)S(1)} %fusion.1.rest_0_), channel_id=1, source_target_pairs={{0,4},{1,5},{2,6},{3,7},{4,0},{5,1},{6,2},{7,3},{8,12},{9,13},{10,... | collective-permute-start | bytes 786440 | tf_op jit(solution)/shard_map/ppermute | solution.py:23
  130.2 21.9 %collective-permute-start.25 = (f32[512,128]{1,0:T(8,128)S(1)}, f32[512,128]{1,0:T(8,128)S(1)}, u32[]{:S(2)}, u32[]{:S(2)}) collective-permute-start(f32[512,128]{1,0:T(8,128)S(1)} %fusion.1.rest_0_), channel_id=1, source_target_pairs={{0,2},{1,3},{2,0},{3,1},{4,6},{5,7},{6,4},{7,5},{8,10},{9,11},{10,... | collective-permute-start | bytes 786440 | tf_op jit(solution)/shard_map/ppermute | solution.py:23
  171.9 27.4 %collective-permute-start.32 = (f32[512,128]{1,0:T(8,128)}, f32[512,128]{1,0:T(8,128)S(1)}, u32[]{:S(2)}, u32[]{:S(2)}) collective-permute-start(f32[512,128]{1,0:T(8,128)} %get-tuple-element.32), channel_id=1, source_target_pairs={{0,16},{8,24},{16,0},{24,8},{1,17},{9,25},{17,1},{25,9},{2,18},{10... | collective-permute-start | bytes 786440 | tf_op jit(solution)/shard_map/ppermute | solution.py:23
  172.7 26.6 %collective-permute-start.33 = (f32[512,128]{1,0:T(8,128)}, f32[512,128]{1,0:T(8,128)S(1)}, u32[]{:S(2)}, u32[]{:S(2)}) collective-permute-start(f32[512,128]{1,0:T(8,128)} %get-tuple-element.33), channel_id=1, source_target_pairs={{0,24},{8,16},{16,8},{24,0},{1,25},{9,17},{17,9},{25,1},{2,26},{10... | collective-permute-start | bytes 786440 | tf_op jit(solution)/shard_map/ppermute | solution.py:23
  176.0 23.3 %collective-permute-start.16 = (f32[512,128]{1,0:T(8,128)S(1)}, f32[512,128]{1,0:T(8,128)S(1)}, u32[]{:S(2)}, u32[]{:S(2)}) collective-permute-start(f32[512,128]{1,0:T(8,128)S(1)} %get-tuple-element.42), channel_id=1, source_target_pairs={{0,6},{1,7},{2,4},{3,5},{4,2},{5,3},{6,0},{7,1},{8,14},{9,15},{10,... | collective-permute-start | bytes 786440 | tf_op jit(solution)/shard_map/ppermute | solution.py:23
  176.7 22.7 %collective-permute-start.15 = (f32[512,128]{1,0:T(8,128)S(1)}, f32[512,128]{1,0:T(8,128)S(1)}, u32[]{:S(2)}, u32[]{:S(2)}) collective-permute-start(f32[512,128]{1,0:T(8,128)S(1)} %get-tuple-element.43), channel_id=1, source_target_pairs={{0,4},{1,5},{2,6},{3,7},{4,0},{5,1},{6,2},{7,3},{8,12},{9,13},{10,... | collective-permute-start | bytes 786440 | tf_op jit(solution)/shard_map/ppermute | solution.py:23
  179.5 19.8 %collective-permute-start.14 = (f32[512,128]{1,0:T(8,128)S(1)}, f32[512,128]{1,0:T(8,128)S(1)}, u32[]{:S(2)}, u32[]{:S(2)}) collective-permute-start(f32[512,128]{1,0:T(8,128)S(1)} %get-tuple-element.44), channel_id=1, source_target_pairs={{0,2},{1,3},{2,0},{3,1},{4,6},{5,7},{6,4},{7,5},{8,10},{9,11},{10,... | collective-permute-start | bytes 786440 | tf_op jit(solution)/shard_map/ppermute | solution.py:23
  (58 other events, 570.5 us)
where the time goes:
time: 244 us; the launch traced here: 243 us
  Pallas kernels  93.4 us (38%)
  starting transfers between devices  75.5 us (31%)
  waiting for transfers between devices  60.5 us (25%)
  local copies, waits for them, and re-layouts  7.79 us (3%)
  other arithmetic  5.28 us (2%)
    ppermute x50, starting transfers between devices, swap(): return lax.ppermute(x, axis, [(i, i ^ mask) for i in range(size)])  75.5 us
    ppermute x50, waiting for transfers between devices, swap(): return lax.ppermute(x, axis, [(i, i ^ mask) for i in range(size)])  60.5 us
    pallas_call x4, Pallas kernels, tile_products(): pl.pallas_call(body, name='tile_flipped' if flipped else 'tile_direct', o...  49.7 us
    pallas_call x2, Pallas kernels, factor_inverse(): pl.pallas_call(functools.partial(factor_kernel, n_own=len(own), total_row...  38.1 us
    pallas_call x2, Pallas kernels, gram_parts(): pl.pallas_call(functools.partial(gram_kernel, n_upper=len(uppers), n_lowe...  5.64 us
    unnamed x64, local copies, waits for them, and re-layouts  5.12 us
  transfers between devices with their start and end apart: 50, of which 19 were waited for; matrix products, arithmetic and copies ran while one was open for 3% of the time, Pallas kernels for 29%

commit v1 on v0

--- a/solution.py
+++ b/solution.py
@@ -170,9 +170,9 @@
     other_ref = rest[n_own]
     rest = rest[n_own + 1 :]
     if apply:
-        y_ref, out_ref, full = rest
+        y_ref, out_ref, full, rows = rest
     else:
-        w_ref, full = rest
+        w_ref, full, rows = rest
     size = full.shape[0]
     half = size // 2
     own = own_refs[0][...]
@@ -181,41 +181,72 @@
     full[pl.ds(here[0] * half, half), :] = own
     full[pl.ds((1 - here[0]) * half, half), :] = other_ref[...]
     sub = 8
-    inv_rows = 1.0 / total_rows
+    groups = size // sub
     lane = lax.broadcasted_iota(jnp.int32, (sub, size), 1)
     row_in = lax.broadcasted_iota(jnp.int32, (sub, size), 0)
-    m = [full[pl.ds(g * sub, sub), :] * inv_rows for g in range(size // sub)]
-    for k in range(size):
-        g0, s0 = divmod(k, sub)
-        at_k = lane == k
-        row = m[g0][s0 : s0 + 1, :]
-        pivot = row[:, k : k + 1]
-        scaled = jnp.where(at_k, 1.0, jnp.broadcast_to(row, (sub, size))) * jnp.broadcast_to(
-            1.0 / pivot, (sub, size)
-        )
-        for g in range(g0, size // sub):
-            if g == g0 and s0 == sub - 1:
-                continue
-            col = jnp.broadcast_to(m[g][:, k : k + 1], (sub, size))
-            new = jnp.where(at_k, 0.0, m[g]) - col * scaled
-            m[g] = jnp.where(row_in > s0, new, m[g]) if g == g0 else new
-    for g in range(size // sub):
-        diag = lane == row_in + g * sub
-        d = jnp.sum(jnp.where(diag, m[g], 0.0), axis=1, keepdims=True)
-        unit = jnp.where(diag, 1.0, jnp.where(lane < row_in + g * sub, m[g], 0.0))
-        full[pl.ds(g * sub, sub), :] = unit * lax.rsqrt(d)
+
+    def spread(x, k):
+        return jnp.broadcast_to(x[:, k : k + 1], (sub, size))
+
+    m = [full[pl.ds(g * sub, sub), :] for g in range(groups)]
+    kept = [jnp.where(lane == row_in + g * sub, m[g], 0.0) for g in range(groups)]
+    across = functools.reduce(jnp.add, [jnp.sum(x, axis=0, keepdims=True) for x in kept])
+    inv_rows = 1.0 / total_rows
+    unit_row = lax.rsqrt(across * inv_rows)
+    for g in range(groups):
+        unit_col = lax.rsqrt(jnp.sum(kept[g], axis=1, keepdims=True) * inv_rows)
+        m[g] = (m[g] * inv_rows * unit_row) * unit_col
+
+    for g0 in range(groups):
+        k = g0 * sub
+        rows[pl.ds(k, sub), :] = m[g0]
+        r = [rows[pl.ds(k + i, sub, stride=0), :] for i in range(sub)]
+        s = {(i, j): spread(r[i], k + j) for i in range(sub) for j in range(i, sub)}
+        in_panel = (lane >= k) & (lane < k + sub)
+        done = lane < k + sub
+        r = [jnp.where(lane == k + i, 1.0, jnp.where(in_panel, 0.0, r[i])) for i in range(sub)]
+        f = [None] * sub
+        q = {}
+        for i in range(0, sub, 2):
+            a, b, c = s[i, i], s[i, i + 1], s[i + 1, i + 1]
+            inv = 1.0 / (a * c - b * b)
+            t = b / a
+            first = jnp.where(done, r[i], 0.0) * lax.rsqrt(a)
+            second = jnp.where(done, r[i + 1] - t * r[i], 0.0) * lax.rsqrt(c - b * t)
+            full[pl.ds(k + i, 1), :] = first[0:1]
+            full[pl.ds(k + i + 1, 1), :] = second[0:1]
+            a, b, c = a * inv, b * inv, c * inv
+            f[i] = c * r[i] - b * r[i + 1]
+            f[i + 1] = a * r[i + 1] - b * r[i]
+            for j in range(i + 2, sub):
+                q[i, j] = c * s[i, j] - b * s[i + 1, j]
+                q[i + 1, j] = a * s[i + 1, j] - b * s[i, j]
+            for j in range(i + 2, sub):
+                r[j] = r[j] - (s[i, j] * f[i] + s[i + 1, j] * f[i + 1])
+                for l in range(j, sub):
+                    s[j, l] = s[j, l] - (s[i, j] * q[i, l] + s[i + 1, j] * q[i + 1, l])
+        for i in range(sub - 4, -1, -2):
+            for j in range(i + 2, sub):
+                f[i] = f[i] - q[i, j] * f[j]
+                f[i + 1] = f[i + 1] - q[i + 1, j] * f[j]
+        for g in range(g0 + 1, groups):
+            change = spread(m[g], k) * f[0]
+            for j in range(1, sub):
+                change = change + spread(m[g], k + j) * f[j]
+            m[g] = jnp.where(in_panel, 0.0, m[g]) - change
+
+    inverse = full[...] * unit_row
     if apply:
-        w = full[...]
         for band in range(2):
             out_ref[band] = lax.dot_general(
                 y_ref[band],
-                w,
+                inverse,
                 (((1,), (1,)), ((), ())),
                 precision=exact_mode,
                 preferred_element_type=f32,
             )
     else:
-        w_ref[...] = full[...].T
+        w_ref[...] = inverse.T
 
 
 def factor_inverse(parity, own, other, total_rows, applied=None):
@@ -235,7 +266,7 @@
         out_shape=out_shape,
         in_specs=[pl.BlockSpec(memory_space=pltpu.SMEM)] + [vmem] * len(args),
         out_specs=vmem,
-        scratch_shapes=[pltpu.VMEM((nv, nv), f32)],
+        scratch_shapes=[pltpu.VMEM((nv, nv), f32), pltpu.VMEM((nv, nv), f32)],
     )(parity, *args)
 
 

time: 244 us -> 228 us (0.934)
  Pallas kernels: 93.4 us -> 66.7 us
  waiting for transfers between devices: 60.5 us -> 68.3 us
    pallas_call x2, Pallas kernels: 38.1 us -> 11.3 us  [factor_inverse(): pl.pallas_call(functools.partial(factor_kernel, n_own=len(own), total_row...]
    ppermute x50, waiting for transfers between devices: 60.5 us -> 68.3 us  [swap(): return lax.ppermute(x, axis, [(i, i ^ mask) for i in range(size)])]
  transfers between devices with their start and end apart: 50 -> 50, of which waited for: 19 -> 20; matrix products, arithmetic and copies ran while one was open for 3% -> 3% of each run, Pallas kernels for 29% -> 25%
where the time goes in v1:
time: 228 us; the launch traced here: 226 us
  starting transfers between devices  77.7 us (34%)
  waiting for transfers between devices  68.3 us (30%)
  Pallas kernels  66.7 us (29%)
  local copies, waits for them, and re-layouts  7.8 us (3%)
  other arithmetic  5.28 us (2%)
    ppermute x50, starting transfers between devices, swap(): return lax.ppermute(x, axis, [(i, i ^ mask) for i in range(size)])  77.7 us
    ppermute x50, waiting for transfers between devices, swap(): return lax.ppermute(x, axis, [(i, i ^ mask) for i in range(size)])  68.3 us
    pallas_call x4, Pallas kernels, tile_products(): pl.pallas_call(body, name='tile_flipped' if flipped else 'tile_direct', o...  49.7 us
    pallas_call x2, Pallas kernels, factor_inverse(): pl.pallas_call(functools.partial(factor_kernel, n_own=len(own), total_row...  11.3 us
    pallas_call x2, Pallas kernels, gram_parts(): pl.pallas_call(functools.partial(gram_kernel, n_upper=len(uppers), n_lowe...  5.64 us
    unnamed x64, local copies, waits for them, and re-layouts  5.13 us
  transfers between devices with their start and end apart: 50, of which 20 were waited for; matrix products, arithmetic and copies ran while one was open for 3% of the time, Pallas kernels for 25%

profile of v1, /device:TPU:1, one launch (start us, length us, event | category | flops | bytes accessed | tf_op | source)
XLA Modules:
  0.0 226.0 jit_solution(12512710041116794676)
XLA Ops:
  1.1 4.2 %collective-permute-start.19 = (f32[512,128]{1,0:T(8,128)S(1)}, f32[512,128]{1,0:T(8,128)S(1)}, u32[]{:S(2)}, u32[]{:S(2)}) collective-permute-start(f32[512,128]{1,0:T(8,128)S(1)} %get-tuple-element.46.rest_0_), channel_id=1, source_target_pairs={{0,24},{8,16},{16,8},{24,0},{1,25},{9,17},{17,9},{25,1},{2,26},{10... | collective-permute-start | bytes 786440 | tf_op jit(solution)/shard_map/ppermute | solution.py:23
  7.9 3.4 %collective-permute-done.19.rest_3_ = f32[512,128]{1,0:T(8,128)S(1)} collective-permute-done((f32[512,128]{1,0:T(8,128)S(1)}, f32[512,128]{1,0:T(8,128)S(1)}, u32[]{:S(2)}, u32[]{:S(2)}) %collective-permute-start.19) | collective-permute-done | bytes 262176 | tf_op jit(solution)/shard_map/ppermute | solution.py:23
  11.4 10.5 %collective-permute-start.17 = (f32[512,128]{1,0:T(8,128)S(1)}, f32[512,128]{1,0:T(8,128)S(1)}, u32[]{:S(2)}, u32[]{:S(2)}) collective-permute-start(f32[512,128]{1,0:T(8,128)S(1)} %get-tuple-element.46.rest_0_), channel_id=1, source_target_pairs={{0,8},{8,0},{16,24},{24,16},{1,9},{9,1},{17,25},{25,17},{2,10},{10... | collective-permute-start | bytes 786440 | tf_op jit(solution)/shard_map/ppermute | solution.py:23
  22.5 4.7 %collective-permute-done.18.rest_2_ = f32[512,128]{1,0:T(8,128)S(1)} collective-permute-done((f32[512,128]{1,0:T(8,128)S(1)}, f32[512,128]{1,0:T(8,128)S(1)}, u32[]{:S(2)}, u32[]{:S(2)}) %collective-permute-start.18) | collective-permute-done | bytes 262176 | tf_op jit(solution)/shard_map/ppermute | solution.py:23
  29.3 4.0 %collective-permute-done.17.rest_1_ = f32[512,128]{1,0:T(8,128)S(1)} collective-permute-done((f32[512,128]{1,0:T(8,128)S(1)}, f32[512,128]{1,0:T(8,128)S(1)}, u32[]{:S(2)}, u32[]{:S(2)}) %collective-permute-start.17) | collective-permute-done | bytes 262176 | tf_op jit(solution)/shard_map/ppermute | solution.py:23
  34.0 12.3 %tile_direct.3 = (f32[2048,128]{1,0:T(8,128)}, f32[2048,128]{1,0:T(8,128)}) custom-call(s32[2,170]{1,0:T(2,128)} %bitcast.13, s32[2]{0:T(128)} %pad_add_fusion.here, f32[170,128,128]{2,1,0:T(8,128)} %bitcast.9, f32[512,128]{1,0:T(8,128)} %copy-done.5, f32[512,128]{1,0:T(8,128)} %copy-done.20, f32[512,128]{1,0:T(8,128)} %copy-done.14, f32[512,128]{1,0:T(8,128)} %copy-done.13), custom_call_target="tpu_custom_call" | custom-call | flops 2852126720 | bytes 11141120 | tf_op jit(solution)/shard_map/tile_direct/pallas_call | solution.py:100
  48.3 12.6 %tile_flipped.2 = (f32[512,128]{1,0:T(8,128)}, f32[512,128]{1,0:T(8,128)}, f32[512,128]{1,0:T(8,128)}, f32[512,128]{1,0:T(8,128)}) custom-call(s32[2,170]{1,0:T(2,128)} %bitcast.14, s32[2]{0:T(128)} %pad_add_fusion.1.here, f32[170,128,128]{2,1,0:T(8,128)} %bitcast.10, f32[512,128]{1,0:T(8,128)} %copy-done.4, f32[512,128]{1,0:T(8,128)} %copy-done.18, ...), custom_call_target="tpu_custom_call" | custom-call | flops 2852126720 | bytes 11141120 | tf_op jit(solution)/shard_map/tile_flipped/pallas_call | solution.py:100
  60.9 2.3 %collective-permute-start.8 = (f32[512,128]{1,0:T(8,128)}, f32[512,128]{1,0:T(8,128)S(1)}, u32[]{:S(2)}, u32[]{:S(2)}) collective-permute-start(f32[512,128]{1,0:T(8,128)} %get-tuple-element.24), channel_id=1, source_target_pairs={{0,16},{8,24},{16,0},{24,8},{1,17},{9,25},{17,1},{25,9},{2,18},{10... | collective-permute-start | bytes 786440 | tf_op jit(solution)/shard_map/ppermute | solution.py:23
  64.5 9.7 %collective-permute-done.7 = f32[512,128]{1,0:T(8,128)S(1)} collective-permute-done((f32[512,128]{1,0:T(8,128)}, f32[512,128]{1,0:T(8,128)S(1)}, u32[]{:S(2)}, u32[]{:S(2)}) %collective-permute-start.7) | collective-permute-done | bytes 262176 | tf_op jit(solution)/shard_map/ppermute | solution.py:23
  74.2 6.9 %collective-permute-done.9 = f32[512,128]{1,0:T(8,128)S(1)} collective-permute-done((f32[512,128]{1,0:T(8,128)}, f32[512,128]{1,0:T(8,128)S(1)}, u32[]{:S(2)}, u32[]{:S(2)}) %collective-permute-start.9) | collective-permute-done | bytes 262176 | tf_op jit(solution)/shard_map/ppermute | solution.py:23
  84.3 10.7 %collective-permute-start.11 = (f32[512,128]{1,0:T(8,128)S(1)}, f32[512,128]{1,0:T(8,128)S(1)}, u32[]{:S(2)}, u32[]{:S(2)}) collective-permute-start(f32[512,128]{1,0:T(8,128)S(1)} %add_add_fusion.rest_0_.rest_1_), channel_id=1, source_target_pairs={{0,16},{8,24},{16,0},{24,8},{1,17},{9,25},{17,1},{25,9},{2,18},{10... | collective-permute-start | bytes 786440 | tf_op jit(solution)/shard_map/ppermute | solution.py:23
  98.7 13.4 %collective-permute-done.11.rest_2_ = f32[512,128]{1,0:T(8,128)S(1)} collective-permute-done((f32[512,128]{1,0:T(8,128)S(1)}, f32[512,128]{1,0:T(8,128)S(1)}, u32[]{:S(2)}, u32[]{:S(2)}) %collective-permute-start.11) | collective-permute-done | bytes 262176 | tf_op jit(solution)/shard_map/ppermute | solution.py:23
  112.8 12.2 %tile_direct.2 = (f32[2048,128]{1,0:T(8,128)}, f32[2048,128]{1,0:T(8,128)}) custom-call(s32[2,170]{1,0:T(2,128)} %bitcast.15, s32[2]{0:T(128)} %pad_add_fusion.here, f32[170,128,128]{2,1,0:T(8,128)} %bitcast.11, f32[512,128]{1,0:T(8,128)} %copy-done.1, f32[512,128]{1,0:T(8,128)} %collective-permute-done.10.rest_1_, f32[512,128]{1,0:T(8,128)} %copy-done.24, ...), custom_call_target="tpu_custom_call" | custom-call | flops 2852126720 | bytes 11141120 | tf_op jit(solution)/shard_map/tile_direct/pallas_call | solution.py:100
  127.8 2.4 %collective-permute-start.26 = (f32[512,128]{1,0:T(8,128)S(1)}, f32[512,128]{1,0:T(8,128)S(1)}, u32[]{:S(2)}, u32[]{:S(2)}) collective-permute-start(f32[512,128]{1,0:T(8,128)S(1)} %fusion.1.rest_0_), channel_id=1, source_target_pairs={{0,4},{1,5},{2,6},{3,7},{4,0},{5,1},{6,2},{7,3},{8,12},{9,13},{10,... | collective-permute-start | bytes 786440 | tf_op jit(solution)/shard_map/ppermute | solution.py:23
  136.2 6.3 %collective-permute-done.37 = f32[64,128]{1,0:T(8,128)S(1)} collective-permute-done((f32[64,128]{1,0:T(8,128)S(1)}, f32[64,128]{1,0:T(8,128)S(1)}, u32[]{:S(2)}, u32[]{:S(2)}) %collective-permute-start.37) | collective-permute-done | bytes 32800 | tf_op jit(solution)/shard_map/ppermute | solution.py:23
  148.0 3.6 %collective-permute-start.24 = (f32[512,128]{1,0:T(8,128)}, f32[512,128]{1,0:T(8,128)S(1)}, u32[]{:S(2)}, u32[]{:S(2)}) collective-permute-start(f32[512,128]{1,0:T(8,128)} %copy-done), channel_id=1, source_target_pairs={{0,1},{1,0},{2,3},{3,2},{4,5},{5,4},{6,7},{7,6},{8,9},{9,8},{10,11... | collective-permute-start | bytes 786440 | tf_op jit(solution)/shard_map/ppermute | solution.py:23
  157.3 12.6 %tile_flipped.3 = (f32[512,128]{1,0:T(8,128)}, f32[512,128]{1,0:T(8,128)}, f32[512,128]{1,0:T(8,128)}, f32[512,128]{1,0:T(8,128)}) custom-call(s32[2,170]{1,0:T(2,128)} %bitcast.16, s32[2]{0:T(128)} %pad_add_fusion.1.here, f32[170,128,128]{2,1,0:T(8,128)} %bitcast.12, f32[512,128]{1,0:T(8,128)} %copy-done, f32[512,128]{1,0:T(8,128)} %copy-done.17, ...), custom_call_target="tpu_custom_call" | custom-call | flops 2852126720 | bytes 11141120 | tf_op jit(solution)/shard_map/tile_flipped/pallas_call | solution.py:100
  172.7 2.4 %collective-permute-start.33 = (f32[512,128]{1,0:T(8,128)}, f32[512,128]{1,0:T(8,128)S(1)}, u32[]{:S(2)}, u32[]{:S(2)}) collective-permute-start(f32[512,128]{1,0:T(8,128)} %get-tuple-element.33), channel_id=1, source_target_pairs={{0,24},{8,16},{16,8},{24,0},{1,25},{9,17},{17,9},{25,1},{2,26},{10... | collective-permute-start | bytes 786440 | tf_op jit(solution)/shard_map/ppermute | solution.py:23
  180.7 4.9 %factor.1.rest_8_ = f32[128,128]{1,0:T(8,128)} custom-call(s32[1]{0:T(128)} %bitcast.here, f32[64,128]{1,0:T(8,128)} %copy-done.29, f32[64,128]{1,0:T(8,128)} %copy-done.31), custom_call_target="tpu_custom_call" | custom-call | tf_op jit(solution)/shard_map/factor/pallas_call | solution.py:261
  185.6 6.5 %collective-permute-done.32.rest_6_ = f32[512,128]{1,0:T(8,128)S(1)} collective-permute-done((f32[512,128]{1,0:T(8,128)}, f32[512,128]{1,0:T(8,128)S(1)}, u32[]{:S(2)}, u32[]{:S(2)}) %collective-permute-start.32) | collective-permute-done | bytes 262176 | tf_op jit(solution)/shard_map/ppermute | solution.py:23
  193.1 3.3 %gram_scaled.1 = (f32[2,512,128]{2,1,0:T(8,128)}, f32[64,128]{1,0:T(8,128)}, f32[64,128]{1,0:T(8,128)}) custom-call(s32[1]{0:T(128)} %bitcast.here, f32[512,128]{1,0:T(8,128)} %get-tuple-element.45.rest_0_, f32[512,128]{1,0:T(8,128)} %copy-done.27, f32[512,128]{1,0:T(8,128)} %copy-done.25, f32[512,128]{1,0:T(8,128)} %copy-done.21, ...), custom_call_target="tpu_custom_call" | custom-call | tf_op jit(solution)/shard_map/gram_scaled/pallas_call | solution.py:156
  206.2 5.3 %collective-permute-start.47 = (f32[64,128]{1,0:T(8,128)S(1)}, f32[64,128]{1,0:T(8,128)S(1)}, u32[]{:S(2)}, u32[]{:S(2)}) collective-permute-start(f32[64,128]{1,0:T(8,128)S(1)} %add_add_fusion.2), channel_id=1, source_target_pairs={{0,16},{8,24},{16,0},{24,8},{1,17},{9,25},{17,1},{25,9},{2,18},{10... | collective-permute-start | bytes 98312 | tf_op jit(solution)/shard_map/ppermute | solution.py:23
  214.3 3.8 %collective-permute-start.49 = (f32[64,128]{1,0:T(8,128)S(1)}, f32[64,128]{1,0:T(8,128)S(1)}, u32[]{:S(2)}, u32[]{:S(2)}) collective-permute-start(f32[64,128]{1,0:T(8,128)S(1)} %add_add_fusion.1.rest_0_), channel_id=1, source_target_pairs={{0,1},{1,0},{2,3},{3,2},{4,5},{5,4},{6,7},{7,6},{8,9},{9,8},{10,11... | collective-permute-start | bytes 98312 | tf_op jit(solution)/shard_map/ppermute | solution.py:23
  219.6 6.5 %factor_apply.1 = f32[2,512,128]{2,1,0:T(8,128)} custom-call(s32[1]{0:T(128)} %bitcast.here, f32[64,128]{1,0:T(8,128)} %copy-done.28, f32[64,128]{1,0:T(8,128)} %copy-done.30, f32[2,512,128]{2,1,0:T(8,128)} %get-tuple-element.38.rest_2_), custom_call_target="tpu_custom_call" | custom-call | tf_op jit(solution)/shard_map/factor_apply/pallas_call | solution.py:261
  (163 shorter events, 61.2 us)
Async XLA Ops:
  5.3 22.0 %collective-permute-start.18 = (f32[512,128]{1,0:T(8,128)S(1)}, f32[512,128]{1,0:T(8,128)S(1)}, u32[]{:S(2)}, u32[]{:S(2)}) collective-permute-start(f32[512,128]{1,0:T(8,128)S(1)} %get-tuple-element.46.rest_0_), channel_id=1, source_target_pairs={{0,16},{8,24},{16,0},{24,8},{1,17},{9,25},{17,1},{25,9},{2,18},{10... | collective-permute-start | bytes 786440 | tf_op jit(solution)/shard_map/ppermute | solution.py:23
  5.3 23.4 %collective-permute-start.3 = (f32[512,128]{1,0:T(8,128)S(1)}, f32[512,128]{1,0:T(8,128)S(1)}, u32[]{:S(2)}, u32[]{:S(2)}) collective-permute-start(f32[512,128]{1,0:T(8,128)S(1)} %get-tuple-element.47.rest_0_), channel_id=1, source_target_pairs={{0,6},{1,7},{2,4},{3,5},{4,2},{5,3},{6,0},{7,1},{8,14},{9,15},{10,... | collective-permute-start | bytes 786440 | tf_op jit(solution)/shard_map/ppermute | solution.py:23
  7.5 21.3 %collective-permute-start.2 = (f32[512,128]{1,0:T(8,128)S(1)}, f32[512,128]{1,0:T(8,128)S(1)}, u32[]{:S(2)}, u32[]{:S(2)}) collective-permute-start(f32[512,128]{1,0:T(8,128)S(1)} %get-tuple-element.47.rest_0_), channel_id=1, source_target_pairs={{0,4},{1,5},{2,6},{3,7},{4,0},{5,1},{6,2},{7,3},{8,12},{9,13},{10,... | collective-permute-start | bytes 786440 | tf_op jit(solution)/shard_map/ppermute | solution.py:23
  7.7 21.5 %collective-permute-start.1 = (f32[512,128]{1,0:T(8,128)S(1)}, f32[512,128]{1,0:T(8,128)S(1)}, u32[]{:S(2)}, u32[]{:S(2)}) collective-permute-start(f32[512,128]{1,0:T(8,128)S(1)} %get-tuple-element.47.rest_0_), channel_id=1, source_target_pairs={{0,2},{1,3},{2,0},{3,1},{4,6},{5,7},{6,4},{7,5},{8,10},{9,11},{10,... | collective-permute-start | bytes 786440 | tf_op jit(solution)/shard_map/ppermute | solution.py:23
  11.4 22.0 %collective-permute-start.17 = (f32[512,128]{1,0:T(8,128)S(1)}, f32[512,128]{1,0:T(8,128)S(1)}, u32[]{:S(2)}, u32[]{:S(2)}) collective-permute-start(f32[512,128]{1,0:T(8,128)S(1)} %get-tuple-element.46.rest_0_), channel_id=1, source_target_pairs={{0,8},{8,0},{16,24},{24,16},{1,9},{9,1},{17,25},{25,17},{2,10},{10... | collective-permute-start | bytes 786440 | tf_op jit(solution)/shard_map/ppermute | solution.py:23
  27.3 20.4 %collective-permute-start = (f32[512,128]{1,0:T(8,128)S(1)}, f32[512,128]{1,0:T(8,128)S(1)}, u32[]{:S(2)}, u32[]{:S(2)}) collective-permute-start(f32[512,128]{1,0:T(8,128)S(1)} %get-tuple-element.47.rest_0_), channel_id=1, source_target_pairs={{0,1},{1,0},{2,3},{3,2},{4,5},{5,4},{6,7},{7,6},{8,9},{9,8},{10,11... | collective-permute-start | bytes 786440 | tf_op jit(solution)/shard_map/ppermute | solution.py:23
  28.7 19.0 %collective-permute-start.6 = (f32[512,128]{1,0:T(8,128)S(1)}, f32[512,128]{1,0:T(8,128)}, u32[]{:S(2)}, u32[]{:S(2)}) collective-permute-start(f32[512,128]{1,0:T(8,128)S(1)} %collective-permute-done.3.rest_4_), channel_id=1, source_target_pairs={{0,1},{1,0},{2,3},{3,2},{4,5},{5,4},{6,7},{7,6},{8,9},{9,8},{10,11... | collective-permute-start | bytes 786440 | tf_op jit(solution)/shard_map/ppermute | solution.py:23
  28.8 18.9 %collective-permute-start.5 = (f32[512,128]{1,0:T(8,128)S(1)}, f32[512,128]{1,0:T(8,128)}, u32[]{:S(2)}, u32[]{:S(2)}) collective-permute-start(f32[512,128]{1,0:T(8,128)S(1)} %collective-permute-done.2.rest_3_), channel_id=1, source_target_pairs={{0,1},{1,0},{2,3},{3,2},{4,5},{5,4},{6,7},{7,6},{8,9},{9,8},{10,11... | collective-permute-start | bytes 786440 | tf_op jit(solution)/shard_map/ppermute | solution.py:23
  29.2 18.4 %collective-permute-start.4 = (f32[512,128]{1,0:T(8,128)S(1)}, f32[512,128]{1,0:T(8,128)}, u32[]{:S(2)}, u32[]{:S(2)}) collective-permute-start(f32[512,128]{1,0:T(8,128)S(1)} %collective-permute-done.1.rest_2_), channel_id=1, source_target_pairs={{0,1},{1,0},{2,3},{3,2},{4,5},{5,4},{6,7},{7,6},{8,9},{9,8},{10,11... | collective-permute-start | bytes 786440 | tf_op jit(solution)/shard_map/ppermute | solution.py:23
  46.3 48.7 %collective-permute-start.20 = (f32[2048,128]{1,0:T(8,128)}, f32[2048,128]{1,0:T(8,128)S(1)}, u32[]{:S(2)}, u32[]{:S(2)}) collective-permute-start(f32[2048,128]{1,0:T(8,128)} %get-tuple-element.29), channel_id=1, source_target_pairs={{0,1},{1,0},{2,3},{3,2},{4,5},{5,4},{6,7},{7,6},{8,9},{9,8},{10,11... | collective-permute-start | bytes 3145736 | tf_op jit(solution)/shard_map/ppermute | solution.py:23
  63.2 17.9 %collective-permute-start.9 = (f32[512,128]{1,0:T(8,128)}, f32[512,128]{1,0:T(8,128)S(1)}, u32[]{:S(2)}, u32[]{:S(2)}) collective-permute-start(f32[512,128]{1,0:T(8,128)} %get-tuple-element.25), channel_id=1, source_target_pairs={{0,24},{8,16},{16,8},{24,0},{1,25},{9,17},{17,9},{25,1},{2,26},{10... | collective-permute-start | bytes 786440 | tf_op jit(solution)/shard_map/ppermute | solution.py:23
  84.3 27.7 %collective-permute-start.11 = (f32[512,128]{1,0:T(8,128)S(1)}, f32[512,128]{1,0:T(8,128)S(1)}, u32[]{:S(2)}, u32[]{:S(2)}) collective-permute-start(f32[512,128]{1,0:T(8,128)S(1)} %add_add_fusion.rest_0_.rest_1_), channel_id=1, source_target_pairs={{0,16},{8,24},{16,0},{24,8},{1,17},{9,25},{17,1},{25,9},{2,18},{10... | collective-permute-start | bytes 786440 | tf_op jit(solution)/shard_map/ppermute | solution.py:23
  95.0 17.7 %collective-permute-start.10 = (f32[512,128]{1,0:T(8,128)S(1)}, f32[512,128]{1,0:T(8,128)}, u32[]{:S(2)}, u32[]{:S(2)}) collective-permute-start(f32[512,128]{1,0:T(8,128)S(1)} %add_add_fusion.rest_0_.rest_1_), channel_id=1, source_target_pairs={{0,8},{8,0},{16,24},{24,16},{1,9},{9,1},{17,25},{25,17},{2,10},{10... | collective-permute-start | bytes 786440 | tf_op jit(solution)/shard_map/ppermute | solution.py:23
  96.0 30.5 %collective-permute-start.21 = (f32[512,128]{1,0:T(8,128)}, f32[512,128]{1,0:T(8,128)}, u32[]{:S(2)}, u32[]{:S(2)}) collective-permute-start(f32[512,128]{1,0:T(8,128)} %get-tuple-element.39), channel_id=1, source_target_pairs={{0,2},{1,3},{2,0},{3,1},{4,6},{5,7},{6,4},{7,5},{8,10},{9,11},{10,... | collective-permute-start | bytes 786440 | tf_op jit(solution)/shard_map/ppermute | solution.py:23
  97.2 29.3 %collective-permute-start.23 = (f32[512,128]{1,0:T(8,128)}, f32[512,128]{1,0:T(8,128)}, u32[]{:S(2)}, u32[]{:S(2)}) collective-permute-start(f32[512,128]{1,0:T(8,128)} %get-tuple-element.40), channel_id=1, source_target_pairs={{0,6},{1,7},{2,4},{3,5},{4,2},{5,3},{6,0},{7,1},{8,14},{9,15},{10,... | collective-permute-start | bytes 786440 | tf_op jit(solution)/shard_map/ppermute | solution.py:23
  98.4 28.1 %collective-permute-start.22 = (f32[512,128]{1,0:T(8,128)S(1)}, f32[512,128]{1,0:T(8,128)}, u32[]{:S(2)}, u32[]{:S(2)}) collective-permute-start(f32[512,128]{1,0:T(8,128)S(1)} %get-tuple-element.41), channel_id=1, source_target_pairs={{0,4},{1,5},{2,6},{3,7},{4,0},{5,1},{6,2},{7,3},{8,12},{9,13},{10,... | collective-permute-start | bytes 786440 | tf_op jit(solution)/shard_map/ppermute | solution.py:23
  125.0 50.1 %collective-permute-start.13 = (f32[2048,128]{1,0:T(8,128)}, f32[2048,128]{1,0:T(8,128)S(1)}, u32[]{:S(2)}, u32[]{:S(2)}) collective-permute-start(f32[2048,128]{1,0:T(8,128)} %get-tuple-element.27), channel_id=1, source_target_pairs={{0,1},{1,0},{2,3},{3,2},{4,5},{5,4},{6,7},{7,6},{8,9},{9,8},{10,11... | collective-permute-start | bytes 3145736 | tf_op jit(solution)/shard_map/ppermute | solution.py:23
  127.7 23.9 %collective-permute-start.27 = (f32[512,128]{1,0:T(8,128)S(1)}, f32[512,128]{1,0:T(8,128)S(1)}, u32[]{:S(2)}, u32[]{:S(2)}) collective-permute-start(f32[512,128]{1,0:T(8,128)S(1)} %fusion.1.rest_0_), channel_id=1, source_target_pairs={{0,6},{1,7},{2,4},{3,5},{4,2},{5,3},{6,0},{7,1},{8,14},{9,15},{10,... | collective-permute-start | bytes 786440 | tf_op jit(solution)/shard_map/ppermute | solution.py:23
  127.8 23.9 %collective-permute-start.26 = (f32[512,128]{1,0:T(8,128)S(1)}, f32[512,128]{1,0:T(8,128)S(1)}, u32[]{:S(2)}, u32[]{:S(2)}) collective-permute-start(f32[512,128]{1,0:T(8,128)S(1)} %fusion.1.rest_0_), channel_id=1, source_target_pairs={{0,4},{1,5},{2,6},{3,7},{4,0},{5,1},{6,2},{7,3},{8,12},{9,13},{10,... | collective-permute-start | bytes 786440 | tf_op jit(solution)/shard_map/ppermute | solution.py:23
  130.2 21.9 %collective-permute-start.25 = (f32[512,128]{1,0:T(8,128)S(1)}, f32[512,128]{1,0:T(8,128)S(1)}, u32[]{:S(2)}, u32[]{:S(2)}) collective-permute-start(f32[512,128]{1,0:T(8,128)S(1)} %fusion.1.rest_0_), channel_id=1, source_target_pairs={{0,2},{1,3},{2,0},{3,1},{4,6},{5,7},{6,4},{7,5},{8,10},{9,11},{10,... | collective-permute-start | bytes 786440 | tf_op jit(solution)/shard_map/ppermute | solution.py:23
  153.0 17.6 %collective-permute-start.40 = (f32[64,128]{1,0:T(8,128)S(1)}, f32[64,128]{1,0:T(8,128)S(1)}, u32[]{:S(2)}, u32[]{:S(2)}) collective-permute-start(f32[64,128]{1,0:T(8,128)S(1)} %add_add_fusion.4), channel_id=1, source_target_pairs={{0,24},{8,16},{16,8},{24,0},{1,25},{9,17},{17,9},{25,1},{2,26},{10... | collective-permute-start | bytes 98312 | tf_op jit(solution)/shard_map/ppermute | solution.py:23
  153.9 16.7 %collective-permute-start.39 = (f32[64,128]{1,0:T(8,128)S(1)}, f32[64,128]{1,0:T(8,128)S(1)}, u32[]{:S(2)}, u32[]{:S(2)}) collective-permute-start(f32[64,128]{1,0:T(8,128)S(1)} %add_add_fusion.4), channel_id=1, source_target_pairs={{0,16},{8,24},{16,0},{24,8},{1,17},{9,25},{17,1},{25,9},{2,18},{10... | collective-permute-start | bytes 98312 | tf_op jit(solution)/shard_map/ppermute | solution.py:23
  171.9 20.2 %collective-permute-start.32 = (f32[512,128]{1,0:T(8,128)}, f32[512,128]{1,0:T(8,128)S(1)}, u32[]{:S(2)}, u32[]{:S(2)}) collective-permute-start(f32[512,128]{1,0:T(8,128)} %get-tuple-element.32), channel_id=1, source_target_pairs={{0,16},{8,24},{16,0},{24,8},{1,17},{9,25},{17,1},{25,9},{2,18},{10... | collective-permute-start | bytes 786440 | tf_op jit(solution)/shard_map/ppermute | solution.py:23
  172.7 19.4 %collective-permute-start.33 = (f32[512,128]{1,0:T(8,128)}, f32[512,128]{1,0:T(8,128)S(1)}, u32[]{:S(2)}, u32[]{:S(2)}) collective-permute-start(f32[512,128]{1,0:T(8,128)} %get-tuple-element.33), channel_id=1, source_target_pairs={{0,24},{8,16},{16,8},{24,0},{1,25},{9,17},{17,9},{25,1},{2,26},{10... | collective-permute-start | bytes 786440 | tf_op jit(solution)/shard_map/ppermute | solution.py:23
  (58 other events, 559.8 us)

commit v2 on v1

--- a/solution.py
+++ b/solution.py
@@ -24,94 +24,103 @@
 
 
 def chunk_of(listed):
-    for size in range(min(listed, 17), 0, -1):
+    for size in range(min(listed, 34), 0, -1):
         if listed % size == 0:
             return size
     return 1
 
 
+def room(*arrays):
+    return sum(a.size * a.dtype.itemsize for a in arrays) + (4 << 20)
+
+
 def tile_kernel(
-    places, here, values_ref, *rest, flipped, in_shards, out_shards, listed, step_blocks, group_blocks
+    places, here, values_ref, *rest, flipped, in_shards, out_shards, step_blocks, group_blocks
 ):
     n_in = len(in_shards)
     n_out = len(out_shards)
     in_refs = rest[:n_in]
     out_refs = rest[n_in : n_in + n_out]
-    stacked, acc = rest[n_in + n_out :]
-    blk = values_ref.shape[1]
-    step = pl.program_id(0)
-
-    @pl.when(step == 0)
-    def _():
-        acc[...] = jnp.zeros_like(acc)
-        for ref, shards in zip(in_refs, in_shards):
-            for place, mask in enumerate(shards):
-                first = (here[0] ^ mask) * group_blocks
-                for g in range(group_blocks):
-                    hi, lo = halves(ref[pl.ds((place * group_blocks + g) * blk, blk), :])
-                    both = jnp.concatenate([hi, lo], axis=1)
-                    stacked[first + g, 0:blk, :] = both
-                    stacked[first + g, blk : 2 * blk, :] = both
-
-    sums = []
-    for q in range(step_blocks):
-        k = step * step_blocks + q
-        i = places[0, k]
-        j = places[1, k]
-        source, target = (i, j) if flipped else (j, i)
-        entry = values_ref[q]
-        hi, lo = halves(entry.T if flipped else entry)
-        p = jnp.dot(
-            jnp.concatenate([hi, lo], axis=1), stacked[source], preferred_element_type=f32
-        )
-        nv = p.shape[1] // 2
-        sums.append((target, p[:, :nv] + p[:, nv:]))
-    for target, p in sums:
-        acc[target] = acc[target] + p
-
-    @pl.when(step == listed // step_blocks - 1)
-    def _():
-        for ref, shards in zip(out_refs, out_shards):
-            for place, mask in enumerate(shards):
-                first = (here[1] ^ mask) * group_blocks
-                for g in range(group_blocks):
-                    ref[pl.ds((place * group_blocks + g) * blk, blk), :] = acc[first + g]
+    stacked, acc, held, sems = rest[n_in + n_out :]
+    listed, blk, _ = values_ref.shape
+    steps = listed // step_blocks
+
+    def fetch(step):
+        part = pl.ds(step * step_blocks, step_blocks)
+        return pltpu.make_async_copy(values_ref.at[part], held.at[part], sems.at[step])
+
+    for step in range(steps):
+        fetch(step).start()
+    acc[...] = jnp.zeros_like(acc)
+    for mask in sorted(set(in_shards)):
+        refs = [r for r, m in zip(in_refs, in_shards) if m == mask]
+        first = (here[0] ^ mask) * group_blocks
+        for g in range(group_blocks):
+            part = functools.reduce(jnp.add, [r[pl.ds(g * blk, blk), :] for r in refs])
+            both = jnp.concatenate(halves(part), axis=1)
+            stacked[first + g, 0:blk, :] = both
+            stacked[first + g, blk : 2 * blk, :] = both
+
+    def run(step, carry):
+        fetch(step).wait()
+        sums = []
+        for q in range(step_blocks):
+            k = step * step_blocks + q
+            i = places[0, k]
+            j = places[1, k]
+            source, target = (i, j) if flipped else (j, i)
+            entry = held[k]
+            hi, lo = halves(entry.T if flipped else entry)
+            p = jnp.dot(
+                jnp.concatenate([hi, lo], axis=1), stacked[source], preferred_element_type=f32
+            )
+            nv = p.shape[1] // 2
+            sums.append((target, p[:, :nv] + p[:, nv:]))
+        for target, p in sums:
+            acc[target] = acc[target] + p
+        return carry
+
+    lax.fori_loop(0, steps, run, 0)
+    for ref, shards in zip(out_refs, out_shards):
+        for place, mask in enumerate(shards):
+            first = (here[1] ^ mask) * group_blocks
+            for g in range(group_blocks):
+                ref[pl.ds((place * group_blocks + g) * blk, blk), :] = acc[first + g]
 
 
 def tile_products(values, places, here, pieces, in_shards, out_shards, flipped):
     listed, blk, _ = values.shape
     nv = pieces[0].shape[1]
-    group = pieces[0].shape[0] // len(in_shards[0])
+    group = pieces[0].shape[0]
     group_blocks = group // blk
     step_blocks = chunk_of(listed)
-    n_in = sum(len(s) for s in in_shards) * group_blocks
+    n_in = len(set(in_shards)) * group_blocks
     n_out = sum(len(s) for s in out_shards) * group_blocks
-    whole = lambda shape: pl.BlockSpec(shape, lambda g, *_: (0, 0))
-    out_shapes = [(len(s) * group, nv) for s in out_shards]
+    vmem = pl.BlockSpec(memory_space=pltpu.VMEM)
+    smem = pl.BlockSpec(memory_space=pltpu.SMEM)
+    out_shape = [jax.ShapeDtypeStruct((len(s) * group, nv), f32) for s in out_shards]
+    scratch = [
+        jax.ShapeDtypeStruct((n_in, 2 * blk, 2 * nv), bf16),
+        jax.ShapeDtypeStruct((n_out, blk, nv), f32),
+        jax.ShapeDtypeStruct(values.shape, f32),
+    ]
     body = functools.partial(
         tile_kernel,
         flipped=flipped,
         in_shards=in_shards,
         out_shards=out_shards,
-        listed=listed,
         step_blocks=step_blocks,
         group_blocks=group_blocks,
     )
     return pl.pallas_call(
         body,
         name="tile_flipped" if flipped else "tile_direct",
-        out_shape=[jax.ShapeDtypeStruct(s, f32) for s in out_shapes],
-        grid_spec=pltpu.PrefetchScalarGridSpec(
-            num_scalar_prefetch=2,
-            grid=(listed // step_blocks,),
-            in_specs=[pl.BlockSpec((step_blocks, blk, blk), lambda g, *_: (g, 0, 0))]
-            + [whole(p.shape) for p in pieces],
-            out_specs=[whole(s) for s in out_shapes],
-            scratch_shapes=[
-                pltpu.VMEM((n_in, 2 * blk, 2 * nv), bf16),
-                pltpu.VMEM((n_out, blk, nv), f32),
-            ],
-        ),
+        out_shape=out_shape,
+        in_specs=[smem, smem, pl.BlockSpec(memory_space=pl.ANY)] + [vmem] * len(pieces),
+        out_specs=[vmem] * len(out_shape),
+        scratch_shapes=[pltpu.VMEM(s.shape, s.dtype) for s in scratch]
+        + [pltpu.SemaphoreType.DMA((listed // step_blocks,))],
+        compiler_params=pltpu.CompilerParams(vmem_limit_bytes=50 << 20),
         cost_estimate=pl.CostEstimate(
             flops=2 * listed * blk * blk * nv * 4, transcendentals=0, bytes_accessed=values.size * 4
         ),
@@ -162,6 +171,7 @@
         in_specs=[pl.BlockSpec(memory_space=pltpu.SMEM)] + [vmem] * len(args),
         out_specs=[vmem] * len(out_shape),
         scratch_shapes=[pltpu.VMEM((nv, nv), f32)],
+        compiler_params=pltpu.CompilerParams(vmem_limit_bytes=room(*out_shape, *args)),
     )(parity, *args)
 
 
@@ -267,6 +277,7 @@
         in_specs=[pl.BlockSpec(memory_space=pltpu.SMEM)] + [vmem] * len(args),
         out_specs=vmem,
         scratch_shapes=[pltpu.VMEM((nv, nv), f32), pltpu.VMEM((nv, nv), f32)],
+        compiler_params=pltpu.CompilerParams(vmem_limit_bytes=room(out_shape, *args)),
     )(parity, *args)
 
 
@@ -286,7 +297,13 @@
     row_masks = list(range(1, n_row))
 
     def spread_row(x):
-        return [x] + [swap(x, "row", m) for m in row_masks]
+        if n_row != 4:
+            return [x] + [swap(x, "row", m) for m in row_masks]
+        two = swap(x, "row", 2)
+        one = swap(x, "row", 1)
+        inner = lax.ppermute(x, "row", [(1, 2), (2, 1)])
+        outer = lax.ppermute(two, "row", [(1, 0), (2, 3)])
+        return [x, one, two, inner, outer]
 
     def spread_col(x):
         far = [swap(x, "col", m) for m in even]
@@ -294,15 +311,16 @@
         joined = [swap(f, "col", 1) for f in far]
         return [x, near] + far + joined
 
-    row_shards = [[0]] + [[m] for m in row_masks]
-    col_shards = [[0], [1]] + [[m] for m in even] + [[m ^ 1] for m in even]
+    row_in = [0] + row_masks + ([3] if n_row == 4 else [])
+    row_out = [[m] for m in [0] + row_masks]
+    col_in = [0, 1] + even + [m ^ 1 for m in even]
     col_out = [[0] + even, [m ^ 1 for m in [0] + even]]
 
     def direct(pieces):
-        return tile_products(values, places, here_direct, pieces, row_shards, col_out, False)
+        return tile_products(values, places, here_direct, pieces, row_in, col_out, False)
 
     def flipped(pieces):
-        return tile_products(values, places, here_flipped, pieces, col_shards, row_shards, True)
+        return tile_products(values, places, here_flipped, pieces, col_in, row_out, True)
 
     def gather_col(outs):
         mine, others = outs

time: 228 us -> 185 us (0.81)
  Pallas kernels: 66.7 us -> 36.1 us
  local copies, waits for them, and re-layouts: 7.8 us -> 1.88 us
  starting transfers between devices: 77.7 us -> 72.1 us
  waiting for transfers between devices: 68.3 us -> 72 us
  other arithmetic: 5.28 us -> 1.85 us
    pallas_call x4, Pallas kernels: 49.7 us -> 25.5 us  [tile_products(): pl.pallas_call(body, name='tile_flipped' if flipped else 'tile_direct', o...]
    ppermute x50 -> x48, starting transfers between devices: 77.7 us -> 68.3 us  [swap(): return lax.ppermute(x, axis, [(i, i ^ mask) for i in range(size)])]
    unnamed x64 -> x4, local copies, waits for them, and re-layouts: 5.13 us -> 0.69 us
    ppermute x0 -> x4, starting transfers between devices: none -> 3.89 us  [the longest x2 2.56 us: spread_row(): outer = lax.ppermute(two, 'row', [(1, 0), (2, 3)])]
    pallas_call x2, Pallas kernels: 5.64 us -> 1.94 us  [gram_parts(): pl.pallas_call(functools.partial(gram_kernel, n_upper=len(uppers), n_lowe...]
    ppermute x0 -> x4, waiting for transfers between devices: none -> 3.19 us  [the longest x2 3.18 us: spread_row(): outer = lax.ppermute(two, 'row', [(1, 0), (2, 3)])]
    pallas_call x2, Pallas kernels: 11.3 us -> 8.71 us  [factor_inverse(): pl.pallas_call(functools.partial(factor_kernel, n_own=len(own), total_row...]
    ppermute x50 -> x48, waiting for transfers between devices: 68.3 us -> 68.8 us  [swap(): return lax.ppermute(x, axis, [(i, i ^ mask) for i in range(size)])]
  transfers between devices with their start and end apart: 50 -> 52, of which waited for: 20 -> 20; matrix products, arithmetic and copies ran while one was open for 3% -> 1% of each run, Pallas kernels for 25% -> 16%
where the time goes in v2:
time: 185 us; the launch traced here: 184 us
  starting transfers between devices  72.1 us (39%)
  waiting for transfers between devices  72 us (39%)
  Pallas kernels  36.1 us (20%)
  local copies, waits for them, and re-layouts  1.88 us (1%)
  other arithmetic  1.85 us (1%)
    ppermute x48, waiting for transfers between devices, swap(): return lax.ppermute(x, axis, [(i, i ^ mask) for i in range(size)])  68.8 us
    ppermute x48, starting transfers between devices, swap(): return lax.ppermute(x, axis, [(i, i ^ mask) for i in range(size)])  68.3 us
    pallas_call x4, Pallas kernels, tile_products(): pl.pallas_call(body, name='tile_flipped' if flipped else 'tile_direct', o...  25.5 us
    pallas_call x2, Pallas kernels, factor_inverse(): pl.pallas_call(functools.partial(factor_kernel, n_own=len(own), total_row...  8.71 us
  transfers between devices with their start and end apart: 52, of which 20 were waited for; matrix products, arithmetic and copies ran while one was open for 1% of the time, Pallas kernels for 16%

profile of v2, /device:TPU:1, one launch (start us, length us, event | category | flops | bytes accessed | tf_op | source)
XLA Modules:
  0.0 184.3 jit_solution(1847788321624140692)
XLA Ops:
  1.1 3.2 %collective-permute-start.19 = (f32[512,128]{1,0:T(8,128)S(1)}, f32[512,128]{1,0:T(8,128)S(1)}, u32[]{:S(2)}, u32[]{:S(2)}) collective-permute-start(f32[512,128]{1,0:T(8,128)S(1)} %get-tuple-element.46.rest_0_), channel_id=1, source_target_pairs={{0,16},{8,24},{16,0},{24,8},{1,17},{9,25},{17,1},{25,9},{2,18},{10... | collective-permute-start | bytes 786440 | tf_op jit(solution)/shard_map/ppermute | solution.py:23
  8.7 7.2 %collective-permute-done.19.rest_2_ = f32[512,128]{1,0:T(8,128)S(1)} collective-permute-done((f32[512,128]{1,0:T(8,128)S(1)}, f32[512,128]{1,0:T(8,128)S(1)}, u32[]{:S(2)}, u32[]{:S(2)}) %collective-permute-start.19) | collective-permute-done | bytes 262176 | tf_op jit(solution)/shard_map/ppermute | solution.py:23
  19.3 2.9 %collective-permute-start = (f32[512,128]{1,0:T(8,128)S(1)}, f32[512,128]{1,0:T(8,128)S(1)}, u32[]{:S(2)}, u32[]{:S(2)}) collective-permute-start(f32[512,128]{1,0:T(8,128)S(1)} %get-tuple-element.47.rest_0_), channel_id=1, source_target_pairs={{0,1},{1,0},{2,3},{3,2},{4,5},{5,4},{6,7},{7,6},{8,9},{9,8},{10,11... | collective-permute-start | bytes 786440 | tf_op jit(solution)/shard_map/ppermute | solution.py:23
  22.8 2.8 %collective-permute-start.6 = (f32[512,128]{1,0:T(8,128)S(1)}, f32[512,128]{1,0:T(8,128)S(1)}, u32[]{:S(2)}, u32[]{:S(2)}) collective-permute-start(f32[512,128]{1,0:T(8,128)S(1)} %collective-permute-done.3.rest_4_), channel_id=1, source_target_pairs={{0,1},{1,0},{2,3},{3,2},{4,5},{5,4},{6,7},{7,6},{8,9},{9,8},{10,11... | collective-permute-start | bytes 786440 | tf_op jit(solution)/shard_map/ppermute | solution.py:23
  26.2 6.2 %tile_direct.3 = (f32[2048,128]{1,0:T(8,128)S(1)}, f32[2048,128]{1,0:T(8,128)S(1)}) custom-call(s32[2,170]{1,0:T(2,128)S(1)} %bitcast.9, s32[2]{0:T(128)S(1)} %pad_add_fusion.here, f32[170,128,128]{2,1,0:T(8,128)} %bitcast.13, f32[512,128]{1,0:T(8,128)S(1)} %get-tuple-element.46.rest_0_, f32[512,128]{1,0:T(8,128)S(1)} %collective-permute-done.18.rest_1_, ...), custom_call_target="tpu_custom_call" | custom-call | flops 2852126720 | bytes 11141120 | tf_op jit(solution)/shard_map/tile_direct/pallas_call | solution.py:115
  32.4 3.6 %collective-permute-start.22 = (f32[2048,128]{1,0:T(8,128)S(1)}, f32[2048,128]{1,0:T(8,128)S(1)}, u32[]{:S(2)}, u32[]{:S(2)}) collective-permute-start(f32[2048,128]{1,0:T(8,128)S(1)} %get-tuple-element.29), channel_id=1, source_target_pairs={{0,1},{1,0},{2,3},{3,2},{4,5},{5,4},{6,7},{7,6},{8,9},{9,8},{10,11... | collective-permute-start | bytes 3145736 | tf_op jit(solution)/shard_map/ppermute | solution.py:23
  36.0 6.5 %tile_flipped.2 = (f32[512,128]{1,0:T(8,128)S(1)}, f32[512,128]{1,0:T(8,128)S(1)}, f32[512,128]{1,0:T(8,128)S(1)}, f32[512,128]{1,0:T(8,128)S(1)}) custom-call(s32[2,170]{1,0:T(2,128)S(1)} %bitcast.10, s32[2]{0:T(128)S(1)} %pad_add_fusion.1.here, f32[170,128,128]{2,1,0:T(8,128)} %bitcast.14, f32[512,128]{1,0:T(8,128)S(1)} %get-tuple-element.47.rest_0_, ...), custom_call_target="tpu_custom_call" | custom-call | flops 2852126720 | bytes 11141120 | tf_op jit(solution)/shard_map/tile_flipped/pallas_call | solution.py:115
  42.6 3.9 %collective-permute-start.8 = (f32[512,128]{1,0:T(8,128)S(1)}, f32[512,128]{1,0:T(8,128)S(1)}, u32[]{:S(2)}, u32[]{:S(2)}) collective-permute-start(f32[512,128]{1,0:T(8,128)S(1)} %get-tuple-element.24), channel_id=1, source_target_pairs={{0,16},{8,24},{16,0},{24,8},{1,17},{9,25},{17,1},{25,9},{2,18},{10... | collective-permute-start | bytes 786440 | tf_op jit(solution)/shard_map/ppermute | solution.py:23
  46.5 9.2 %collective-permute-done.7 = f32[512,128]{1,0:T(8,128)S(1)} collective-permute-done((f32[512,128]{1,0:T(8,128)S(1)}, f32[512,128]{1,0:T(8,128)S(1)}, u32[]{:S(2)}, u32[]{:S(2)}) %collective-permute-start.7) | collective-permute-done | bytes 262176 | tf_op jit(solution)/shard_map/ppermute | solution.py:23
  55.7 8.5 %collective-permute-done.9 = f32[512,128]{1,0:T(8,128)S(1)} collective-permute-done((f32[512,128]{1,0:T(8,128)S(1)}, f32[512,128]{1,0:T(8,128)S(1)}, u32[]{:S(2)}, u32[]{:S(2)}) %collective-permute-start.9) | collective-permute-done | bytes 262176 | tf_op jit(solution)/shard_map/ppermute | solution.py:23
  64.2 6.9 %collective-permute-start.11 = (f32[512,128]{1,0:T(8,128)S(1)}, f32[512,128]{1,0:T(8,128)S(1)}, u32[]{:S(2)}, u32[]{:S(2)}) collective-permute-start(f32[512,128]{1,0:T(8,128)S(1)} %add_add_fusion.rest_0_.rest_1_), channel_id=1, source_target_pairs={{0,16},{8,24},{16,0},{24,8},{1,17},{9,25},{17,1},{25,9},{2,18},{10... | collective-permute-start | bytes 786440 | tf_op jit(solution)/shard_map/ppermute | solution.py:23
  71.8 10.8 %collective-permute-done.11.rest_2_ = f32[512,128]{1,0:T(8,128)S(1)} collective-permute-done((f32[512,128]{1,0:T(8,128)S(1)}, f32[512,128]{1,0:T(8,128)S(1)}, u32[]{:S(2)}, u32[]{:S(2)}) %collective-permute-start.11) | collective-permute-done | bytes 262176 | tf_op jit(solution)/shard_map/ppermute | solution.py:23
  86.8 3.2 %collective-permute-done.13.rest_4_ = f32[512,128]{1,0:T(8,128)S(1)} collective-permute-done((f32[512,128]{1,0:T(8,128)S(1)}, f32[512,128]{1,0:T(8,128)S(1)}, u32[]{:S(2)}, u32[]{:S(2)}) %collective-permute-start.13) | collective-permute-done | bytes 262176 | tf_op jit(solution)/shard_map/ppermute | solution.py:305
  90.0 6.2 %tile_direct.2 = (f32[2048,128]{1,0:T(8,128)S(1)}, f32[2048,128]{1,0:T(8,128)S(1)}) custom-call(s32[2,170]{1,0:T(2,128)S(1)} %bitcast.11, s32[2]{0:T(128)S(1)} %pad_add_fusion.here, f32[170,128,128]{2,1,0:T(8,128)} %bitcast.15, f32[512,128]{1,0:T(8,128)S(1)} %add_add_fusion.rest_0_.rest_1_, f32[512,128]{1,0:T(8,128)S(1)} %collective-permute-done.10.rest_1_, ...), custom_call_target="tpu_custom_call" | custom-call | flops 2852126720 | bytes 11141120 | tf_op jit(solution)/shard_map/tile_direct/pallas_call | solution.py:115
  96.2 3.5 %collective-permute-start.14 = (f32[2048,128]{1,0:T(8,128)S(1)}, f32[2048,128]{1,0:T(8,128)}, u32[]{:S(2)}, u32[]{:S(2)}) collective-permute-start(f32[2048,128]{1,0:T(8,128)S(1)} %get-tuple-element.27), channel_id=1, source_target_pairs={{0,1},{1,0},{2,3},{3,2},{4,5},{5,4},{6,7},{7,6},{8,9},{9,8},{10,11... | collective-permute-start | bytes 3145736 | tf_op jit(solution)/shard_map/ppermute | solution.py:23
  105.2 8.8 %collective-permute-done.37 = f32[64,128]{1,0:T(8,128)S(1)} collective-permute-done((f32[64,128]{1,0:T(8,128)S(1)}, f32[64,128]{1,0:T(8,128)S(1)}, u32[]{:S(2)}, u32[]{:S(2)}) %collective-permute-start.37) | collective-permute-done | bytes 32800 | tf_op jit(solution)/shard_map/ppermute | solution.py:23
  116.9 3.5 %collective-permute-done.39 = f32[64,128]{1,0:T(8,128)S(1)} collective-permute-done((f32[64,128]{1,0:T(8,128)S(1)}, f32[64,128]{1,0:T(8,128)S(1)}, u32[]{:S(2)}, u32[]{:S(2)}) %collective-permute-start.39) | collective-permute-done | bytes 32800 | tf_op jit(solution)/shard_map/ppermute | solution.py:23
  120.4 3.2 %collective-permute-start.26 = (f32[512,128]{1,0:T(8,128)S(1)}, f32[512,128]{1,0:T(8,128)S(1)}, u32[]{:S(2)}, u32[]{:S(2)}) collective-permute-start(f32[512,128]{1,0:T(8,128)S(1)} %fusion.1.rest_0_), channel_id=1, source_target_pairs={{0,1},{1,0},{2,3},{3,2},{4,5},{5,4},{6,7},{7,6},{8,9},{9,8},{10,11... | collective-permute-start | bytes 786440 | tf_op jit(solution)/shard_map/ppermute | solution.py:23
  128.3 6.6 %tile_flipped.3 = (f32[512,128]{1,0:T(8,128)S(1)}, f32[512,128]{1,0:T(8,128)S(1)}, f32[512,128]{1,0:T(8,128)S(1)}, f32[512,128]{1,0:T(8,128)S(1)}) custom-call(s32[2,170]{1,0:T(2,128)S(1)} %bitcast.12, s32[2]{0:T(128)S(1)} %pad_add_fusion.1.here, f32[170,128,128]{2,1,0:T(8,128)} %bitcast.16, f32[512,128]{1,0:T(8,128)S(1)} %fusion.1.rest_0_, ...), custom_call_target="tpu_custom_call" | custom-call | flops 2852126720 | bytes 11141120 | tf_op jit(solution)/shard_map/tile_flipped/pallas_call | solution.py:115
  145.0 3.5 %factor.1.rest_8_ = f32[128,128]{1,0:T(8,128)S(1)} custom-call(s32[1]{0:T(128)} %bitcast.here, f32[64,128]{1,0:T(8,128)S(1)} %add_add_fusion.3.rest_0_, f32[64,128]{1,0:T(8,128)S(1)} %collective-permute-done.43.rest_1_), custom_call_target="tpu_custom_call" | custom-call | tf_op jit(solution)/shard_map/factor/pallas_call | solution.py:271
  148.4 7.9 %collective-permute-done.34.rest_6_ = f32[512,128]{1,0:T(8,128)S(1)} collective-permute-done((f32[512,128]{1,0:T(8,128)S(1)}, f32[512,128]{1,0:T(8,128)S(1)}, u32[]{:S(2)}, u32[]{:S(2)}) %collective-permute-start.34) | collective-permute-done | bytes 262176 | tf_op jit(solution)/shard_map/ppermute | solution.py:23
  164.4 5.4 %collective-permute-start.48 = (f32[64,128]{1,0:T(8,128)S(1)}, f32[64,128]{1,0:T(8,128)S(1)}, u32[]{:S(2)}, u32[]{:S(2)}) collective-permute-start(f32[64,128]{1,0:T(8,128)S(1)} %add_add_fusion.2), channel_id=1, source_target_pairs={{0,8},{8,0},{16,24},{24,16},{1,9},{9,1},{17,25},{25,17},{2,10},{10... | collective-permute-start | bytes 98312 | tf_op jit(solution)/shard_map/ppermute | solution.py:23
  174.8 3.4 %collective-permute-start.51 = (f32[64,128]{1,0:T(8,128)S(1)}, f32[64,128]{1,0:T(8,128)S(1)}, u32[]{:S(2)}, u32[]{:S(2)}) collective-permute-start(f32[64,128]{1,0:T(8,128)S(1)} %add_add_fusion.1.rest_0_), channel_id=1, source_target_pairs={{0,1},{1,0},{2,3},{3,2},{4,5},{5,4},{6,7},{7,6},{8,9},{9,8},{10,11... | collective-permute-start | bytes 98312 | tf_op jit(solution)/shard_map/ppermute | solution.py:23
  179.0 5.2 %factor_apply.1 = f32[2,512,128]{2,1,0:T(8,128)} custom-call(s32[1]{0:T(128)} %bitcast.here, f32[64,128]{1,0:T(8,128)S(1)} %add_add_fusion.1.rest_0_, f32[64,128]{1,0:T(8,128)S(1)} %collective-permute-done.51.rest_1_, f32[2,512,128]{2,1,0:T(8,128)S(1)} %get-tuple-element.38.rest_2_), custom_call_target="tpu_custom_call" | custom-call | tf_op jit(solution)/shard_map/factor_apply/pallas_call | solution.py:271
  (107 shorter events, 52.2 us)
Async XLA Ops:
  1.1 14.9 %collective-permute-start.19 = (f32[512,128]{1,0:T(8,128)S(1)}, f32[512,128]{1,0:T(8,128)S(1)}, u32[]{:S(2)}, u32[]{:S(2)}) collective-permute-start(f32[512,128]{1,0:T(8,128)S(1)} %get-tuple-element.46.rest_0_), channel_id=1, source_target_pairs={{0,16},{8,24},{16,0},{24,8},{1,17},{9,25},{17,1},{25,9},{2,18},{10... | collective-permute-start | bytes 786440 | tf_op jit(solution)/shard_map/ppermute | solution.py:23
  4.3 13.6 %collective-permute-start.18 = (f32[512,128]{1,0:T(8,128)S(1)}, f32[512,128]{1,0:T(8,128)S(1)}, u32[]{:S(2)}, u32[]{:S(2)}) collective-permute-start(f32[512,128]{1,0:T(8,128)S(1)} %get-tuple-element.46.rest_0_), channel_id=1, source_target_pairs={{0,8},{8,0},{16,24},{24,16},{1,9},{9,1},{17,25},{25,17},{2,10},{10... | collective-permute-start | bytes 786440 | tf_op jit(solution)/shard_map/ppermute | solution.py:23
  5.6 13.8 %collective-permute-start.20 = (f32[512,128]{1,0:T(8,128)S(1)}, f32[512,128]{1,0:T(8,128)S(1)}, u32[]{:S(2)}, u32[]{:S(2)}) collective-permute-start(f32[512,128]{1,0:T(8,128)S(1)} %get-tuple-element.46.rest_0_), channel_id=1, source_target_pairs={{8,16},{16,8},{9,17},{17,9},{10,18},{18,10},{11,19},{19,11},{12,20... | collective-permute-start | bytes 786440 | tf_op jit(solution)/shard_map/ppermute | solution.py:304
  6.2 16.0 %collective-permute-start.1 = (f32[512,128]{1,0:T(8,128)S(1)}, f32[512,128]{1,0:T(8,128)S(1)}, u32[]{:S(2)}, u32[]{:S(2)}) collective-permute-start(f32[512,128]{1,0:T(8,128)S(1)} %get-tuple-element.47.rest_0_), channel_id=1, source_target_pairs={{0,2},{1,3},{2,0},{3,1},{4,6},{5,7},{6,4},{7,5},{8,10},{9,11},{10,... | collective-permute-start | bytes 786440 | tf_op jit(solution)/shard_map/ppermute | solution.py:23
  7.5 14.8 %collective-permute-start.2 = (f32[512,128]{1,0:T(8,128)S(1)}, f32[512,128]{1,0:T(8,128)S(1)}, u32[]{:S(2)}, u32[]{:S(2)}) collective-permute-start(f32[512,128]{1,0:T(8,128)S(1)} %get-tuple-element.47.rest_0_), channel_id=1, source_target_pairs={{0,4},{1,5},{2,6},{3,7},{4,0},{5,1},{6,2},{7,3},{8,12},{9,13},{10,... | collective-permute-start | bytes 786440 | tf_op jit(solution)/shard_map/ppermute | solution.py:23
  19.3 16.7 %collective-permute-start = (f32[512,128]{1,0:T(8,128)S(1)}, f32[512,128]{1,0:T(8,128)S(1)}, u32[]{:S(2)}, u32[]{:S(2)}) collective-permute-start(f32[512,128]{1,0:T(8,128)S(1)} %get-tuple-element.47.rest_0_), channel_id=1, source_target_pairs={{0,1},{1,0},{2,3},{3,2},{4,5},{5,4},{6,7},{7,6},{8,9},{9,8},{10,11... | collective-permute-start | bytes 786440 | tf_op jit(solution)/shard_map/ppermute | solution.py:23
  22.2 13.8 %collective-permute-start.4 = (f32[512,128]{1,0:T(8,128)S(1)}, f32[512,128]{1,0:T(8,128)S(1)}, u32[]{:S(2)}, u32[]{:S(2)}) collective-permute-start(f32[512,128]{1,0:T(8,128)S(1)} %collective-permute-done.1.rest_2_), channel_id=1, source_target_pairs={{0,1},{1,0},{2,3},{3,2},{4,5},{5,4},{6,7},{7,6},{8,9},{9,8},{10,11... | collective-permute-start | bytes 786440 | tf_op jit(solution)/shard_map/ppermute | solution.py:23
  22.3 13.7 %collective-permute-start.5 = (f32[512,128]{1,0:T(8,128)S(1)}, f32[512,128]{1,0:T(8,128)S(1)}, u32[]{:S(2)}, u32[]{:S(2)}) collective-permute-start(f32[512,128]{1,0:T(8,128)S(1)} %collective-permute-done.2.rest_3_), channel_id=1, source_target_pairs={{0,1},{1,0},{2,3},{3,2},{4,5},{5,4},{6,7},{7,6},{8,9},{9,8},{10,11... | collective-permute-start | bytes 786440 | tf_op jit(solution)/shard_map/ppermute | solution.py:23
  32.4 51.5 %collective-permute-start.22 = (f32[2048,128]{1,0:T(8,128)S(1)}, f32[2048,128]{1,0:T(8,128)S(1)}, u32[]{:S(2)}, u32[]{:S(2)}) collective-permute-start(f32[2048,128]{1,0:T(8,128)S(1)} %get-tuple-element.29), channel_id=1, source_target_pairs={{0,1},{1,0},{2,3},{3,2},{4,5},{5,4},{6,7},{7,6},{8,9},{9,8},{10,11... | collective-permute-start | bytes 3145736 | tf_op jit(solution)/shard_map/ppermute | solution.py:23
  46.5 17.6 %collective-permute-start.9 = (f32[512,128]{1,0:T(8,128)S(1)}, f32[512,128]{1,0:T(8,128)S(1)}, u32[]{:S(2)}, u32[]{:S(2)}) collective-permute-start(f32[512,128]{1,0:T(8,128)S(1)} %get-tuple-element.25), channel_id=1, source_target_pairs={{0,24},{8,16},{16,8},{24,0},{1,25},{9,17},{17,9},{25,1},{2,26},{10... | collective-permute-start | bytes 786440 | tf_op jit(solution)/shard_map/ppermute | solution.py:23
  64.2 18.4 %collective-permute-start.11 = (f32[512,128]{1,0:T(8,128)S(1)}, f32[512,128]{1,0:T(8,128)S(1)}, u32[]{:S(2)}, u32[]{:S(2)}) collective-permute-start(f32[512,128]{1,0:T(8,128)S(1)} %add_add_fusion.rest_0_.rest_1_), channel_id=1, source_target_pairs={{0,16},{8,24},{16,0},{24,8},{1,17},{9,25},{17,1},{25,9},{2,18},{10... | collective-permute-start | bytes 786440 | tf_op jit(solution)/shard_map/ppermute | solution.py:23
  71.2 13.5 %collective-permute-start.10 = (f32[512,128]{1,0:T(8,128)S(1)}, f32[512,128]{1,0:T(8,128)S(1)}, u32[]{:S(2)}, u32[]{:S(2)}) collective-permute-start(f32[512,128]{1,0:T(8,128)S(1)} %add_add_fusion.rest_0_.rest_1_), channel_id=1, source_target_pairs={{0,8},{8,0},{16,24},{24,16},{1,9},{9,1},{17,25},{25,17},{2,10},{10... | collective-permute-start | bytes 786440 | tf_op jit(solution)/shard_map/ppermute | solution.py:23
  71.2 15.7 %collective-permute-start.12 = (f32[512,128]{1,0:T(8,128)S(1)}, f32[512,128]{1,0:T(8,128)S(1)}, u32[]{:S(2)}, u32[]{:S(2)}) collective-permute-start(f32[512,128]{1,0:T(8,128)S(1)} %add_add_fusion.rest_0_.rest_1_), channel_id=1, source_target_pairs={{8,16},{16,8},{9,17},{17,9},{10,18},{18,10},{11,19},{19,11},{12,20... | collective-permute-start | bytes 786440 | tf_op jit(solution)/shard_map/ppermute | solution.py:304
  84.1 15.6 %collective-permute-start.23 = (f32[512,128]{1,0:T(8,128)S(1)}, f32[512,128]{1,0:T(8,128)S(1)}, u32[]{:S(2)}, u32[]{:S(2)}) collective-permute-start(f32[512,128]{1,0:T(8,128)S(1)} %get-tuple-element.39), channel_id=1, source_target_pairs={{0,2},{1,3},{2,0},{3,1},{4,6},{5,7},{6,4},{7,5},{8,10},{9,11},{10,... | collective-permute-start | bytes 786440 | tf_op jit(solution)/shard_map/ppermute | solution.py:23
  84.5 15.2 %collective-permute-start.24 = (f32[512,128]{1,0:T(8,128)S(1)}, f32[512,128]{1,0:T(8,128)S(1)}, u32[]{:S(2)}, u32[]{:S(2)}) collective-permute-start(f32[512,128]{1,0:T(8,128)S(1)} %get-tuple-element.41), channel_id=1, source_target_pairs={{0,4},{1,5},{2,6},{3,7},{4,0},{5,1},{6,2},{7,3},{8,12},{9,13},{10,... | collective-permute-start | bytes 786440 | tf_op jit(solution)/shard_map/ppermute | solution.py:23
  84.7 15.0 %collective-permute-start.25 = (f32[512,128]{1,0:T(8,128)S(1)}, f32[512,128]{1,0:T(8,128)S(1)}, u32[]{:S(2)}, u32[]{:S(2)}) collective-permute-start(f32[512,128]{1,0:T(8,128)S(1)} %get-tuple-element.40), channel_id=1, source_target_pairs={{0,6},{1,7},{2,4},{3,5},{4,2},{5,3},{6,0},{7,1},{8,14},{9,15},{10,... | collective-permute-start | bytes 786440 | tf_op jit(solution)/shard_map/ppermute | solution.py:23
  96.2 44.0 %collective-permute-start.14 = (f32[2048,128]{1,0:T(8,128)S(1)}, f32[2048,128]{1,0:T(8,128)}, u32[]{:S(2)}, u32[]{:S(2)}) collective-permute-start(f32[2048,128]{1,0:T(8,128)S(1)} %get-tuple-element.27), channel_id=1, source_target_pairs={{0,1},{1,0},{2,3},{3,2},{4,5},{5,4},{6,7},{7,6},{8,9},{9,8},{10,11... | collective-permute-start | bytes 3145736 | tf_op jit(solution)/shard_map/ppermute | solution.py:23
  99.8 23.8 %collective-permute-start.27 = (f32[512,128]{1,0:T(8,128)S(1)}, f32[512,128]{1,0:T(8,128)S(1)}, u32[]{:S(2)}, u32[]{:S(2)}) collective-permute-start(f32[512,128]{1,0:T(8,128)S(1)} %fusion.1.rest_0_), channel_id=1, source_target_pairs={{0,2},{1,3},{2,0},{3,1},{4,6},{5,7},{6,4},{7,5},{8,10},{9,11},{10,... | collective-permute-start | bytes 786440 | tf_op jit(solution)/shard_map/ppermute | solution.py:23
  100.1 23.5 %collective-permute-start.28 = (f32[512,128]{1,0:T(8,128)S(1)}, f32[512,128]{1,0:T(8,128)S(1)}, u32[]{:S(2)}, u32[]{:S(2)}) collective-permute-start(f32[512,128]{1,0:T(8,128)S(1)} %fusion.1.rest_0_), channel_id=1, source_target_pairs={{0,4},{1,5},{2,6},{3,7},{4,0},{5,1},{6,2},{7,3},{8,12},{9,13},{10,... | collective-permute-start | bytes 786440 | tf_op jit(solution)/shard_map/ppermute | solution.py:23
  100.3 23.8 %collective-permute-start.29 = (f32[512,128]{1,0:T(8,128)S(1)}, f32[512,128]{1,0:T(8,128)S(1)}, u32[]{:S(2)}, u32[]{:S(2)}) collective-permute-start(f32[512,128]{1,0:T(8,128)S(1)} %fusion.1.rest_0_), channel_id=1, source_target_pairs={{0,6},{1,7},{2,4},{3,5},{4,2},{5,3},{6,0},{7,1},{8,14},{9,15},{10,... | collective-permute-start | bytes 786440 | tf_op jit(solution)/shard_map/ppermute | solution.py:23
  136.4 20.0 %collective-permute-start.34 = (f32[512,128]{1,0:T(8,128)S(1)}, f32[512,128]{1,0:T(8,128)S(1)}, u32[]{:S(2)}, u32[]{:S(2)}) collective-permute-start(f32[512,128]{1,0:T(8,128)S(1)} %get-tuple-element.32), channel_id=1, source_target_pairs={{0,16},{8,24},{16,0},{24,8},{1,17},{9,25},{17,1},{25,9},{2,18},{10... | collective-permute-start | bytes 786440 | tf_op jit(solution)/shard_map/ppermute | solution.py:23
  138.0 18.4 %collective-permute-start.35 = (f32[512,128]{1,0:T(8,128)S(1)}, f32[512,128]{1,0:T(8,128)S(1)}, u32[]{:S(2)}, u32[]{:S(2)}) collective-permute-start(f32[512,128]{1,0:T(8,128)S(1)} %get-tuple-element.33), channel_id=1, source_target_pairs={{0,24},{8,16},{16,8},{24,0},{1,25},{9,17},{17,9},{25,1},{2,26},{10... | collective-permute-start | bytes 786440 | tf_op jit(solution)/shard_map/ppermute | solution.py:23
  141.6 14.8 %collective-permute-start.15 = (f32[512,128]{1,0:T(8,128)S(1)}, f32[512,128]{1,0:T(8,128)S(1)}, u32[]{:S(2)}, u32[]{:S(2)}) collective-permute-start(f32[512,128]{1,0:T(8,128)S(1)} %get-tuple-element.44), channel_id=1, source_target_pairs={{0,2},{1,3},{2,0},{3,1},{4,6},{5,7},{6,4},{7,5},{8,10},{9,11},{10,... | collective-permute-start | bytes 786440 | tf_op jit(solution)/shard_map/ppermute | solution.py:23
  142.0 14.4 %collective-permute-start.16 = (f32[512,128]{1,0:T(8,128)S(1)}, f32[512,128]{1,0:T(8,128)S(1)}, u32[]{:S(2)}, u32[]{:S(2)}) collective-permute-start(f32[512,128]{1,0:T(8,128)S(1)} %get-tuple-element.43), channel_id=1, source_target_pairs={{0,4},{1,5},{2,6},{3,7},{4,0},{5,1},{6,2},{7,3},{8,12},{9,13},{10,... | collective-permute-start | bytes 786440 | tf_op jit(solution)/shard_map/ppermute | solution.py:23
  (30 other events, 267.1 us)

commit v3 on v2

--- a/solution.py
+++ b/solution.py
@@ -294,7 +294,7 @@
     here_flipped = jnp.stack([col_id, row_id]).astype(jnp.int32)
     parity = (col_id & 1).astype(jnp.int32).reshape(1)
     even = list(range(2, n_col, 2))
-    row_masks = list(range(1, n_row))
+    row_masks = list(range(1, n_row))[::-1]
 
     def spread_row(x):
         if n_row != 4:
@@ -311,10 +311,12 @@
         joined = [swap(f, "col", 1) for f in far]
         return [x, near] + far + joined
 
-    row_in = [0] + row_masks + ([3] if n_row == 4 else [])
+    row_in = [0, 1, 2, 3, 3] if n_row == 4 else [0] + row_masks
     row_out = [[m] for m in [0] + row_masks]
     col_in = [0, 1] + even + [m ^ 1 for m in even]
-    col_out = [[0] + even, [m ^ 1 for m in [0] + even]]
+    order = even + [0]
+    col_masks = [p for p in (order[: len(order) // 2], order[len(order) // 2 :]) if p]
+    col_out = col_masks + [[m ^ 1 for m in p] for p in col_masks]
 
     def direct(pieces):
         return tile_products(values, places, here_direct, pieces, row_in, col_out, False)
@@ -323,10 +325,12 @@
         return tile_products(values, places, here_flipped, pieces, col_in, row_out, True)
 
     def gather_col(outs):
-        mine, others = outs
-        both = mine + swap(others, "col", 1)
-        parts = [both[i * group : (i + 1) * group] for i in range(len(even) + 1)]
-        return [parts[0]] + [swap(p, "col", m) for p, m in zip(parts[1:], even)]
+        count = len(col_masks)
+        parts = []
+        for mine, others, masks in zip(outs[:count], outs[count:], col_masks):
+            both = mine + swap(others, "col", 1)
+            parts += [both[i * group : (i + 1) * group] for i in range(len(masks))]
+        return [parts[-1]] + [swap(p, "col", m) for p, m in zip(parts, even)]
 
     def gather_row(outs):
         return [outs[0]] + [swap(p, "row", m) for p, m in zip(outs[1:], row_masks)]

time: 185 us -> 168 us (0.908)
  waiting for transfers between devices: 72 us -> 61.2 us
  starting transfers between devices: 72.1 us -> 67.1 us
    ppermute x48 -> x50, waiting for transfers between devices: 68.8 us -> 61.1 us  [swap(): return lax.ppermute(x, axis, [(i, i ^ mask) for i in range(size)])]
    ppermute x48 -> x50, starting transfers between devices: 68.3 us -> 63.3 us  [swap(): return lax.ppermute(x, axis, [(i, i ^ mask) for i in range(size)])]
    ppermute x2, waiting for transfers between devices: 3.18 us -> 0.19 us  [spread_row(): outer = lax.ppermute(two, 'row', [(1, 0), (2, 3)])]
  transfers between devices with their start and end apart: 52 -> 54, of which waited for: 20 -> 17; matrix products, arithmetic and copies ran while one was open for 1% -> 1% of each run, Pallas kernels for 16% -> 18%
where the time goes in v3:
time: 168 us
  starting transfers between devices  67.1 us (40%)
  waiting for transfers between devices  61.2 us (36%)
  Pallas kernels  36 us (21%)
  local copies, waits for them, and re-layouts  2.68 us (2%)
    ppermute x50, starting transfers between devices, swap(): return lax.ppermute(x, axis, [(i, i ^ mask) for i in range(size)])  63.3 us
    ppermute x50, waiting for transfers between devices, swap(): return lax.ppermute(x, axis, [(i, i ^ mask) for i in range(size)])  61.1 us
    pallas_call x4, Pallas kernels, tile_products(): pl.pallas_call(body, name='tile_flipped' if flipped else 'tile_direct', o...  25.3 us
    pallas_call x2, Pallas kernels, factor_inverse(): pl.pallas_call(functools.partial(factor_kernel, n_own=len(own), total_row...  8.71 us
  transfers between devices with their start and end apart: 54, of which 17 were waited for; matrix products, arithmetic and copies ran while one was open for 1% of the time, Pallas kernels for 18%

profile of v3, /device:TPU:1, one launch (start us, length us, event | category | flops | bytes accessed | tf_op | source)
XLA Modules:
  0.0 167.9 jit_solution(13384393769211459942)
XLA Ops:
  1.1 3.2 %collective-permute-start.20 = (f32[512,128]{1,0:T(8,128)S(1)}, f32[512,128]{1,0:T(8,128)S(1)}, u32[]{:S(2)}, u32[]{:S(2)}) collective-permute-start(f32[512,128]{1,0:T(8,128)S(1)} %get-tuple-element.49.rest_0_), channel_id=1, source_target_pairs={{0,16},{8,24},{16,0},{24,8},{1,17},{9,25},{17,1},{25,9},{2,18},{10... | collective-permute-start | bytes 786440 | tf_op jit(solution)/shard_map/ppermute | solution.py:23
  8.7 7.2 %collective-permute-done.20.rest_2_ = f32[512,128]{1,0:T(8,128)S(1)} collective-permute-done((f32[512,128]{1,0:T(8,128)S(1)}, f32[512,128]{1,0:T(8,128)S(1)}, u32[]{:S(2)}, u32[]{:S(2)}) %collective-permute-start.20) | collective-permute-done | bytes 262176 | tf_op jit(solution)/shard_map/ppermute | solution.py:23
  19.3 2.9 %collective-permute-start = (f32[512,128]{1,0:T(8,128)S(1)}, f32[512,128]{1,0:T(8,128)S(1)}, u32[]{:S(2)}, u32[]{:S(2)}) collective-permute-start(f32[512,128]{1,0:T(8,128)S(1)} %get-tuple-element.50.rest_0_), channel_id=1, source_target_pairs={{0,1},{1,0},{2,3},{3,2},{4,5},{5,4},{6,7},{7,6},{8,9},{9,8},{10,11... | collective-permute-start | bytes 786440 | tf_op jit(solution)/shard_map/ppermute | solution.py:23
  22.7 2.9 %collective-permute-start.6 = (f32[512,128]{1,0:T(8,128)S(1)}, f32[512,128]{1,0:T(8,128)S(1)}, u32[]{:S(2)}, u32[]{:S(2)}) collective-permute-start(f32[512,128]{1,0:T(8,128)S(1)} %collective-permute-done.3.rest_4_), channel_id=1, source_target_pairs={{0,1},{1,0},{2,3},{3,2},{4,5},{5,4},{6,7},{7,6},{8,9},{9,8},{10,11... | collective-permute-start | bytes 786440 | tf_op jit(solution)/shard_map/ppermute | solution.py:23
  26.2 6.2 %tile_direct.3 = (f32[1024,128]{1,0:T(8,128)S(1)}, f32[1024,128]{1,0:T(8,128)S(1)}, f32[1024,128]{1,0:T(8,128)S(1)}, f32[1024,128]{1,0:T(8,128)S(1)}) custom-call(s32[2,170]{1,0:T(2,128)S(1)} %bitcast.9, s32[2]{0:T(128)S(1)} %pad_add_fusion.here, f32[170,128,128]{2,1,0:T(8,128)} %bitcast.13, f32[512,128]{1,0:T(8,128)S(1)} %get-tuple-element.49.rest_0_, ...), custom_call_target="tpu_custom_call" | custom-call | flops 2852126720 | bytes 11141120 | tf_op jit(solution)/shard_map/tile_direct/pallas_call | solution.py:115
  32.5 3.6 %collective-permute-start.24 = (f32[1024,128]{1,0:T(8,128)S(1)}, f32[1024,128]{1,0:T(8,128)S(1)}, u32[]{:S(2)}, u32[]{:S(2)}) collective-permute-start(f32[1024,128]{1,0:T(8,128)S(1)} %get-tuple-element.37), channel_id=1, source_target_pairs={{0,1},{1,0},{2,3},{3,2},{4,5},{5,4},{6,7},{7,6},{8,9},{9,8},{10,11... | collective-permute-start | bytes 1572872 | tf_op jit(solution)/shard_map/ppermute | solution.py:23
  36.1 6.5 %tile_flipped.2 = (f32[512,128]{1,0:T(8,128)S(1)}, f32[512,128]{1,0:T(8,128)S(1)}, f32[512,128]{1,0:T(8,128)S(1)}, f32[512,128]{1,0:T(8,128)S(1)}) custom-call(s32[2,170]{1,0:T(2,128)S(1)} %bitcast.10, s32[2]{0:T(128)S(1)} %pad_add_fusion.1.here, f32[170,128,128]{2,1,0:T(8,128)} %bitcast.14, f32[512,128]{1,0:T(8,128)S(1)} %get-tuple-element.50.rest_0_, ...), custom_call_target="tpu_custom_call" | custom-call | flops 2852126720 | bytes 11141120 | tf_op jit(solution)/shard_map/tile_flipped/pallas_call | solution.py:115
  42.6 3.7 %collective-permute-start.7 = (f32[512,128]{1,0:T(8,128)S(1)}, f32[512,128]{1,0:T(8,128)S(1)}, u32[]{:S(2)}, u32[]{:S(2)}) collective-permute-start(f32[512,128]{1,0:T(8,128)S(1)} %get-tuple-element.27), channel_id=1, source_target_pairs={{0,24},{8,16},{16,8},{24,0},{1,25},{9,17},{17,9},{25,1},{2,26},{10... | collective-permute-start | bytes 786440 | tf_op jit(solution)/shard_map/ppermute | solution.py:23
  48.1 4.5 %collective-permute-done.7 = f32[512,128]{1,0:T(8,128)S(1)} collective-permute-done((f32[512,128]{1,0:T(8,128)S(1)}, f32[512,128]{1,0:T(8,128)S(1)}, u32[]{:S(2)}, u32[]{:S(2)}) %collective-permute-start.7) | collective-permute-done | bytes 262176 | tf_op jit(solution)/shard_map/ppermute | solution.py:23
  52.8 14.6 %collective-permute-done.8 = f32[512,128]{1,0:T(8,128)S(1)} collective-permute-done((f32[512,128]{1,0:T(8,128)S(1)}, f32[512,128]{1,0:T(8,128)S(1)}, u32[]{:S(2)}, u32[]{:S(2)}) %collective-permute-start.8) | collective-permute-done | bytes 262176 | tf_op jit(solution)/shard_map/ppermute | solution.py:23
  67.6 2.4 %collective-permute-start.10 = (f32[512,128]{1,0:T(8,128)S(1)}, f32[512,128]{1,0:T(8,128)S(1)}, u32[]{:S(2)}, u32[]{:S(2)}) collective-permute-start(f32[512,128]{1,0:T(8,128)S(1)} %add_add_fusion.rest_0_.rest_1_), channel_id=1, source_target_pairs={{0,8},{8,0},{16,24},{24,16},{1,9},{9,1},{17,25},{25,17},{2,10},{10... | collective-permute-start | bytes 786440 | tf_op jit(solution)/shard_map/ppermute | solution.py:23
  70.7 2.0 %collective-permute-start.38 = (f32[64,128]{1,0:T(8,128)S(1)}, f32[64,128]{1,0:T(8,128)S(1)}, u32[]{:S(2)}, u32[]{:S(2)}) collective-permute-start(f32[64,128]{1,0:T(8,128)S(1)} %get-tuple-element.43), channel_id=1, source_target_pairs={{0,1},{1,0},{2,3},{3,2},{4,5},{5,4},{6,7},{7,6},{8,9},{9,8},{10,11... | collective-permute-start | bytes 98312 | tf_op jit(solution)/shard_map/ppermute | solution.py:23
  73.4 8.7 %collective-permute-done.11.rest_2_ = f32[512,128]{1,0:T(8,128)S(1)} collective-permute-done((f32[512,128]{1,0:T(8,128)S(1)}, f32[512,128]{1,0:T(8,128)S(1)}, u32[]{:S(2)}, u32[]{:S(2)}) %collective-permute-start.11) | collective-permute-done | bytes 262176 | tf_op jit(solution)/shard_map/ppermute | solution.py:23
  84.0 2.2 %collective-permute-start.41 = (f32[64,128]{1,0:T(8,128)S(1)}, f32[64,128]{1,0:T(8,128)S(1)}, u32[]{:S(2)}, u32[]{:S(2)}) collective-permute-start(f32[64,128]{1,0:T(8,128)S(1)} %add.82), channel_id=1, source_target_pairs={{0,6},{1,7},{2,4},{3,5},{4,2},{5,3},{6,0},{7,1},{8,14},{9,15},{10,... | collective-permute-start | bytes 98312 | tf_op jit(solution)/shard_map/ppermute | solution.py:23
  87.6 2.2 %collective-permute-start.31 = (f32[512,128]{1,0:T(8,128)S(1)}, f32[512,128]{1,0:T(8,128)S(1)}, u32[]{:S(2)}, u32[]{:S(2)}) collective-permute-start(f32[512,128]{1,0:T(8,128)S(1)} %fusion.1.rest_0_), channel_id=1, source_target_pairs={{0,6},{1,7},{2,4},{3,5},{4,2},{5,3},{6,0},{7,1},{8,14},{9,15},{10,... | collective-permute-start | bytes 786440 | tf_op jit(solution)/shard_map/ppermute | solution.py:23
  94.5 4.0 %collective-permute-start.28 = (f32[512,128]{1,0:T(8,128)S(1)}, f32[512,128]{1,0:T(8,128)S(1)}, u32[]{:S(2)}, u32[]{:S(2)}) collective-permute-start(f32[512,128]{1,0:T(8,128)S(1)} %fusion.1.rest_0_), channel_id=1, source_target_pairs={{0,1},{1,0},{2,3},{3,2},{4,5},{5,4},{6,7},{7,6},{8,9},{9,8},{10,11... | collective-permute-start | bytes 786440 | tf_op jit(solution)/shard_map/ppermute | solution.py:23
  101.4 6.2 %tile_direct.2 = (f32[1024,128]{1,0:T(8,128)S(1)}, f32[1024,128]{1,0:T(8,128)S(1)}, f32[1024,128]{1,0:T(8,128)S(1)}, f32[1024,128]{1,0:T(8,128)S(1)}) custom-call(s32[2,170]{1,0:T(2,128)S(1)} %bitcast.11, s32[2]{0:T(128)S(1)} %pad_add_fusion.here, f32[170,128,128]{2,1,0:T(8,128)} %bitcast.15, f32[512,128]{1,0:T(8,128)S(1)} %add_add_fusion.rest_0_.rest_1_, ...), custom_call_target="tpu_custom_call" | custom-call | flops 2852126720 | bytes 11141120 | tf_op jit(solution)/shard_map/tile_direct/pallas_call | solution.py:115
  108.6 6.5 %tile_flipped.3 = (f32[512,128]{1,0:T(8,128)S(1)}, f32[512,128]{1,0:T(8,128)S(1)}, f32[512,128]{1,0:T(8,128)S(1)}, f32[512,128]{1,0:T(8,128)S(1)}) custom-call(s32[2,170]{1,0:T(2,128)S(1)} %bitcast.12, s32[2]{0:T(128)S(1)} %pad_add_fusion.1.here, f32[170,128,128]{2,1,0:T(8,128)} %bitcast.16, f32[512,128]{1,0:T(8,128)S(1)} %fusion.1.rest_0_, ...), custom_call_target="tpu_custom_call" | custom-call | flops 2852126720 | bytes 11141120 | tf_op jit(solution)/shard_map/tile_flipped/pallas_call | solution.py:115
  120.8 3.9 %collective-permute-done.35.rest_5_ = f32[512,128]{1,0:T(8,128)S(1)} collective-permute-done((f32[512,128]{1,0:T(8,128)S(1)}, f32[512,128]{1,0:T(8,128)S(1)}, u32[]{:S(2)}, u32[]{:S(2)}) %collective-permute-start.35) | collective-permute-done | bytes 262176 | tf_op jit(solution)/shard_map/ppermute | solution.py:23
  126.2 3.5 %factor.1.rest_8_ = f32[128,128]{1,0:T(8,128)S(1)} custom-call(s32[1]{0:T(128)} %bitcast.here, f32[64,128]{1,0:T(8,128)S(1)} %add_add_fusion.3.rest_0_, f32[64,128]{1,0:T(8,128)S(1)} %collective-permute-done.45.rest_1_), custom_call_target="tpu_custom_call" | custom-call | tf_op jit(solution)/shard_map/factor/pallas_call | solution.py:271
  129.7 12.3 %collective-permute-done.36.rest_6_ = f32[512,128]{1,0:T(8,128)S(1)} collective-permute-done((f32[512,128]{1,0:T(8,128)S(1)}, f32[512,128]{1,0:T(8,128)S(1)}, u32[]{:S(2)}, u32[]{:S(2)}) %collective-permute-start.36) | collective-permute-done | bytes 262176 | tf_op jit(solution)/shard_map/ppermute | solution.py:23
  151.5 3.8 %collective-permute-start.51 = (f32[64,128]{1,0:T(8,128)S(1)}, f32[64,128]{1,0:T(8,128)S(1)}, u32[]{:S(2)}, u32[]{:S(2)}) collective-permute-start(f32[64,128]{1,0:T(8,128)S(1)} %add_add_fusion.2), channel_id=1, source_target_pairs={{0,16},{8,24},{16,0},{24,8},{1,17},{9,25},{17,1},{25,9},{2,18},{10... | collective-permute-start | bytes 98312 | tf_op jit(solution)/shard_map/ppermute | solution.py:23
  158.1 3.7 %collective-permute-start.53 = (f32[64,128]{1,0:T(8,128)S(1)}, f32[64,128]{1,0:T(8,128)S(1)}, u32[]{:S(2)}, u32[]{:S(2)}) collective-permute-start(f32[64,128]{1,0:T(8,128)S(1)} %add_add_fusion.1.rest_0_), channel_id=1, source_target_pairs={{0,1},{1,0},{2,3},{3,2},{4,5},{5,4},{6,7},{7,6},{8,9},{9,8},{10,11... | collective-permute-start | bytes 98312 | tf_op jit(solution)/shard_map/ppermute | solution.py:23
  162.7 5.2 %factor_apply.1 = f32[2,512,128]{2,1,0:T(8,128)} custom-call(s32[1]{0:T(128)} %bitcast.here, f32[64,128]{1,0:T(8,128)S(1)} %add_add_fusion.1.rest_0_, f32[64,128]{1,0:T(8,128)S(1)} %collective-permute-done.53.rest_1_, f32[2,512,128]{2,1,0:T(8,128)S(1)} %get-tuple-element.46.rest_2_), custom_call_target="tpu_custom_call" | custom-call | tf_op jit(solution)/shard_map/factor_apply/pallas_call | solution.py:271
  (115 shorter events, 45.8 us)
Async XLA Ops:
  1.1 14.9 %collective-permute-start.20 = (f32[512,128]{1,0:T(8,128)S(1)}, f32[512,128]{1,0:T(8,128)S(1)}, u32[]{:S(2)}, u32[]{:S(2)}) collective-permute-start(f32[512,128]{1,0:T(8,128)S(1)} %get-tuple-element.49.rest_0_), channel_id=1, source_target_pairs={{0,16},{8,24},{16,0},{24,8},{1,17},{9,25},{17,1},{25,9},{2,18},{10... | collective-permute-start | bytes 786440 | tf_op jit(solution)/shard_map/ppermute | solution.py:23
  4.3 13.6 %collective-permute-start.19 = (f32[512,128]{1,0:T(8,128)S(1)}, f32[512,128]{1,0:T(8,128)S(1)}, u32[]{:S(2)}, u32[]{:S(2)}) collective-permute-start(f32[512,128]{1,0:T(8,128)S(1)} %get-tuple-element.49.rest_0_), channel_id=1, source_target_pairs={{0,8},{8,0},{16,24},{24,16},{1,9},{9,1},{17,25},{25,17},{2,10},{10... | collective-permute-start | bytes 786440 | tf_op jit(solution)/shard_map/ppermute | solution.py:23
  5.6 13.7 %collective-permute-start.21 = (f32[512,128]{1,0:T(8,128)S(1)}, f32[512,128]{1,0:T(8,128)S(1)}, u32[]{:S(2)}, u32[]{:S(2)}) collective-permute-start(f32[512,128]{1,0:T(8,128)S(1)} %get-tuple-element.49.rest_0_), channel_id=1, source_target_pairs={{8,16},{16,8},{9,17},{17,9},{10,18},{18,10},{11,19},{19,11},{12,20... | collective-permute-start | bytes 786440 | tf_op jit(solution)/shard_map/ppermute | solution.py:304
  6.2 15.9 %collective-permute-start.1 = (f32[512,128]{1,0:T(8,128)S(1)}, f32[512,128]{1,0:T(8,128)S(1)}, u32[]{:S(2)}, u32[]{:S(2)}) collective-permute-start(f32[512,128]{1,0:T(8,128)S(1)} %get-tuple-element.50.rest_0_), channel_id=1, source_target_pairs={{0,2},{1,3},{2,0},{3,1},{4,6},{5,7},{6,4},{7,5},{8,10},{9,11},{10,... | collective-permute-start | bytes 786440 | tf_op jit(solution)/shard_map/ppermute | solution.py:23
  7.5 14.8 %collective-permute-start.2 = (f32[512,128]{1,0:T(8,128)S(1)}, f32[512,128]{1,0:T(8,128)S(1)}, u32[]{:S(2)}, u32[]{:S(2)}) collective-permute-start(f32[512,128]{1,0:T(8,128)S(1)} %get-tuple-element.50.rest_0_), channel_id=1, source_target_pairs={{0,4},{1,5},{2,6},{3,7},{4,0},{5,1},{6,2},{7,3},{8,12},{9,13},{10,... | collective-permute-start | bytes 786440 | tf_op jit(solution)/shard_map/ppermute | solution.py:23
  19.3 16.8 %collective-permute-start = (f32[512,128]{1,0:T(8,128)S(1)}, f32[512,128]{1,0:T(8,128)S(1)}, u32[]{:S(2)}, u32[]{:S(2)}) collective-permute-start(f32[512,128]{1,0:T(8,128)S(1)} %get-tuple-element.50.rest_0_), channel_id=1, source_target_pairs={{0,1},{1,0},{2,3},{3,2},{4,5},{5,4},{6,7},{7,6},{8,9},{9,8},{10,11... | collective-permute-start | bytes 786440 | tf_op jit(solution)/shard_map/ppermute | solution.py:23
  22.2 13.9 %collective-permute-start.4 = (f32[512,128]{1,0:T(8,128)S(1)}, f32[512,128]{1,0:T(8,128)S(1)}, u32[]{:S(2)}, u32[]{:S(2)}) collective-permute-start(f32[512,128]{1,0:T(8,128)S(1)} %collective-permute-done.1.rest_2_), channel_id=1, source_target_pairs={{0,1},{1,0},{2,3},{3,2},{4,5},{5,4},{6,7},{7,6},{8,9},{9,8},{10,11... | collective-permute-start | bytes 786440 | tf_op jit(solution)/shard_map/ppermute | solution.py:23
  22.3 13.9 %collective-permute-start.5 = (f32[512,128]{1,0:T(8,128)S(1)}, f32[512,128]{1,0:T(8,128)S(1)}, u32[]{:S(2)}, u32[]{:S(2)}) collective-permute-start(f32[512,128]{1,0:T(8,128)S(1)} %collective-permute-done.2.rest_3_), channel_id=1, source_target_pairs={{0,1},{1,0},{2,3},{3,2},{4,5},{5,4},{6,7},{7,6},{8,9},{9,8},{10,11... | collective-permute-start | bytes 786440 | tf_op jit(solution)/shard_map/ppermute | solution.py:23
  32.5 14.2 %collective-permute-start.24 = (f32[1024,128]{1,0:T(8,128)S(1)}, f32[1024,128]{1,0:T(8,128)S(1)}, u32[]{:S(2)}, u32[]{:S(2)}) collective-permute-start(f32[1024,128]{1,0:T(8,128)S(1)} %get-tuple-element.37), channel_id=1, source_target_pairs={{0,1},{1,0},{2,3},{3,2},{4,5},{5,4},{6,7},{7,6},{8,9},{9,8},{10,11... | collective-permute-start | bytes 1572872 | tf_op jit(solution)/shard_map/ppermute | solution.py:23
  46.3 21.1 %collective-permute-start.8 = (f32[512,128]{1,0:T(8,128)S(1)}, f32[512,128]{1,0:T(8,128)S(1)}, u32[]{:S(2)}, u32[]{:S(2)}) collective-permute-start(f32[512,128]{1,0:T(8,128)S(1)} %get-tuple-element.28), channel_id=1, source_target_pairs={{0,16},{8,24},{16,0},{24,8},{1,17},{9,25},{17,1},{25,9},{2,18},{10... | collective-permute-start | bytes 786440 | tf_op jit(solution)/shard_map/ppermute | solution.py:23
  46.3 21.1 %collective-permute-start.9 = (f32[512,128]{1,0:T(8,128)S(1)}, f32[512,128]{1,0:T(8,128)S(1)}, u32[]{:S(2)}, u32[]{:S(2)}) collective-permute-start(f32[512,128]{1,0:T(8,128)S(1)} %get-tuple-element.29), channel_id=1, source_target_pairs={{0,8},{8,0},{16,24},{24,16},{1,9},{9,1},{17,25},{25,17},{2,10},{10... | collective-permute-start | bytes 786440 | tf_op jit(solution)/shard_map/ppermute | solution.py:23
  47.6 22.4 %collective-permute-start.25 = (f32[512,128]{1,0:T(8,128)}, f32[512,128]{1,0:T(8,128)S(1)}, u32[]{:S(2)}, u32[]{:S(2)}) collective-permute-start(f32[512,128]{1,0:T(8,128)} %get-tuple-element.47), channel_id=1, source_target_pairs={{0,2},{1,3},{2,0},{3,1},{4,6},{5,7},{6,4},{7,5},{8,10},{9,11},{10,... | collective-permute-start | bytes 786440 | tf_op jit(solution)/shard_map/ppermute | solution.py:23
  47.8 22.1 %collective-permute-start.26 = (f32[512,128]{1,0:T(8,128)}, f32[512,128]{1,0:T(8,128)S(1)}, u32[]{:S(2)}, u32[]{:S(2)}) collective-permute-start(f32[512,128]{1,0:T(8,128)} %get-tuple-element.48), channel_id=1, source_target_pairs={{0,4},{1,5},{2,6},{3,7},{4,0},{5,1},{6,2},{7,3},{8,12},{9,13},{10,... | collective-permute-start | bytes 786440 | tf_op jit(solution)/shard_map/ppermute | solution.py:23
  52.6 17.4 %collective-permute-start.27 = (f32[512,128]{1,0:T(8,128)S(1)}, f32[512,128]{1,0:T(8,128)S(1)}, u32[]{:S(2)}, u32[]{:S(2)}) collective-permute-start(f32[512,128]{1,0:T(8,128)S(1)} %slice.47), channel_id=1, source_target_pairs={{0,6},{1,7},{2,4},{3,5},{4,2},{5,3},{6,0},{7,1},{8,14},{9,15},{10,... | collective-permute-start | bytes 786440 | tf_op jit(solution)/shard_map/ppermute | solution.py:23
  67.5 14.6 %collective-permute-start.11 = (f32[512,128]{1,0:T(8,128)S(1)}, f32[512,128]{1,0:T(8,128)S(1)}, u32[]{:S(2)}, u32[]{:S(2)}) collective-permute-start(f32[512,128]{1,0:T(8,128)S(1)} %add_add_fusion.rest_0_.rest_1_), channel_id=1, source_target_pairs={{0,16},{8,24},{16,0},{24,8},{1,17},{9,25},{17,1},{25,9},{2,18},{10... | collective-permute-start | bytes 786440 | tf_op jit(solution)/shard_map/ppermute | solution.py:23
  67.6 16.3 %collective-permute-start.10 = (f32[512,128]{1,0:T(8,128)S(1)}, f32[512,128]{1,0:T(8,128)S(1)}, u32[]{:S(2)}, u32[]{:S(2)}) collective-permute-start(f32[512,128]{1,0:T(8,128)S(1)} %add_add_fusion.rest_0_.rest_1_), channel_id=1, source_target_pairs={{0,8},{8,0},{16,24},{24,16},{1,9},{9,1},{17,25},{25,17},{2,10},{10... | collective-permute-start | bytes 786440 | tf_op jit(solution)/shard_map/ppermute | solution.py:23
  72.7 17.1 %collective-permute-start.12 = (f32[512,128]{1,0:T(8,128)S(1)}, f32[512,128]{1,0:T(8,128)S(1)}, u32[]{:S(2)}, u32[]{:S(2)}) collective-permute-start(f32[512,128]{1,0:T(8,128)S(1)} %add_add_fusion.rest_0_.rest_1_), channel_id=1, source_target_pairs={{8,16},{16,8},{9,17},{17,9},{10,18},{18,10},{11,19},{19,11},{12,20... | collective-permute-start | bytes 786440 | tf_op jit(solution)/shard_map/ppermute | solution.py:304
  86.5 14.4 %collective-permute-start.30 = (f32[512,128]{1,0:T(8,128)S(1)}, f32[512,128]{1,0:T(8,128)S(1)}, u32[]{:S(2)}, u32[]{:S(2)}) collective-permute-start(f32[512,128]{1,0:T(8,128)S(1)} %fusion.1.rest_0_), channel_id=1, source_target_pairs={{0,4},{1,5},{2,6},{3,7},{4,0},{5,1},{6,2},{7,3},{8,12},{9,13},{10,... | collective-permute-start | bytes 786440 | tf_op jit(solution)/shard_map/ppermute | solution.py:23
  87.6 13.5 %collective-permute-start.31 = (f32[512,128]{1,0:T(8,128)S(1)}, f32[512,128]{1,0:T(8,128)S(1)}, u32[]{:S(2)}, u32[]{:S(2)}) collective-permute-start(f32[512,128]{1,0:T(8,128)S(1)} %fusion.1.rest_0_), channel_id=1, source_target_pairs={{0,6},{1,7},{2,4},{3,5},{4,2},{5,3},{6,0},{7,1},{8,14},{9,15},{10,... | collective-permute-start | bytes 786440 | tf_op jit(solution)/shard_map/ppermute | solution.py:23
  117.0 25.1 %collective-permute-start.36 = (f32[512,128]{1,0:T(8,128)S(1)}, f32[512,128]{1,0:T(8,128)S(1)}, u32[]{:S(2)}, u32[]{:S(2)}) collective-permute-start(f32[512,128]{1,0:T(8,128)S(1)} %get-tuple-element.40), channel_id=1, source_target_pairs={{0,16},{8,24},{16,0},{24,8},{1,17},{9,25},{17,1},{25,9},{2,18},{10... | collective-permute-start | bytes 786440 | tf_op jit(solution)/shard_map/ppermute | solution.py:23
  118.4 23.6 %collective-permute-start.37 = (f32[512,128]{1,0:T(8,128)S(1)}, f32[512,128]{1,0:T(8,128)S(1)}, u32[]{:S(2)}, u32[]{:S(2)}) collective-permute-start(f32[512,128]{1,0:T(8,128)S(1)} %get-tuple-element.41), channel_id=1, source_target_pairs={{0,8},{8,0},{16,24},{24,16},{1,9},{9,1},{17,25},{25,17},{2,10},{10... | collective-permute-start | bytes 786440 | tf_op jit(solution)/shard_map/ppermute | solution.py:23
  118.8 23.3 %collective-permute-start.16 = (f32[512,128]{1,0:T(8,128)S(1)}, f32[512,128]{1,0:T(8,128)S(1)}, u32[]{:S(2)}, u32[]{:S(2)}) collective-permute-start(f32[512,128]{1,0:T(8,128)S(1)} %get-tuple-element.54), channel_id=1, source_target_pairs={{0,2},{1,3},{2,0},{3,1},{4,6},{5,7},{6,4},{7,5},{8,10},{9,11},{10,... | collective-permute-start | bytes 786440 | tf_op jit(solution)/shard_map/ppermute | solution.py:23
  120.3 21.7 %collective-permute-start.17 = (f32[512,128]{1,0:T(8,128)S(1)}, f32[512,128]{1,0:T(8,128)S(1)}, u32[]{:S(2)}, u32[]{:S(2)}) collective-permute-start(f32[512,128]{1,0:T(8,128)S(1)} %get-tuple-element.53), channel_id=1, source_target_pairs={{0,4},{1,5},{2,6},{3,7},{4,0},{5,1},{6,2},{7,3},{8,12},{9,13},{10,... | collective-permute-start | bytes 786440 | tf_op jit(solution)/shard_map/ppermute | solution.py:23
  124.7 17.4 %collective-permute-start.18 = (f32[512,128]{1,0:T(8,128)S(1)}, f32[512,128]{1,0:T(8,128)S(1)}, u32[]{:S(2)}, u32[]{:S(2)}) collective-permute-start(f32[512,128]{1,0:T(8,128)S(1)} %get-tuple-element.51), channel_id=1, source_target_pairs={{0,6},{1,7},{2,4},{3,5},{4,2},{5,3},{6,0},{7,1},{8,14},{9,15},{10,... | collective-permute-start | bytes 786440 | tf_op jit(solution)/shard_map/ppermute | solution.py:23
  (32 other events, 294.1 us)

commit v4 on v3

--- a/solution.py
+++ b/solution.py
@@ -293,7 +293,7 @@
     here_direct = jnp.stack([row_id, col_id]).astype(jnp.int32)
     here_flipped = jnp.stack([col_id, row_id]).astype(jnp.int32)
     parity = (col_id & 1).astype(jnp.int32).reshape(1)
-    even = list(range(2, n_col, 2))
+    even = list(range(2, n_col, 2))[::-1]
     row_masks = list(range(1, n_row))[::-1]
 
     def spread_row(x):
@@ -333,7 +333,10 @@
         return [parts[-1]] + [swap(p, "col", m) for p, m in zip(parts, even)]
 
     def gather_row(outs):
-        return [outs[0]] + [swap(p, "row", m) for p, m in zip(outs[1:], row_masks)]
+        got = []
+        for p, m in zip(outs[1:], row_masks):
+            got.append(swap(p, "row", m))
+        return [outs[0]] + got
 
     def reduce_gram(mine, other):
         own = mine + swap(other, "col", 1)

time: 168 us -> 167 us (level)
  starting transfers between devices: 67.1 us -> 64.6 us
    ppermute x50, starting transfers between devices: 63.3 us -> 60.7 us  [swap(): return lax.ppermute(x, axis, [(i, i ^ mask) for i in range(size)])]
  transfers between devices with their start and end apart: 54 -> 54, of which waited for: 17 -> 18; matrix products, arithmetic and copies ran while one was open for 1% -> 1% of each run, Pallas kernels for 18% -> 18%
where the time goes in v4:
time: 167 us; the launch traced here: 166 us
  starting transfers between devices  64.6 us (39%)
  waiting for transfers between devices  62.2 us (37%)
  Pallas kernels  36 us (22%)
  local copies, waits for them, and re-layouts  2.68 us (2%)
    ppermute x50, waiting for transfers between devices, swap(): return lax.ppermute(x, axis, [(i, i ^ mask) for i in range(size)])  62 us
    ppermute x50, starting transfers between devices, swap(): return lax.ppermute(x, axis, [(i, i ^ mask) for i in range(size)])  60.7 us
    pallas_call x4, Pallas kernels, tile_products(): pl.pallas_call(body, name='tile_flipped' if flipped else 'tile_direct', o...  25.3 us
    pallas_call x2, Pallas kernels, factor_inverse(): pl.pallas_call(functools.partial(factor_kernel, n_own=len(own), total_row...  8.72 us
  transfers between devices with their start and end apart: 54, of which 18 were waited for; matrix products, arithmetic and copies ran while one was open for 1% of the time, Pallas kernels for 18%

profile of v4, /device:TPU:1, one launch (start us, length us, event | category | flops | bytes accessed | tf_op | source)
XLA Modules:
  0.0 166.3 jit_solution(3571947741371285660)
XLA Ops:
  1.1 3.2 %collective-permute-start.20 = (f32[512,128]{1,0:T(8,128)S(1)}, f32[512,128]{1,0:T(8,128)S(1)}, u32[]{:S(2)}, u32[]{:S(2)}) collective-permute-start(f32[512,128]{1,0:T(8,128)S(1)} %get-tuple-element.49.rest_0_), channel_id=1, source_target_pairs={{0,16},{8,24},{16,0},{24,8},{1,17},{9,25},{17,1},{25,9},{2,18},{10... | collective-permute-start | bytes 786440 | tf_op jit(solution)/shard_map/ppermute | solution.py:23
  6.2 2.2 %collective-permute-start.1 = (f32[512,128]{1,0:T(8,128)S(1)}, f32[512,128]{1,0:T(8,128)S(1)}, u32[]{:S(2)}, u32[]{:S(2)}) collective-permute-start(f32[512,128]{1,0:T(8,128)S(1)} %get-tuple-element.50.rest_0_), channel_id=1, source_target_pairs={{0,6},{1,7},{2,4},{3,5},{4,2},{5,3},{6,0},{7,1},{8,14},{9,15},{10,... | collective-permute-start | bytes 786440 | tf_op jit(solution)/shard_map/ppermute | solution.py:23
  8.7 7.2 %collective-permute-done.20.rest_2_ = f32[512,128]{1,0:T(8,128)S(1)} collective-permute-done((f32[512,128]{1,0:T(8,128)S(1)}, f32[512,128]{1,0:T(8,128)S(1)}, u32[]{:S(2)}, u32[]{:S(2)}) %collective-permute-start.20) | collective-permute-done | bytes 262176 | tf_op jit(solution)/shard_map/ppermute | solution.py:23
  18.3 2.9 %collective-permute-start = (f32[512,128]{1,0:T(8,128)S(1)}, f32[512,128]{1,0:T(8,128)S(1)}, u32[]{:S(2)}, u32[]{:S(2)}) collective-permute-start(f32[512,128]{1,0:T(8,128)S(1)} %get-tuple-element.50.rest_0_), channel_id=1, source_target_pairs={{0,1},{1,0},{2,3},{3,2},{4,5},{5,4},{6,7},{7,6},{8,9},{9,8},{10,11... | collective-permute-start | bytes 786440 | tf_op jit(solution)/shard_map/ppermute | solution.py:23
  21.7 2.9 %collective-permute-start.6 = (f32[512,128]{1,0:T(8,128)S(1)}, f32[512,128]{1,0:T(8,128)S(1)}, u32[]{:S(2)}, u32[]{:S(2)}) collective-permute-start(f32[512,128]{1,0:T(8,128)S(1)} %collective-permute-done.3.rest_4_), channel_id=1, source_target_pairs={{0,1},{1,0},{2,3},{3,2},{4,5},{5,4},{6,7},{7,6},{8,9},{9,8},{10,11... | collective-permute-start | bytes 786440 | tf_op jit(solution)/shard_map/ppermute | solution.py:23
  25.3 6.2 %tile_direct.3 = (f32[1024,128]{1,0:T(8,128)S(1)}, f32[1024,128]{1,0:T(8,128)S(1)}, f32[1024,128]{1,0:T(8,128)S(1)}, f32[1024,128]{1,0:T(8,128)S(1)}) custom-call(s32[2,170]{1,0:T(2,128)S(1)} %bitcast.9, s32[2]{0:T(128)S(1)} %pad_add_fusion.here, f32[170,128,128]{2,1,0:T(8,128)} %bitcast.13, f32[512,128]{1,0:T(8,128)S(1)} %get-tuple-element.49.rest_0_, ...), custom_call_target="tpu_custom_call" | custom-call | flops 2852126720 | bytes 11141120 | tf_op jit(solution)/shard_map/tile_direct/pallas_call | solution.py:115
  31.6 3.5 %collective-permute-start.24 = (f32[1024,128]{1,0:T(8,128)S(1)}, f32[1024,128]{1,0:T(8,128)S(1)}, u32[]{:S(2)}, u32[]{:S(2)}) collective-permute-start(f32[1024,128]{1,0:T(8,128)S(1)} %get-tuple-element.37), channel_id=1, source_target_pairs={{0,1},{1,0},{2,3},{3,2},{4,5},{5,4},{6,7},{7,6},{8,9},{9,8},{10,11... | collective-permute-start | bytes 1572872 | tf_op jit(solution)/shard_map/ppermute | solution.py:23
  35.2 6.5 %tile_flipped.2 = (f32[512,128]{1,0:T(8,128)S(1)}, f32[512,128]{1,0:T(8,128)S(1)}, f32[512,128]{1,0:T(8,128)S(1)}, f32[512,128]{1,0:T(8,128)S(1)}) custom-call(s32[2,170]{1,0:T(2,128)S(1)} %bitcast.10, s32[2]{0:T(128)S(1)} %pad_add_fusion.1.here, f32[170,128,128]{2,1,0:T(8,128)} %bitcast.14, f32[512,128]{1,0:T(8,128)S(1)} %get-tuple-element.50.rest_0_, ...), custom_call_target="tpu_custom_call" | custom-call | flops 2852126720 | bytes 11141120 | tf_op jit(solution)/shard_map/tile_flipped/pallas_call | solution.py:115
  41.7 3.7 %collective-permute-start.7 = (f32[512,128]{1,0:T(8,128)S(1)}, f32[512,128]{1,0:T(8,128)S(1)}, u32[]{:S(2)}, u32[]{:S(2)}) collective-permute-start(f32[512,128]{1,0:T(8,128)S(1)} %get-tuple-element.27), channel_id=1, source_target_pairs={{0,24},{8,16},{16,8},{24,0},{1,25},{9,17},{17,9},{25,1},{2,26},{10... | collective-permute-start | bytes 786440 | tf_op jit(solution)/shard_map/ppermute | solution.py:23
  48.1 3.5 %collective-permute-done.7 = f32[512,128]{1,0:T(8,128)S(1)} collective-permute-done((f32[512,128]{1,0:T(8,128)S(1)}, f32[512,128]{1,0:T(8,128)S(1)}, u32[]{:S(2)}, u32[]{:S(2)}) %collective-permute-start.7) | collective-permute-done | bytes 262176 | tf_op jit(solution)/shard_map/ppermute | solution.py:23
  51.9 14.6 %collective-permute-done.8 = f32[512,128]{1,0:T(8,128)S(1)} collective-permute-done((f32[512,128]{1,0:T(8,128)S(1)}, f32[512,128]{1,0:T(8,128)S(1)}, u32[]{:S(2)}, u32[]{:S(2)}) %collective-permute-start.8) | collective-permute-done | bytes 262176 | tf_op jit(solution)/shard_map/ppermute | solution.py:23
  66.6 2.3 %collective-permute-start.10 = (f32[512,128]{1,0:T(8,128)S(1)}, f32[512,128]{1,0:T(8,128)S(1)}, u32[]{:S(2)}, u32[]{:S(2)}) collective-permute-start(f32[512,128]{1,0:T(8,128)S(1)} %add_add_fusion.rest_0_.rest_1_), channel_id=1, source_target_pairs={{0,8},{8,0},{16,24},{24,16},{1,9},{9,1},{17,25},{25,17},{2,10},{10... | collective-permute-start | bytes 786440 | tf_op jit(solution)/shard_map/ppermute | solution.py:23
  69.8 2.0 %collective-permute-start.38 = (f32[64,128]{1,0:T(8,128)S(1)}, f32[64,128]{1,0:T(8,128)S(1)}, u32[]{:S(2)}, u32[]{:S(2)}) collective-permute-start(f32[64,128]{1,0:T(8,128)S(1)} %get-tuple-element.43), channel_id=1, source_target_pairs={{0,1},{1,0},{2,3},{3,2},{4,5},{5,4},{6,7},{7,6},{8,9},{9,8},{10,11... | collective-permute-start | bytes 98312 | tf_op jit(solution)/shard_map/ppermute | solution.py:23
  72.4 8.7 %collective-permute-done.11.rest_2_ = f32[512,128]{1,0:T(8,128)S(1)} collective-permute-done((f32[512,128]{1,0:T(8,128)S(1)}, f32[512,128]{1,0:T(8,128)S(1)}, u32[]{:S(2)}, u32[]{:S(2)}) %collective-permute-start.11) | collective-permute-done | bytes 262176 | tf_op jit(solution)/shard_map/ppermute | solution.py:23
  93.5 3.7 %collective-permute-start.28 = (f32[512,128]{1,0:T(8,128)S(1)}, f32[512,128]{1,0:T(8,128)S(1)}, u32[]{:S(2)}, u32[]{:S(2)}) collective-permute-start(f32[512,128]{1,0:T(8,128)S(1)} %fusion.1.rest_0_), channel_id=1, source_target_pairs={{0,1},{1,0},{2,3},{3,2},{4,5},{5,4},{6,7},{7,6},{8,9},{9,8},{10,11... | collective-permute-start | bytes 786440 | tf_op jit(solution)/shard_map/ppermute | solution.py:23
  101.5 6.2 %tile_direct.2 = (f32[1024,128]{1,0:T(8,128)S(1)}, f32[1024,128]{1,0:T(8,128)S(1)}, f32[1024,128]{1,0:T(8,128)S(1)}, f32[1024,128]{1,0:T(8,128)S(1)}) custom-call(s32[2,170]{1,0:T(2,128)S(1)} %bitcast.11, s32[2]{0:T(128)S(1)} %pad_add_fusion.here, f32[170,128,128]{2,1,0:T(8,128)} %bitcast.15, f32[512,128]{1,0:T(8,128)S(1)} %add_add_fusion.rest_0_.rest_1_, ...), custom_call_target="tpu_custom_call" | custom-call | flops 2852126720 | bytes 11141120 | tf_op jit(solution)/shard_map/tile_direct/pallas_call | solution.py:115
  108.8 6.5 %tile_flipped.3 = (f32[512,128]{1,0:T(8,128)S(1)}, f32[512,128]{1,0:T(8,128)S(1)}, f32[512,128]{1,0:T(8,128)S(1)}, f32[512,128]{1,0:T(8,128)S(1)}) custom-call(s32[2,170]{1,0:T(2,128)S(1)} %bitcast.12, s32[2]{0:T(128)S(1)} %pad_add_fusion.1.here, f32[170,128,128]{2,1,0:T(8,128)} %bitcast.16, f32[512,128]{1,0:T(8,128)S(1)} %fusion.1.rest_0_, ...), custom_call_target="tpu_custom_call" | custom-call | flops 2852126720 | bytes 11141120 | tf_op jit(solution)/shard_map/tile_flipped/pallas_call | solution.py:115
  116.5 2.2 %collective-permute-start.36 = (f32[512,128]{1,0:T(8,128)S(1)}, f32[512,128]{1,0:T(8,128)S(1)}, u32[]{:S(2)}, u32[]{:S(2)}) collective-permute-start(f32[512,128]{1,0:T(8,128)S(1)} %get-tuple-element.40), channel_id=1, source_target_pairs={{0,16},{8,24},{16,0},{24,8},{1,17},{9,25},{17,1},{25,9},{2,18},{10... | collective-permute-start | bytes 786440 | tf_op jit(solution)/shard_map/ppermute | solution.py:23
  121.1 3.9 %collective-permute-done.35.rest_5_ = f32[512,128]{1,0:T(8,128)S(1)} collective-permute-done((f32[512,128]{1,0:T(8,128)S(1)}, f32[512,128]{1,0:T(8,128)S(1)}, u32[]{:S(2)}, u32[]{:S(2)}) %collective-permute-start.35) | collective-permute-done | bytes 262176 | tf_op jit(solution)/shard_map/ppermute | solution.py:23
  125.6 3.5 %factor.1.rest_8_ = f32[128,128]{1,0:T(8,128)S(1)} custom-call(s32[1]{0:T(128)} %bitcast.here, f32[64,128]{1,0:T(8,128)S(1)} %add_add_fusion.3.rest_0_, f32[64,128]{1,0:T(8,128)S(1)} %collective-permute-done.45.rest_1_), custom_call_target="tpu_custom_call" | custom-call | tf_op jit(solution)/shard_map/factor/pallas_call | solution.py:271
  129.1 13.2 %collective-permute-done.36.rest_6_ = f32[512,128]{1,0:T(8,128)S(1)} collective-permute-done((f32[512,128]{1,0:T(8,128)S(1)}, f32[512,128]{1,0:T(8,128)S(1)}, u32[]{:S(2)}, u32[]{:S(2)}) %collective-permute-start.36) | collective-permute-done | bytes 262176 | tf_op jit(solution)/shard_map/ppermute | solution.py:23
  151.0 2.9 %collective-permute-start.51 = (f32[64,128]{1,0:T(8,128)S(1)}, f32[64,128]{1,0:T(8,128)S(1)}, u32[]{:S(2)}, u32[]{:S(2)}) collective-permute-start(f32[64,128]{1,0:T(8,128)S(1)} %add_add_fusion.2), channel_id=1, source_target_pairs={{0,16},{8,24},{16,0},{24,8},{1,17},{9,25},{17,1},{25,9},{2,18},{10... | collective-permute-start | bytes 98312 | tf_op jit(solution)/shard_map/ppermute | solution.py:23
  157.3 2.9 %collective-permute-start.53 = (f32[64,128]{1,0:T(8,128)S(1)}, f32[64,128]{1,0:T(8,128)S(1)}, u32[]{:S(2)}, u32[]{:S(2)}) collective-permute-start(f32[64,128]{1,0:T(8,128)S(1)} %add_add_fusion.1.rest_0_), channel_id=1, source_target_pairs={{0,1},{1,0},{2,3},{3,2},{4,5},{5,4},{6,7},{7,6},{8,9},{9,8},{10,11... | collective-permute-start | bytes 98312 | tf_op jit(solution)/shard_map/ppermute | solution.py:23
  161.1 5.2 %factor_apply.1 = f32[2,512,128]{2,1,0:T(8,128)} custom-call(s32[1]{0:T(128)} %bitcast.here, f32[64,128]{1,0:T(8,128)S(1)} %add_add_fusion.1.rest_0_, f32[64,128]{1,0:T(8,128)S(1)} %collective-permute-done.53.rest_1_, f32[2,512,128]{2,1,0:T(8,128)S(1)} %get-tuple-element.46.rest_2_), custom_call_target="tpu_custom_call" | custom-call | tf_op jit(solution)/shard_map/factor_apply/pallas_call | solution.py:271
  (115 shorter events, 46.4 us)
Async XLA Ops:
  1.1 14.9 %collective-permute-start.20 = (f32[512,128]{1,0:T(8,128)S(1)}, f32[512,128]{1,0:T(8,128)S(1)}, u32[]{:S(2)}, u32[]{:S(2)}) collective-permute-start(f32[512,128]{1,0:T(8,128)S(1)} %get-tuple-element.49.rest_0_), channel_id=1, source_target_pairs={{0,16},{8,24},{16,0},{24,8},{1,17},{9,25},{17,1},{25,9},{2,18},{10... | collective-permute-start | bytes 786440 | tf_op jit(solution)/shard_map/ppermute | solution.py:23
  6.2 15.0 %collective-permute-start.1 = (f32[512,128]{1,0:T(8,128)S(1)}, f32[512,128]{1,0:T(8,128)S(1)}, u32[]{:S(2)}, u32[]{:S(2)}) collective-permute-start(f32[512,128]{1,0:T(8,128)S(1)} %get-tuple-element.50.rest_0_), channel_id=1, source_target_pairs={{0,6},{1,7},{2,4},{3,5},{4,2},{5,3},{6,0},{7,1},{8,14},{9,15},{10,... | collective-permute-start | bytes 786440 | tf_op jit(solution)/shard_map/ppermute | solution.py:23
  8.5 12.9 %collective-permute-start.2 = (f32[512,128]{1,0:T(8,128)S(1)}, f32[512,128]{1,0:T(8,128)S(1)}, u32[]{:S(2)}, u32[]{:S(2)}) collective-permute-start(f32[512,128]{1,0:T(8,128)S(1)} %get-tuple-element.50.rest_0_), channel_id=1, source_target_pairs={{0,4},{1,5},{2,6},{3,7},{4,0},{5,1},{6,2},{7,3},{8,12},{9,13},{10,... | collective-permute-start | bytes 786440 | tf_op jit(solution)/shard_map/ppermute | solution.py:23
  18.3 16.8 %collective-permute-start = (f32[512,128]{1,0:T(8,128)S(1)}, f32[512,128]{1,0:T(8,128)S(1)}, u32[]{:S(2)}, u32[]{:S(2)}) collective-permute-start(f32[512,128]{1,0:T(8,128)S(1)} %get-tuple-element.50.rest_0_), channel_id=1, source_target_pairs={{0,1},{1,0},{2,3},{3,2},{4,5},{5,4},{6,7},{7,6},{8,9},{9,8},{10,11... | collective-permute-start | bytes 786440 | tf_op jit(solution)/shard_map/ppermute | solution.py:23
  21.2 13.9 %collective-permute-start.4 = (f32[512,128]{1,0:T(8,128)S(1)}, f32[512,128]{1,0:T(8,128)S(1)}, u32[]{:S(2)}, u32[]{:S(2)}) collective-permute-start(f32[512,128]{1,0:T(8,128)S(1)} %collective-permute-done.1.rest_2_), channel_id=1, source_target_pairs={{0,1},{1,0},{2,3},{3,2},{4,5},{5,4},{6,7},{7,6},{8,9},{9,8},{10,11... | collective-permute-start | bytes 786440 | tf_op jit(solution)/shard_map/ppermute | solution.py:23
  21.3 13.9 %collective-permute-start.5 = (f32[512,128]{1,0:T(8,128)S(1)}, f32[512,128]{1,0:T(8,128)S(1)}, u32[]{:S(2)}, u32[]{:S(2)}) collective-permute-start(f32[512,128]{1,0:T(8,128)S(1)} %collective-permute-done.2.rest_3_), channel_id=1, source_target_pairs={{0,1},{1,0},{2,3},{3,2},{4,5},{5,4},{6,7},{7,6},{8,9},{9,8},{10,11... | collective-permute-start | bytes 786440 | tf_op jit(solution)/shard_map/ppermute | solution.py:23
  21.7 13.4 %collective-permute-start.6 = (f32[512,128]{1,0:T(8,128)S(1)}, f32[512,128]{1,0:T(8,128)S(1)}, u32[]{:S(2)}, u32[]{:S(2)}) collective-permute-start(f32[512,128]{1,0:T(8,128)S(1)} %collective-permute-done.3.rest_4_), channel_id=1, source_target_pairs={{0,1},{1,0},{2,3},{3,2},{4,5},{5,4},{6,7},{7,6},{8,9},{9,8},{10,11... | collective-permute-start | bytes 786440 | tf_op jit(solution)/shard_map/ppermute | solution.py:23
  31.6 14.2 %collective-permute-start.24 = (f32[1024,128]{1,0:T(8,128)S(1)}, f32[1024,128]{1,0:T(8,128)S(1)}, u32[]{:S(2)}, u32[]{:S(2)}) collective-permute-start(f32[1024,128]{1,0:T(8,128)S(1)} %get-tuple-element.37), channel_id=1, source_target_pairs={{0,1},{1,0},{2,3},{3,2},{4,5},{5,4},{6,7},{7,6},{8,9},{9,8},{10,11... | collective-permute-start | bytes 1572872 | tf_op jit(solution)/shard_map/ppermute | solution.py:23
  45.3 21.1 %collective-permute-start.8 = (f32[512,128]{1,0:T(8,128)S(1)}, f32[512,128]{1,0:T(8,128)S(1)}, u32[]{:S(2)}, u32[]{:S(2)}) collective-permute-start(f32[512,128]{1,0:T(8,128)S(1)} %get-tuple-element.28), channel_id=1, source_target_pairs={{0,16},{8,24},{16,0},{24,8},{1,17},{9,25},{17,1},{25,9},{2,18},{10... | collective-permute-start | bytes 786440 | tf_op jit(solution)/shard_map/ppermute | solution.py:23
  45.3 21.1 %collective-permute-start.9 = (f32[512,128]{1,0:T(8,128)S(1)}, f32[512,128]{1,0:T(8,128)S(1)}, u32[]{:S(2)}, u32[]{:S(2)}) collective-permute-start(f32[512,128]{1,0:T(8,128)S(1)} %get-tuple-element.29), channel_id=1, source_target_pairs={{0,8},{8,0},{16,24},{24,16},{1,9},{9,1},{17,25},{25,17},{2,10},{10... | collective-permute-start | bytes 786440 | tf_op jit(solution)/shard_map/ppermute | solution.py:23
  46.6 22.4 %collective-permute-start.25 = (f32[512,128]{1,0:T(8,128)}, f32[512,128]{1,0:T(8,128)S(1)}, u32[]{:S(2)}, u32[]{:S(2)}) collective-permute-start(f32[512,128]{1,0:T(8,128)} %get-tuple-element.47), channel_id=1, source_target_pairs={{0,6},{1,7},{2,4},{3,5},{4,2},{5,3},{6,0},{7,1},{8,14},{9,15},{10,... | collective-permute-start | bytes 786440 | tf_op jit(solution)/shard_map/ppermute | solution.py:23
  47.8 21.2 %collective-permute-start.26 = (f32[512,128]{1,0:T(8,128)}, f32[512,128]{1,0:T(8,128)S(1)}, u32[]{:S(2)}, u32[]{:S(2)}) collective-permute-start(f32[512,128]{1,0:T(8,128)} %get-tuple-element.48), channel_id=1, source_target_pairs={{0,4},{1,5},{2,6},{3,7},{4,0},{5,1},{6,2},{7,3},{8,12},{9,13},{10,... | collective-permute-start | bytes 786440 | tf_op jit(solution)/shard_map/ppermute | solution.py:23
  51.6 17.4 %collective-permute-start.27 = (f32[512,128]{1,0:T(8,128)S(1)}, f32[512,128]{1,0:T(8,128)S(1)}, u32[]{:S(2)}, u32[]{:S(2)}) collective-permute-start(f32[512,128]{1,0:T(8,128)S(1)} %slice.47), channel_id=1, source_target_pairs={{0,2},{1,3},{2,0},{3,1},{4,6},{5,7},{6,4},{7,5},{8,10},{9,11},{10,... | collective-permute-start | bytes 786440 | tf_op jit(solution)/shard_map/ppermute | solution.py:23
  66.6 14.6 %collective-permute-start.11 = (f32[512,128]{1,0:T(8,128)S(1)}, f32[512,128]{1,0:T(8,128)S(1)}, u32[]{:S(2)}, u32[]{:S(2)}) collective-permute-start(f32[512,128]{1,0:T(8,128)S(1)} %add_add_fusion.rest_0_.rest_1_), channel_id=1, source_target_pairs={{0,16},{8,24},{16,0},{24,8},{1,17},{9,25},{17,1},{25,9},{2,18},{10... | collective-permute-start | bytes 786440 | tf_op jit(solution)/shard_map/ppermute | solution.py:23
  66.6 17.3 %collective-permute-start.10 = (f32[512,128]{1,0:T(8,128)S(1)}, f32[512,128]{1,0:T(8,128)S(1)}, u32[]{:S(2)}, u32[]{:S(2)}) collective-permute-start(f32[512,128]{1,0:T(8,128)S(1)} %add_add_fusion.rest_0_.rest_1_), channel_id=1, source_target_pairs={{0,8},{8,0},{16,24},{24,16},{1,9},{9,1},{17,25},{25,17},{2,10},{10... | collective-permute-start | bytes 786440 | tf_op jit(solution)/shard_map/ppermute | solution.py:23
  71.7 17.1 %collective-permute-start.12 = (f32[512,128]{1,0:T(8,128)S(1)}, f32[512,128]{1,0:T(8,128)S(1)}, u32[]{:S(2)}, u32[]{:S(2)}) collective-permute-start(f32[512,128]{1,0:T(8,128)S(1)} %add_add_fusion.rest_0_.rest_1_), channel_id=1, source_target_pairs={{8,16},{16,8},{9,17},{17,9},{10,18},{18,10},{11,19},{19,11},{12,20... | collective-permute-start | bytes 786440 | tf_op jit(solution)/shard_map/ppermute | solution.py:304
  87.4 13.5 %collective-permute-start.30 = (f32[512,128]{1,0:T(8,128)S(1)}, f32[512,128]{1,0:T(8,128)S(1)}, u32[]{:S(2)}, u32[]{:S(2)}) collective-permute-start(f32[512,128]{1,0:T(8,128)S(1)} %fusion.1.rest_0_), channel_id=1, source_target_pairs={{0,4},{1,5},{2,6},{3,7},{4,0},{5,1},{6,2},{7,3},{8,12},{9,13},{10,... | collective-permute-start | bytes 786440 | tf_op jit(solution)/shard_map/ppermute | solution.py:23
  87.6 13.8 %collective-permute-start.31 = (f32[512,128]{1,0:T(8,128)S(1)}, f32[512,128]{1,0:T(8,128)S(1)}, u32[]{:S(2)}, u32[]{:S(2)}) collective-permute-start(f32[512,128]{1,0:T(8,128)S(1)} %fusion.1.rest_0_), channel_id=1, source_target_pairs={{0,2},{1,3},{2,0},{3,1},{4,6},{5,7},{6,4},{7,5},{8,10},{9,11},{10,... | collective-permute-start | bytes 786440 | tf_op jit(solution)/shard_map/ppermute | solution.py:23
  93.5 14.7 %collective-permute-start.28 = (f32[512,128]{1,0:T(8,128)S(1)}, f32[512,128]{1,0:T(8,128)S(1)}, u32[]{:S(2)}, u32[]{:S(2)}) collective-permute-start(f32[512,128]{1,0:T(8,128)S(1)} %fusion.1.rest_0_), channel_id=1, source_target_pairs={{0,1},{1,0},{2,3},{3,2},{4,5},{5,4},{6,7},{7,6},{8,9},{9,8},{10,11... | collective-permute-start | bytes 786440 | tf_op jit(solution)/shard_map/ppermute | solution.py:23
  116.5 25.7 %collective-permute-start.36 = (f32[512,128]{1,0:T(8,128)S(1)}, f32[512,128]{1,0:T(8,128)S(1)}, u32[]{:S(2)}, u32[]{:S(2)}) collective-permute-start(f32[512,128]{1,0:T(8,128)S(1)} %get-tuple-element.40), channel_id=1, source_target_pairs={{0,16},{8,24},{16,0},{24,8},{1,17},{9,25},{17,1},{25,9},{2,18},{10... | collective-permute-start | bytes 786440 | tf_op jit(solution)/shard_map/ppermute | solution.py:23
  118.7 23.6 %collective-permute-start.37 = (f32[512,128]{1,0:T(8,128)S(1)}, f32[512,128]{1,0:T(8,128)S(1)}, u32[]{:S(2)}, u32[]{:S(2)}) collective-permute-start(f32[512,128]{1,0:T(8,128)S(1)} %get-tuple-element.41), channel_id=1, source_target_pairs={{0,8},{8,0},{16,24},{24,16},{1,9},{9,1},{17,25},{25,17},{2,10},{10... | collective-permute-start | bytes 786440 | tf_op jit(solution)/shard_map/ppermute | solution.py:23
  119.0 23.3 %collective-permute-start.16 = (f32[512,128]{1,0:T(8,128)S(1)}, f32[512,128]{1,0:T(8,128)S(1)}, u32[]{:S(2)}, u32[]{:S(2)}) collective-permute-start(f32[512,128]{1,0:T(8,128)S(1)} %get-tuple-element.54), channel_id=1, source_target_pairs={{0,6},{1,7},{2,4},{3,5},{4,2},{5,3},{6,0},{7,1},{8,14},{9,15},{10,... | collective-permute-start | bytes 786440 | tf_op jit(solution)/shard_map/ppermute | solution.py:23
  120.4 21.9 %collective-permute-start.17 = (f32[512,128]{1,0:T(8,128)S(1)}, f32[512,128]{1,0:T(8,128)S(1)}, u32[]{:S(2)}, u32[]{:S(2)}) collective-permute-start(f32[512,128]{1,0:T(8,128)S(1)} %get-tuple-element.53), channel_id=1, source_target_pairs={{0,4},{1,5},{2,6},{3,7},{4,0},{5,1},{6,2},{7,3},{8,12},{9,13},{10,... | collective-permute-start | bytes 786440 | tf_op jit(solution)/shard_map/ppermute | solution.py:23
  125.0 17.3 %collective-permute-start.18 = (f32[512,128]{1,0:T(8,128)S(1)}, f32[512,128]{1,0:T(8,128)S(1)}, u32[]{:S(2)}, u32[]{:S(2)}) collective-permute-start(f32[512,128]{1,0:T(8,128)S(1)} %get-tuple-element.51), channel_id=1, source_target_pairs={{0,2},{1,3},{2,0},{3,1},{4,6},{5,7},{6,4},{7,5},{8,10},{9,11},{10,... | collective-permute-start | bytes 786440 | tf_op jit(solution)/shard_map/ppermute | solution.py:23
  (32 other events, 295.5 us)

commit v5 on v4

--- a/solution.py
+++ b/solution.py
@@ -180,7 +180,7 @@
     other_ref = rest[n_own]
     rest = rest[n_own + 1 :]
     if apply:
-        y_ref, out_ref, full, rows = rest
+        y_ref, out_ref, full, rows, ready, sems = rest
     else:
         w_ref, full, rows = rest
     size = full.shape[0]
@@ -247,14 +247,21 @@
 
     inverse = full[...] * unit_row
     if apply:
+        sends = []
         for band in range(2):
-            out_ref[band] = lax.dot_general(
+            ready[band] = lax.dot_general(
                 y_ref[band],
                 inverse,
                 (((1,), (1,)), ((), ())),
                 precision=exact_mode,
                 preferred_element_type=f32,
             )
+            sends.append(
+                pltpu.make_async_copy(ready.at[band], out_ref.at[band], sems.at[band])
+            )
+            sends[-1].start()
+        for send in sends:
+            send.wait()
     else:
         w_ref[...] = inverse.T
 
@@ -263,11 +270,15 @@
     _, nv = other.shape
     vmem = pl.BlockSpec(memory_space=pltpu.VMEM)
     args = list(own) + [other]
+    scratch = [pltpu.VMEM((nv, nv), f32), pltpu.VMEM((nv, nv), f32)]
+    out_spec = vmem
     if applied is None:
         out_shape = jax.ShapeDtypeStruct((nv, nv), f32)
     else:
         out_shape = jax.ShapeDtypeStruct(applied.shape, f32)
         args.append(applied)
+        scratch += [pltpu.VMEM(applied.shape, f32), pltpu.SemaphoreType.DMA((2,))]
+        out_spec = pl.BlockSpec(memory_space=pl.ANY)
     return pl.pallas_call(
         functools.partial(
             factor_kernel, n_own=len(own), total_rows=total_rows, apply=applied is not None
@@ -275,8 +286,8 @@
         name="factor" if applied is None else "factor_apply",
         out_shape=out_shape,
         in_specs=[pl.BlockSpec(memory_space=pltpu.SMEM)] + [vmem] * len(args),
-        out_specs=vmem,
-        scratch_shapes=[pltpu.VMEM((nv, nv), f32), pltpu.VMEM((nv, nv), f32)],
+        out_specs=out_spec,
+        scratch_shapes=scratch,
         compiler_params=pltpu.CompilerParams(vmem_limit_bytes=room(out_shape, *args)),
     )(parity, *args)
 
@@ -287,7 +298,7 @@
     group = vectors.shape[1]
     total_rows = 2 * group * n_row * n_col
     values = blocks.reshape(blocks.shape[2], blocks.shape[3], blocks.shape[4])
-    places = coords.reshape(2, coords.shape[3])
+    places = jnp.maximum(coords.reshape(2, coords.shape[3]), 0)
     row_id = lax.axis_index("row")
     col_id = lax.axis_index("col")
     here_direct = jnp.stack([row_id, col_id]).astype(jnp.int32)
@@ -341,7 +352,9 @@
     def reduce_gram(mine, other):
         own = mine + swap(other, "col", 1)
         own = functools.reduce(jnp.add, [own] + [swap(own, "col", m) for m in even])
-        parts = [own] + [swap(own, "row", m) for m in row_masks]
+        parts = [own]
+        for m in row_masks:
+            parts.append(swap(own, "row", m))
         own = functools.reduce(jnp.add, parts)
         return [own], swap(own, "col", 1)
 

time: 167 us -> 166 us (level)
  no operation moved by 1% of the time
where the time goes in v5:
time: 166 us
  starting transfers between devices  63.9 us (38%)
  waiting for transfers between devices  62.2 us (37%)
  Pallas kernels  36 us (22%)
  local copies, waits for them, and re-layouts  2 us (1%)
    ppermute x50, waiting for transfers between devices, swap(): return lax.ppermute(x, axis, [(i, i ^ mask) for i in range(size)])  62 us
    ppermute x50, starting transfers between devices, swap(): return lax.ppermute(x, axis, [(i, i ^ mask) for i in range(size)])  60 us
    pallas_call x4, Pallas kernels, tile_products(): pl.pallas_call(body, name='tile_flipped' if flipped else 'tile_direct', o...  25.3 us
    pallas_call x2, Pallas kernels, factor_inverse(): pl.pallas_call(functools.partial(factor_kernel, n_own=len(own), total_row...  8.75 us
  transfers between devices with their start and end apart: 54, of which 18 were waited for; matrix products, arithmetic and copies ran while one was open for 1% of the time, Pallas kernels for 18%

profile of v5, /device:TPU:1, one launch (start us, length us, event | category | flops | bytes accessed | tf_op | source)
XLA Modules:
  0.0 165.8 jit_solution(255311454895795477)
XLA Ops:
  1.1 3.2 %collective-permute-start.20 = (f32[512,128]{1,0:T(8,128)S(1)}, f32[512,128]{1,0:T(8,128)S(1)}, u32[]{:S(2)}, u32[]{:S(2)}) collective-permute-start(f32[512,128]{1,0:T(8,128)S(1)} %get-tuple-element.49.rest_0_), channel_id=1, source_target_pairs={{0,16},{8,24},{16,0},{24,8},{1,17},{9,25},{17,1},{25,9},{2,18},{10... | collective-permute-start | bytes 786440 | tf_op jit(solution)/shard_map/ppermute | solution.py:23
  6.2 2.2 %collective-permute-start.1 = (f32[512,128]{1,0:T(8,128)S(1)}, f32[512,128]{1,0:T(8,128)S(1)}, u32[]{:S(2)}, u32[]{:S(2)}) collective-permute-start(f32[512,128]{1,0:T(8,128)S(1)} %get-tuple-element.50.rest_0_), channel_id=1, source_target_pairs={{0,6},{1,7},{2,4},{3,5},{4,2},{5,3},{6,0},{7,1},{8,14},{9,15},{10,... | collective-permute-start | bytes 786440 | tf_op jit(solution)/shard_map/ppermute | solution.py:23
  8.7 7.2 %collective-permute-done.20.rest_2_ = f32[512,128]{1,0:T(8,128)S(1)} collective-permute-done((f32[512,128]{1,0:T(8,128)S(1)}, f32[512,128]{1,0:T(8,128)S(1)}, u32[]{:S(2)}, u32[]{:S(2)}) %collective-permute-start.20) | collective-permute-done | bytes 262176 | tf_op jit(solution)/shard_map/ppermute | solution.py:23
  19.0 2.9 %collective-permute-start = (f32[512,128]{1,0:T(8,128)S(1)}, f32[512,128]{1,0:T(8,128)S(1)}, u32[]{:S(2)}, u32[]{:S(2)}) collective-permute-start(f32[512,128]{1,0:T(8,128)S(1)} %get-tuple-element.50.rest_0_), channel_id=1, source_target_pairs={{0,1},{1,0},{2,3},{3,2},{4,5},{5,4},{6,7},{7,6},{8,9},{9,8},{10,11... | collective-permute-start | bytes 786440 | tf_op jit(solution)/shard_map/ppermute | solution.py:23
  22.4 2.2 %collective-permute-start.6 = (f32[512,128]{1,0:T(8,128)S(1)}, f32[512,128]{1,0:T(8,128)S(1)}, u32[]{:S(2)}, u32[]{:S(2)}) collective-permute-start(f32[512,128]{1,0:T(8,128)S(1)} %collective-permute-done.3.rest_4_), channel_id=1, source_target_pairs={{0,1},{1,0},{2,3},{3,2},{4,5},{5,4},{6,7},{7,6},{8,9},{9,8},{10,11... | collective-permute-start | bytes 786440 | tf_op jit(solution)/shard_map/ppermute | solution.py:23
  24.7 6.2 %tile_direct.3 = (f32[1024,128]{1,0:T(8,128)S(1)}, f32[1024,128]{1,0:T(8,128)S(1)}, f32[1024,128]{1,0:T(8,128)S(1)}, f32[1024,128]{1,0:T(8,128)S(1)}) custom-call(s32[2,170]{1,0:T(2,128)S(1)} %maximum_bitcast_fusion.places, s32[2]{0:T(128)S(1)} %pad_add_fusion.here, f32[170,128,128]{2,1,0:T(8,128)} %bitcast.10, f32[512,128]{1,0:T(8,128)S(1)} %get-tuple-element.49.rest_0_, ...), custom_call_target="tpu_custom_call" | custom-call | flops 2852126720 | bytes 11141120 | tf_op jit(solution)/shard_map/tile_direct/pallas_call | solution.py:115
  30.9 3.5 %collective-permute-start.24 = (f32[1024,128]{1,0:T(8,128)S(1)}, f32[1024,128]{1,0:T(8,128)S(1)}, u32[]{:S(2)}, u32[]{:S(2)}) collective-permute-start(f32[1024,128]{1,0:T(8,128)S(1)} %get-tuple-element.37), channel_id=1, source_target_pairs={{0,1},{1,0},{2,3},{3,2},{4,5},{5,4},{6,7},{7,6},{8,9},{9,8},{10,11... | collective-permute-start | bytes 1572872 | tf_op jit(solution)/shard_map/ppermute | solution.py:23
  34.5 6.5 %tile_flipped.2 = (f32[512,128]{1,0:T(8,128)S(1)}, f32[512,128]{1,0:T(8,128)S(1)}, f32[512,128]{1,0:T(8,128)S(1)}, f32[512,128]{1,0:T(8,128)S(1)}) custom-call(s32[2,170]{1,0:T(2,128)S(1)} %maximum_bitcast_fusion.places, s32[2]{0:T(128)S(1)} %pad_add_fusion.1.here, f32[170,128,128]{2,1,0:T(8,128)} %bitcast.11, f32[512,128]{1,0:T(8,128)S(1)} %get-tuple-element.50.rest_0_, ...), custom_call_target="tpu_custom_call" | custom-call | flops 2852126720 | bytes 11141120 | tf_op jit(solution)/shard_map/tile_flipped/pallas_call | solution.py:115
  41.0 3.7 %collective-permute-start.7 = (f32[512,128]{1,0:T(8,128)S(1)}, f32[512,128]{1,0:T(8,128)S(1)}, u32[]{:S(2)}, u32[]{:S(2)}) collective-permute-start(f32[512,128]{1,0:T(8,128)S(1)} %get-tuple-element.27), channel_id=1, source_target_pairs={{0,24},{8,16},{16,8},{24,0},{1,25},{9,17},{17,9},{25,1},{2,26},{10... | collective-permute-start | bytes 786440 | tf_op jit(solution)/shard_map/ppermute | solution.py:23
  47.4 3.5 %collective-permute-done.7 = f32[512,128]{1,0:T(8,128)S(1)} collective-permute-done((f32[512,128]{1,0:T(8,128)S(1)}, f32[512,128]{1,0:T(8,128)S(1)}, u32[]{:S(2)}, u32[]{:S(2)}) %collective-permute-start.7) | collective-permute-done | bytes 262176 | tf_op jit(solution)/shard_map/ppermute | solution.py:23
  51.2 14.6 %collective-permute-done.8 = f32[512,128]{1,0:T(8,128)S(1)} collective-permute-done((f32[512,128]{1,0:T(8,128)S(1)}, f32[512,128]{1,0:T(8,128)S(1)}, u32[]{:S(2)}, u32[]{:S(2)}) %collective-permute-start.8) | collective-permute-done | bytes 262176 | tf_op jit(solution)/shard_map/ppermute | solution.py:23
  66.0 2.4 %collective-permute-start.10 = (f32[512,128]{1,0:T(8,128)S(1)}, f32[512,128]{1,0:T(8,128)S(1)}, u32[]{:S(2)}, u32[]{:S(2)}) collective-permute-start(f32[512,128]{1,0:T(8,128)S(1)} %add_add_fusion.rest_0_.rest_1_), channel_id=1, source_target_pairs={{0,8},{8,0},{16,24},{24,16},{1,9},{9,1},{17,25},{25,17},{2,10},{10... | collective-permute-start | bytes 786440 | tf_op jit(solution)/shard_map/ppermute | solution.py:23
  69.1 2.0 %collective-permute-start.38 = (f32[64,128]{1,0:T(8,128)S(1)}, f32[64,128]{1,0:T(8,128)S(1)}, u32[]{:S(2)}, u32[]{:S(2)}) collective-permute-start(f32[64,128]{1,0:T(8,128)S(1)} %get-tuple-element.43), channel_id=1, source_target_pairs={{0,1},{1,0},{2,3},{3,2},{4,5},{5,4},{6,7},{7,6},{8,9},{9,8},{10,11... | collective-permute-start | bytes 98312 | tf_op jit(solution)/shard_map/ppermute | solution.py:23
  71.7 8.7 %collective-permute-done.11.rest_2_ = f32[512,128]{1,0:T(8,128)S(1)} collective-permute-done((f32[512,128]{1,0:T(8,128)S(1)}, f32[512,128]{1,0:T(8,128)S(1)}, u32[]{:S(2)}, u32[]{:S(2)}) %collective-permute-start.11) | collective-permute-done | bytes 262176 | tf_op jit(solution)/shard_map/ppermute | solution.py:23
  92.8 3.7 %collective-permute-start.28 = (f32[512,128]{1,0:T(8,128)S(1)}, f32[512,128]{1,0:T(8,128)S(1)}, u32[]{:S(2)}, u32[]{:S(2)}) collective-permute-start(f32[512,128]{1,0:T(8,128)S(1)} %fusion.1.rest_0_), channel_id=1, source_target_pairs={{0,1},{1,0},{2,3},{3,2},{4,5},{5,4},{6,7},{7,6},{8,9},{9,8},{10,11... | collective-permute-start | bytes 786440 | tf_op jit(solution)/shard_map/ppermute | solution.py:23
  100.8 6.2 %tile_direct.2 = (f32[1024,128]{1,0:T(8,128)S(1)}, f32[1024,128]{1,0:T(8,128)S(1)}, f32[1024,128]{1,0:T(8,128)S(1)}, f32[1024,128]{1,0:T(8,128)S(1)}) custom-call(s32[2,170]{1,0:T(2,128)S(1)} %maximum_bitcast_fusion.places, s32[2]{0:T(128)S(1)} %pad_add_fusion.here, f32[170,128,128]{2,1,0:T(8,128)} %bitcast.12, f32[512,128]{1,0:T(8,128)S(1)} %add_add_fusion.rest_0_.rest_1_, ...), custom_call_target="tpu_custom_call" | custom-call | flops 2852126720 | bytes 11141120 | tf_op jit(solution)/shard_map/tile_direct/pallas_call | solution.py:115
  108.1 6.5 %tile_flipped.3 = (f32[512,128]{1,0:T(8,128)S(1)}, f32[512,128]{1,0:T(8,128)S(1)}, f32[512,128]{1,0:T(8,128)S(1)}, f32[512,128]{1,0:T(8,128)S(1)}) custom-call(s32[2,170]{1,0:T(2,128)S(1)} %maximum_bitcast_fusion.places, s32[2]{0:T(128)S(1)} %pad_add_fusion.1.here, f32[170,128,128]{2,1,0:T(8,128)} %bitcast.13, f32[512,128]{1,0:T(8,128)S(1)} %fusion.1.rest_0_, ...), custom_call_target="tpu_custom_call" | custom-call | flops 2852126720 | bytes 11141120 | tf_op jit(solution)/shard_map/tile_flipped/pallas_call | solution.py:115
  115.9 2.1 %collective-permute-start.36 = (f32[512,128]{1,0:T(8,128)S(1)}, f32[512,128]{1,0:T(8,128)S(1)}, u32[]{:S(2)}, u32[]{:S(2)}) collective-permute-start(f32[512,128]{1,0:T(8,128)S(1)} %get-tuple-element.40), channel_id=1, source_target_pairs={{0,16},{8,24},{16,0},{24,8},{1,17},{9,25},{17,1},{25,9},{2,18},{10... | collective-permute-start | bytes 786440 | tf_op jit(solution)/shard_map/ppermute | solution.py:23
  120.4 3.9 %collective-permute-done.35.rest_5_ = f32[512,128]{1,0:T(8,128)S(1)} collective-permute-done((f32[512,128]{1,0:T(8,128)S(1)}, f32[512,128]{1,0:T(8,128)S(1)}, u32[]{:S(2)}, u32[]{:S(2)}) %collective-permute-start.35) | collective-permute-done | bytes 262176 | tf_op jit(solution)/shard_map/ppermute | solution.py:23
  125.0 3.5 %factor.1.rest_8_ = f32[128,128]{1,0:T(8,128)S(1)} custom-call(s32[1]{0:T(128)} %bitcast.here, f32[64,128]{1,0:T(8,128)S(1)} %add_add_fusion.3.rest_0_, f32[64,128]{1,0:T(8,128)S(1)} %collective-permute-done.45.rest_1_), custom_call_target="tpu_custom_call" | custom-call | tf_op jit(solution)/shard_map/factor/pallas_call | solution.py:282
  128.4 13.2 %collective-permute-done.36.rest_6_ = f32[512,128]{1,0:T(8,128)S(1)} collective-permute-done((f32[512,128]{1,0:T(8,128)S(1)}, f32[512,128]{1,0:T(8,128)S(1)}, u32[]{:S(2)}, u32[]{:S(2)}) %collective-permute-start.36) | collective-permute-done | bytes 262176 | tf_op jit(solution)/shard_map/ppermute | solution.py:23
  150.3 2.9 %collective-permute-start.51 = (f32[64,128]{1,0:T(8,128)S(1)}, f32[64,128]{1,0:T(8,128)S(1)}, u32[]{:S(2)}, u32[]{:S(2)}) collective-permute-start(f32[64,128]{1,0:T(8,128)S(1)} %add_add_fusion.2), channel_id=1, source_target_pairs={{0,16},{8,24},{16,0},{24,8},{1,17},{9,25},{17,1},{25,9},{2,18},{10... | collective-permute-start | bytes 98312 | tf_op jit(solution)/shard_map/ppermute | solution.py:23
  156.6 2.9 %collective-permute-start.53 = (f32[64,128]{1,0:T(8,128)S(1)}, f32[64,128]{1,0:T(8,128)S(1)}, u32[]{:S(2)}, u32[]{:S(2)}) collective-permute-start(f32[64,128]{1,0:T(8,128)S(1)} %add_add_fusion.1.rest_0_), channel_id=1, source_target_pairs={{0,1},{1,0},{2,3},{3,2},{4,5},{5,4},{6,7},{7,6},{8,9},{9,8},{10,11... | collective-permute-start | bytes 98312 | tf_op jit(solution)/shard_map/ppermute | solution.py:23
  160.4 5.3 %factor_apply.1 = f32[2,512,128]{2,1,0:T(8,128)} custom-call(s32[1]{0:T(128)} %bitcast.here, f32[64,128]{1,0:T(8,128)S(1)} %add_add_fusion.1.rest_0_, f32[64,128]{1,0:T(8,128)S(1)} %collective-permute-done.53.rest_1_, f32[2,512,128]{2,1,0:T(8,128)S(1)} %get-tuple-element.46.rest_2_), custom_call_target="tpu_custom_call" | custom-call | tf_op jit(solution)/shard_map/factor_apply/pallas_call | solution.py:282
  (112 shorter events, 46.4 us)
Async XLA Ops:
  1.1 14.9 %collective-permute-start.20 = (f32[512,128]{1,0:T(8,128)S(1)}, f32[512,128]{1,0:T(8,128)S(1)}, u32[]{:S(2)}, u32[]{:S(2)}) collective-permute-start(f32[512,128]{1,0:T(8,128)S(1)} %get-tuple-element.49.rest_0_), channel_id=1, source_target_pairs={{0,16},{8,24},{16,0},{24,8},{1,17},{9,25},{17,1},{25,9},{2,18},{10... | collective-permute-start | bytes 786440 | tf_op jit(solution)/shard_map/ppermute | solution.py:23
  4.3 12.7 %collective-permute-start.19 = (f32[512,128]{1,0:T(8,128)S(1)}, f32[512,128]{1,0:T(8,128)S(1)}, u32[]{:S(2)}, u32[]{:S(2)}) collective-permute-start(f32[512,128]{1,0:T(8,128)S(1)} %get-tuple-element.49.rest_0_), channel_id=1, source_target_pairs={{0,8},{8,0},{16,24},{24,16},{1,9},{9,1},{17,25},{25,17},{2,10},{10... | collective-permute-start | bytes 786440 | tf_op jit(solution)/shard_map/ppermute | solution.py:23
  5.6 13.4 %collective-permute-start.21 = (f32[512,128]{1,0:T(8,128)S(1)}, f32[512,128]{1,0:T(8,128)S(1)}, u32[]{:S(2)}, u32[]{:S(2)}) collective-permute-start(f32[512,128]{1,0:T(8,128)S(1)} %get-tuple-element.49.rest_0_), channel_id=1, source_target_pairs={{8,16},{16,8},{9,17},{17,9},{10,18},{18,10},{11,19},{19,11},{12,20... | collective-permute-start | bytes 786440 | tf_op jit(solution)/shard_map/ppermute | solution.py:315
  6.2 15.7 %collective-permute-start.1 = (f32[512,128]{1,0:T(8,128)S(1)}, f32[512,128]{1,0:T(8,128)S(1)}, u32[]{:S(2)}, u32[]{:S(2)}) collective-permute-start(f32[512,128]{1,0:T(8,128)S(1)} %get-tuple-element.50.rest_0_), channel_id=1, source_target_pairs={{0,6},{1,7},{2,4},{3,5},{4,2},{5,3},{6,0},{7,1},{8,14},{9,15},{10,... | collective-permute-start | bytes 786440 | tf_op jit(solution)/shard_map/ppermute | solution.py:23
  8.5 13.5 %collective-permute-start.2 = (f32[512,128]{1,0:T(8,128)S(1)}, f32[512,128]{1,0:T(8,128)S(1)}, u32[]{:S(2)}, u32[]{:S(2)}) collective-permute-start(f32[512,128]{1,0:T(8,128)S(1)} %get-tuple-element.50.rest_0_), channel_id=1, source_target_pairs={{0,4},{1,5},{2,6},{3,7},{4,0},{5,1},{6,2},{7,3},{8,12},{9,13},{10,... | collective-permute-start | bytes 786440 | tf_op jit(solution)/shard_map/ppermute | solution.py:23
  19.0 15.4 %collective-permute-start = (f32[512,128]{1,0:T(8,128)S(1)}, f32[512,128]{1,0:T(8,128)S(1)}, u32[]{:S(2)}, u32[]{:S(2)}) collective-permute-start(f32[512,128]{1,0:T(8,128)S(1)} %get-tuple-element.50.rest_0_), channel_id=1, source_target_pairs={{0,1},{1,0},{2,3},{3,2},{4,5},{5,4},{6,7},{7,6},{8,9},{9,8},{10,11... | collective-permute-start | bytes 786440 | tf_op jit(solution)/shard_map/ppermute | solution.py:23
  30.9 14.2 %collective-permute-start.24 = (f32[1024,128]{1,0:T(8,128)S(1)}, f32[1024,128]{1,0:T(8,128)S(1)}, u32[]{:S(2)}, u32[]{:S(2)}) collective-permute-start(f32[1024,128]{1,0:T(8,128)S(1)} %get-tuple-element.37), channel_id=1, source_target_pairs={{0,1},{1,0},{2,3},{3,2},{4,5},{5,4},{6,7},{7,6},{8,9},{9,8},{10,11... | collective-permute-start | bytes 1572872 | tf_op jit(solution)/shard_map/ppermute | solution.py:23
  34.4 12.7 %collective-permute-start.23 = (f32[1024,128]{1,0:T(8,128)S(1)}, f32[1024,128]{1,0:T(8,128)S(1)}, u32[]{:S(2)}, u32[]{:S(2)}) collective-permute-start(f32[1024,128]{1,0:T(8,128)S(1)} %get-tuple-element.35), channel_id=1, source_target_pairs={{0,1},{1,0},{2,3},{3,2},{4,5},{5,4},{6,7},{7,6},{8,9},{9,8},{10,11... | collective-permute-start | bytes 1572872 | tf_op jit(solution)/shard_map/ppermute | solution.py:23
  44.7 21.1 %collective-permute-start.8 = (f32[512,128]{1,0:T(8,128)S(1)}, f32[512,128]{1,0:T(8,128)S(1)}, u32[]{:S(2)}, u32[]{:S(2)}) collective-permute-start(f32[512,128]{1,0:T(8,128)S(1)} %get-tuple-element.28), channel_id=1, source_target_pairs={{0,16},{8,24},{16,0},{24,8},{1,17},{9,25},{17,1},{25,9},{2,18},{10... | collective-permute-start | bytes 786440 | tf_op jit(solution)/shard_map/ppermute | solution.py:23
  44.7 21.1 %collective-permute-start.9 = (f32[512,128]{1,0:T(8,128)S(1)}, f32[512,128]{1,0:T(8,128)S(1)}, u32[]{:S(2)}, u32[]{:S(2)}) collective-permute-start(f32[512,128]{1,0:T(8,128)S(1)} %get-tuple-element.29), channel_id=1, source_target_pairs={{0,8},{8,0},{16,24},{24,16},{1,9},{9,1},{17,25},{25,17},{2,10},{10... | collective-permute-start | bytes 786440 | tf_op jit(solution)/shard_map/ppermute | solution.py:23
  45.9 22.4 %collective-permute-start.25 = (f32[512,128]{1,0:T(8,128)}, f32[512,128]{1,0:T(8,128)S(1)}, u32[]{:S(2)}, u32[]{:S(2)}) collective-permute-start(f32[512,128]{1,0:T(8,128)} %get-tuple-element.47), channel_id=1, source_target_pairs={{0,6},{1,7},{2,4},{3,5},{4,2},{5,3},{6,0},{7,1},{8,14},{9,15},{10,... | collective-permute-start | bytes 786440 | tf_op jit(solution)/shard_map/ppermute | solution.py:23
  47.1 21.2 %collective-permute-start.26 = (f32[512,128]{1,0:T(8,128)}, f32[512,128]{1,0:T(8,128)S(1)}, u32[]{:S(2)}, u32[]{:S(2)}) collective-permute-start(f32[512,128]{1,0:T(8,128)} %get-tuple-element.48), channel_id=1, source_target_pairs={{0,4},{1,5},{2,6},{3,7},{4,0},{5,1},{6,2},{7,3},{8,12},{9,13},{10,... | collective-permute-start | bytes 786440 | tf_op jit(solution)/shard_map/ppermute | solution.py:23
  50.9 17.4 %collective-permute-start.27 = (f32[512,128]{1,0:T(8,128)S(1)}, f32[512,128]{1,0:T(8,128)S(1)}, u32[]{:S(2)}, u32[]{:S(2)}) collective-permute-start(f32[512,128]{1,0:T(8,128)S(1)} %slice.47), channel_id=1, source_target_pairs={{0,2},{1,3},{2,0},{3,1},{4,6},{5,7},{6,4},{7,5},{8,10},{9,11},{10,... | collective-permute-start | bytes 786440 | tf_op jit(solution)/shard_map/ppermute | solution.py:23
  65.9 14.6 %collective-permute-start.11 = (f32[512,128]{1,0:T(8,128)S(1)}, f32[512,128]{1,0:T(8,128)S(1)}, u32[]{:S(2)}, u32[]{:S(2)}) collective-permute-start(f32[512,128]{1,0:T(8,128)S(1)} %add_add_fusion.rest_0_.rest_1_), channel_id=1, source_target_pairs={{0,16},{8,24},{16,0},{24,8},{1,17},{9,25},{17,1},{25,9},{2,18},{10... | collective-permute-start | bytes 786440 | tf_op jit(solution)/shard_map/ppermute | solution.py:23
  66.0 17.3 %collective-permute-start.10 = (f32[512,128]{1,0:T(8,128)S(1)}, f32[512,128]{1,0:T(8,128)S(1)}, u32[]{:S(2)}, u32[]{:S(2)}) collective-permute-start(f32[512,128]{1,0:T(8,128)S(1)} %add_add_fusion.rest_0_.rest_1_), channel_id=1, source_target_pairs={{0,8},{8,0},{16,24},{24,16},{1,9},{9,1},{17,25},{25,17},{2,10},{10... | collective-permute-start | bytes 786440 | tf_op jit(solution)/shard_map/ppermute | solution.py:23
  71.0 17.1 %collective-permute-start.12 = (f32[512,128]{1,0:T(8,128)S(1)}, f32[512,128]{1,0:T(8,128)S(1)}, u32[]{:S(2)}, u32[]{:S(2)}) collective-permute-start(f32[512,128]{1,0:T(8,128)S(1)} %add_add_fusion.rest_0_.rest_1_), channel_id=1, source_target_pairs={{8,16},{16,8},{9,17},{17,9},{10,18},{18,10},{11,19},{19,11},{12,20... | collective-permute-start | bytes 786440 | tf_op jit(solution)/shard_map/ppermute | solution.py:315
  86.7 13.5 %collective-permute-start.30 = (f32[512,128]{1,0:T(8,128)S(1)}, f32[512,128]{1,0:T(8,128)S(1)}, u32[]{:S(2)}, u32[]{:S(2)}) collective-permute-start(f32[512,128]{1,0:T(8,128)S(1)} %fusion.1.rest_0_), channel_id=1, source_target_pairs={{0,4},{1,5},{2,6},{3,7},{4,0},{5,1},{6,2},{7,3},{8,12},{9,13},{10,... | collective-permute-start | bytes 786440 | tf_op jit(solution)/shard_map/ppermute | solution.py:23
  87.0 13.8 %collective-permute-start.31 = (f32[512,128]{1,0:T(8,128)S(1)}, f32[512,128]{1,0:T(8,128)S(1)}, u32[]{:S(2)}, u32[]{:S(2)}) collective-permute-start(f32[512,128]{1,0:T(8,128)S(1)} %fusion.1.rest_0_), channel_id=1, source_target_pairs={{0,2},{1,3},{2,0},{3,1},{4,6},{5,7},{6,4},{7,5},{8,10},{9,11},{10,... | collective-permute-start | bytes 786440 | tf_op jit(solution)/shard_map/ppermute | solution.py:23
  92.8 14.7 %collective-permute-start.28 = (f32[512,128]{1,0:T(8,128)S(1)}, f32[512,128]{1,0:T(8,128)S(1)}, u32[]{:S(2)}, u32[]{:S(2)}) collective-permute-start(f32[512,128]{1,0:T(8,128)S(1)} %fusion.1.rest_0_), channel_id=1, source_target_pairs={{0,1},{1,0},{2,3},{3,2},{4,5},{5,4},{6,7},{7,6},{8,9},{9,8},{10,11... | collective-permute-start | bytes 786440 | tf_op jit(solution)/shard_map/ppermute | solution.py:23
  115.9 25.7 %collective-permute-start.36 = (f32[512,128]{1,0:T(8,128)S(1)}, f32[512,128]{1,0:T(8,128)S(1)}, u32[]{:S(2)}, u32[]{:S(2)}) collective-permute-start(f32[512,128]{1,0:T(8,128)S(1)} %get-tuple-element.40), channel_id=1, source_target_pairs={{0,16},{8,24},{16,0},{24,8},{1,17},{9,25},{17,1},{25,9},{2,18},{10... | collective-permute-start | bytes 786440 | tf_op jit(solution)/shard_map/ppermute | solution.py:23
  118.0 23.6 %collective-permute-start.37 = (f32[512,128]{1,0:T(8,128)S(1)}, f32[512,128]{1,0:T(8,128)S(1)}, u32[]{:S(2)}, u32[]{:S(2)}) collective-permute-start(f32[512,128]{1,0:T(8,128)S(1)} %get-tuple-element.41), channel_id=1, source_target_pairs={{0,8},{8,0},{16,24},{24,16},{1,9},{9,1},{17,25},{25,17},{2,10},{10... | collective-permute-start | bytes 786440 | tf_op jit(solution)/shard_map/ppermute | solution.py:23
  118.3 23.3 %collective-permute-start.16 = (f32[512,128]{1,0:T(8,128)S(1)}, f32[512,128]{1,0:T(8,128)S(1)}, u32[]{:S(2)}, u32[]{:S(2)}) collective-permute-start(f32[512,128]{1,0:T(8,128)S(1)} %get-tuple-element.54), channel_id=1, source_target_pairs={{0,6},{1,7},{2,4},{3,5},{4,2},{5,3},{6,0},{7,1},{8,14},{9,15},{10,... | collective-permute-start | bytes 786440 | tf_op jit(solution)/shard_map/ppermute | solution.py:23
  119.7 21.9 %collective-permute-start.17 = (f32[512,128]{1,0:T(8,128)S(1)}, f32[512,128]{1,0:T(8,128)S(1)}, u32[]{:S(2)}, u32[]{:S(2)}) collective-permute-start(f32[512,128]{1,0:T(8,128)S(1)} %get-tuple-element.53), channel_id=1, source_target_pairs={{0,4},{1,5},{2,6},{3,7},{4,0},{5,1},{6,2},{7,3},{8,12},{9,13},{10,... | collective-permute-start | bytes 786440 | tf_op jit(solution)/shard_map/ppermute | solution.py:23
  124.3 17.3 %collective-permute-start.18 = (f32[512,128]{1,0:T(8,128)S(1)}, f32[512,128]{1,0:T(8,128)S(1)}, u32[]{:S(2)}, u32[]{:S(2)}) collective-permute-start(f32[512,128]{1,0:T(8,128)S(1)} %get-tuple-element.51), channel_id=1, source_target_pairs={{0,2},{1,3},{2,0},{3,1},{4,6},{5,7},{6,4},{7,5},{8,10},{9,11},{10,... | collective-permute-start | bytes 786440 | tf_op jit(solution)/shard_map/ppermute | solution.py:23
  (30 other events, 224.5 us)
